TPU v7x, 32 devices: a whole 2x2x4 slice. The times are simulated.
32 devices in a mesh: dp: 8 (over y, x, core), seq: 4 (over z).
Axes of the slice: x: 2, y: 2, z: 4, core: 2. Of those that a mesh axis runs over, the one named last changes fastest.
Arguments:
- tokens: bfloat16 [4096, 2048], P(('dp', 'seq')), may hold values from -6 to 6
- doc_lengths: int32 [8, 4], P('dp'), may hold values from 1 to 384, 512 in all within a row
- qkv_weight: bfloat16 [2048, 6144], P('dp'), may hold values from -0.125 to 0.125
- qkv_bias: bfloat16 [6144], P('dp'), may hold values from -1.5 to 1.5
- dense_weight: bfloat16 [2048, 2048], P('dp'), may hold values from -1 to 1
- dense_bias: bfloat16 [2048], P('dp'), may hold values from -1.5 to 1.5
- up_weight: bfloat16 [2048, 8192], P('dp'), may hold values from -0.125 to 0.125
- up_bias: bfloat16 [8192], P('dp'), may hold values from -2.5 to 2.5
- down_weight: bfloat16 [8192, 2048], P('dp'), may hold values from -0.0625 to 0.0625
- down_bias: bfloat16 [2048], P('dp'), may hold values from -1.5 to 1.5
- norm1_gain: bfloat16 [2048], P('dp'), may hold values from 0.5 to 1.5
- norm1_shift: bfloat16 [2048], P('dp'), may hold values from -1.5 to 1.5
- norm2_gain: bfloat16 [2048], P('dp'), may hold values from 0.5 to 1.5
- norm2_shift: bfloat16 [2048], P('dp'), may hold values from -1.5 to 1.5
- cotangent: bfloat16 [4096, 2048], P(('dp', 'seq')), may hold values from -6 to 6
Outputs:
- output: bfloat16 [4096, 2048], P(('dp', 'seq'))
- input_grad: bfloat16 [4096, 2048], P(('dp', 'seq'))
- qkv_weight_grad: float32 [2048, 6144], P('dp', 'seq')
- qkv_bias_grad: float32 [6144], P(('dp', 'seq'))
- dense_weight_grad: float32 [2048, 2048], P('seq', 'dp')
- dense_bias_grad: float32 [2048], P(('dp', 'seq'))
- up_weight_grad: float32 [2048, 8192], P('dp', 'seq')
- up_bias_grad: float32 [8192], P(('dp', 'seq'))
- down_weight_grad: float32 [8192, 2048], P('seq', 'dp')
- down_bias_grad: float32 [2048], P(('dp', 'seq'))
- norm1_gain_grad: float32 [2048], P(('dp', 'seq'))
- norm1_shift_grad: float32 [2048], P(('dp', 'seq'))
- norm2_gain_grad: float32 [2048], P(('dp', 'seq'))
- norm2_shift_grad: float32 [2048], P(('dp', 'seq'))
Inputs may be any that keep to these rules, and one draw needn't show every extreme that they name: `doc_lengths`: each stream's 4 document lengths sum to 512, and the longest of each stream is exactly 384.
All inputs are finite; a program needn't handle non-finite values.
Results may differ from a plain program's by a relative error of at most 0.0094.
Values may be sent and summed in bfloat16 or wider, within the bound.
No kernel may reach another device: no remote copies, remote signals or barrier semaphores. Data moves between devices by JAX's collectives and lax.ppermute only.
A program may use at most 320 MiB of HBM per device.

v0:
```python
from functools import partial

import jax
import jax.numpy as jnp
from jax import lax
from jax.sharding import PartitionSpec as P

H = 8
HS = 256
ROT = 64


def layer_norm(values, gain, shift):
    average = jnp.mean(values, axis=-1, keepdims=True)
    centred = values - average
    variance = jnp.mean(centred * centred, axis=-1, keepdims=True)
    return centred * lax.rsqrt(variance + 1e-05) * gain + shift


def doc_layout(lengths_row, places):
    starts = jnp.cumsum(lengths_row) - lengths_row
    after = places[:, None] >= starts[None, :]
    doc_ids = jnp.sum(after.astype(jnp.int32), axis=1)
    begins = jnp.max(jnp.where(after, starts[None, :], 0), axis=1)
    return (doc_ids, places - begins)


def turn_tables(positions, rot_dims):
    half_rot = rot_dims // 2
    inverse = 10000.0 ** (-(jnp.arange(half_rot, dtype=jnp.float32) * 2.0 / rot_dims))
    angles = positions.astype(jnp.float32)[:, None] * inverse[None, :]
    angles = jnp.concatenate([angles, angles], axis=1)
    return (jnp.cos(angles), jnp.sin(angles))


def rotate(values, cosine, sine_table):
    rot_dims = cosine.shape[1]
    half_rot = rot_dims // 2
    leading = values[..., :rot_dims]
    swapped = jnp.concatenate([-leading[..., half_rot:], leading[..., :half_rot]], axis=-1)
    turned = leading * cosine[:, None, :] + swapped * sine_table[:, None, :]
    return jnp.concatenate([turned, values[..., rot_dims:]], axis=-1)


def unrotate(gradient, cosine, sine_table):
    rot_dims = cosine.shape[1]
    half_rot = rot_dims // 2
    leading = gradient[..., :rot_dims]
    scaled = leading * sine_table[:, None, :]
    moved = jnp.concatenate([scaled[..., half_rot:], -scaled[..., :half_rot]], axis=-1)
    return jnp.concatenate(
        [leading * cosine[:, None, :] + moved, gradient[..., rot_dims:]], axis=-1
    )


def times_transposed(left, right):
    return lax.dot_general(
        left, right, (((1,), (1,)), ((), ())), preferred_element_type=jnp.float32
    )


def left_transposed(left, right):
    return lax.dot_general(
        left, right, (((0,), (0,)), ((), ())), preferred_element_type=jnp.float32
    )


def on_device(
    tokens,
    doc_lengths,
    qkv_weight,
    qkv_bias,
    dense_weight,
    dense_bias,
    up_weight,
    up_bias,
    down_weight,
    down_bias,
    norm1_gain,
    norm1_shift,
    norm2_gain,
    norm2_shift,
    cotangent,
):
    gathered = (
        lax.all_gather(qkv_weight, "dp", axis=0, tiled=True),
        lax.all_gather(qkv_bias, "dp", axis=0, tiled=True),
        lax.all_gather(dense_weight, "dp", axis=0, tiled=True),
        lax.all_gather(dense_bias, "dp", axis=0, tiled=True),
        lax.all_gather(up_weight, "dp", axis=0, tiled=True),
        lax.all_gather(up_bias, "dp", axis=0, tiled=True),
        lax.all_gather(down_weight, "dp", axis=0, tiled=True),
        lax.all_gather(down_bias, "dp", axis=0, tiled=True),
        lax.all_gather(norm1_gain, "dp", axis=0, tiled=True),
        lax.all_gather(norm1_shift, "dp", axis=0, tiled=True),
        lax.all_gather(norm2_gain, "dp", axis=0, tiled=True),
        lax.all_gather(norm2_shift, "dp", axis=0, tiled=True),
    )
    (
        w_qkv,
        b_qkv,
        w_dense,
        b_dense,
        w_up,
        b_up,
        w_down,
        b_down,
        gain_one,
        shift_one,
        gain_two,
        shift_two,
    ) = gathered
    norm_params = tuple((p.astype(jnp.float32) for p in (gain_one, shift_one, gain_two, shift_two)))
    tok_rows = tokens.shape[0]
    seq_len = tok_rows * lax.axis_size("seq")
    inputs = tokens.astype(jnp.float32)
    lengths_row = doc_lengths[0]
    local_places = lax.axis_index("seq") * tok_rows + jnp.arange(tok_rows, dtype=jnp.int32)
    local_docs, local_positions = doc_layout(lengths_row, local_places)
    normed_one = layer_norm(inputs, norm_params[0], norm_params[1]).astype(jnp.bfloat16)
    normed_two = layer_norm(inputs, norm_params[2], norm_params[3]).astype(jnp.bfloat16)
    projected = jnp.dot(normed_one, w_qkv, preferred_element_type=jnp.float32) + b_qkv.astype(
        jnp.float32
    )
    projected = projected.reshape(tok_rows, H, 3 * HS)
    cos_local, sin_local = turn_tables(local_positions, ROT)
    packed = jnp.concatenate(
        [
            rotate(projected[..., :HS], cos_local, sin_local),
            rotate(projected[..., HS : 2 * HS], cos_local, sin_local),
            projected[..., 2 * HS :],
        ],
        axis=-1,
    ).astype(jnp.bfloat16)
    by_head = lax.all_to_all(packed, "seq", split_axis=1, concat_axis=0, tiled=True)
    heads_here = by_head.shape[1]
    queries = by_head[..., :HS]
    keys_all = by_head[..., HS : 2 * HS]
    values_all = by_head[..., 2 * HS :]
    all_places = jnp.arange(seq_len, dtype=jnp.int32)
    doc_all, pos_all = doc_layout(lengths_row, all_places)
    block_rows = min(512, seq_len)
    block_count = seq_len // block_rows
    score_scale = HS ** (-0.5)

    def scores_for(first_row):
        query_block = lax.dynamic_slice_in_dim(queries, first_row, block_rows, 0)
        raw_scores = (
            jnp.einsum("qhd,khd->hqk", query_block, keys_all, preferred_element_type=jnp.float32)
            * score_scale
        )
        row_ids = first_row + jnp.arange(block_rows, dtype=jnp.int32)
        doc_rows = lax.dynamic_slice_in_dim(doc_all, first_row, block_rows, 0)
        allowed = (doc_rows[:, None] == doc_all[None, :]) & (
            all_places[None, :] <= row_ids[:, None]
        )
        return (query_block, raw_scores, allowed)

    def forward_block(block_index):
        query_block, raw_scores, allowed = scores_for(block_index * block_rows)
        masked = jnp.where(allowed[None], raw_scores, -1e30)
        largest = jnp.max(masked, axis=-1, keepdims=True)
        exponent = jnp.exp(masked - largest)
        summed = jnp.sum(exponent, axis=-1, keepdims=True)
        probs_low = (exponent / summed).astype(jnp.bfloat16)
        mixed_out = jnp.einsum(
            "hqk,khd->qhd", probs_low, values_all, preferred_element_type=jnp.float32
        )
        return (mixed_out.astype(jnp.bfloat16), (largest + jnp.log(summed))[..., 0])

    mixed_blocks, lse_blocks = lax.map(forward_block, jnp.arange(block_count, dtype=jnp.int32))
    attended_heads = mixed_blocks.reshape(seq_len, heads_here, HS)
    attended = lax.all_to_all(
        attended_heads, "seq", split_axis=0, concat_axis=1, tiled=True
    ).reshape(tok_rows, H * HS)
    hidden = jnp.dot(normed_two, w_up, preferred_element_type=jnp.float32) + b_up.astype(
        jnp.float32
    )
    activated = jax.nn.gelu(hidden, approximate=False).astype(jnp.bfloat16)
    branch_att = jnp.dot(attended, w_dense, preferred_element_type=jnp.float32) + b_dense.astype(
        jnp.float32
    )
    branch_ffn = jnp.dot(activated, w_down, preferred_element_type=jnp.float32) + b_down.astype(
        jnp.float32
    )
    output = (inputs + branch_att + branch_ffn).astype(jnp.bfloat16)
    cotan_rows = cotangent.astype(jnp.float32)
    grad_attended = times_transposed(cotangent, w_dense).astype(jnp.bfloat16)
    grad_heads = lax.all_to_all(
        grad_attended.reshape(tok_rows, H, HS), "seq", split_axis=1, concat_axis=0, tiled=True
    )
    column_total = jnp.sum(cotan_rows, axis=0)
    grad_activated = times_transposed(cotangent, w_down)
    _, gelu_pull = jax.vjp(partial(jax.nn.gelu, approximate=False), hidden)
    grad_hidden = gelu_pull(grad_activated)[0].astype(jnp.bfloat16)
    grad_up_bias = jnp.sum(grad_hidden.astype(jnp.float32), axis=0)
    grad_normed_two = times_transposed(grad_hidden, w_up)
    normed_full, normed_two_full, cotan_full = (
        lax.all_gather(normed_one, "seq", axis=0, tiled=True),
        lax.all_gather(normed_two, "seq", axis=0, tiled=True),
        lax.all_gather(cotangent, "seq", axis=0, tiled=True),
    )
    act_cols, hidden_cols = (
        lax.all_to_all(activated, "seq", split_axis=1, concat_axis=0, tiled=True),
        lax.all_to_all(grad_hidden, "seq", split_axis=1, concat_axis=0, tiled=True),
    )
    part_up = left_transposed(normed_two_full, hidden_cols)
    part_down = left_transposed(act_cols, cotan_full)
    sum_up, sum_down = (
        lax.psum_scatter(part_up, "dp", scatter_dimension=0, tiled=True),
        lax.psum_scatter(part_down, "dp", scatter_dimension=1, tiled=True),
    )

    def backward_block(carry, block_item):
        grad_keys, grad_values = carry
        block_index, lse_block = block_item
        first_row = block_index * block_rows
        query_block, raw_scores, allowed = scores_for(first_row)
        probs = jnp.where(allowed[None], jnp.exp(raw_scores - lse_block[..., None]), 0.0)
        grad_out = lax.dynamic_slice_in_dim(grad_heads, first_row, block_rows, 0)
        grad_probs = jnp.einsum(
            "qhd,khd->hqk", grad_out, values_all, preferred_element_type=jnp.float32
        )
        inner = jnp.sum(probs * grad_probs, axis=-1, keepdims=True)
        grad_scores = (probs * (grad_probs - inner)).astype(jnp.bfloat16)
        grad_query = (
            jnp.einsum("hqk,khd->qhd", grad_scores, keys_all, preferred_element_type=jnp.float32)
            * score_scale
        )
        grad_keys = (
            grad_keys
            + jnp.einsum(
                "hqk,qhd->khd", grad_scores, query_block, preferred_element_type=jnp.float32
            )
            * score_scale
        )
        grad_values = grad_values + jnp.einsum(
            "hqk,qhd->khd", probs.astype(jnp.bfloat16), grad_out, preferred_element_type=jnp.float32
        )
        return ((grad_keys, grad_values), grad_query)

    zero_heads = jnp.zeros((seq_len, heads_here, HS), jnp.float32)
    (grad_keys, grad_values), query_grads = lax.scan(
        backward_block,
        (zero_heads, zero_heads),
        (jnp.arange(block_count, dtype=jnp.int32), lse_blocks),
    )
    grad_queries = query_grads.reshape(seq_len, heads_here, HS)
    cos_all, sin_all = turn_tables(pos_all, ROT)
    grad_packed = jnp.concatenate(
        [
            unrotate(grad_queries, cos_all, sin_all),
            unrotate(grad_keys, cos_all, sin_all),
            grad_values,
        ],
        axis=-1,
    ).astype(jnp.bfloat16)
    grad_tokens = lax.all_to_all(
        grad_packed, "seq", split_axis=0, concat_axis=1, tiled=True
    ).reshape(tok_rows, 3 * H * HS)
    part_qkv = left_transposed(normed_full, grad_packed.reshape(seq_len, heads_here * 3 * HS))
    part_dense = left_transposed(attended_heads.reshape(seq_len, heads_here * HS), cotan_full)
    sum_qkv, sum_dense = (
        lax.psum_scatter(part_qkv, "dp", scatter_dimension=0, tiled=True),
        lax.psum_scatter(part_dense, "dp", scatter_dimension=1, tiled=True),
    )
    grad_qkv_bias = jnp.sum(grad_tokens.astype(jnp.float32), axis=0)
    grad_normed_one = times_transposed(grad_tokens, w_qkv)
    _, norm_pull_one = jax.vjp(layer_norm, inputs, norm_params[0], norm_params[1])
    grad_in_one, grad_gain_one, grad_shift_one = norm_pull_one(grad_normed_one)
    _, norm_pull_two = jax.vjp(layer_norm, inputs, norm_params[2], norm_params[3])
    grad_in_two, grad_gain_two, grad_shift_two = norm_pull_two(grad_normed_two)
    input_grad = (cotan_rows + grad_in_one + grad_in_two).astype(jnp.bfloat16)
    small_sums = (
        lax.psum_scatter(grad_qkv_bias, ("dp", "seq"), scatter_dimension=0, tiled=True),
        lax.psum_scatter(column_total, ("dp", "seq"), scatter_dimension=0, tiled=True),
        lax.psum_scatter(grad_up_bias, ("dp", "seq"), scatter_dimension=0, tiled=True),
        lax.psum_scatter(grad_gain_one, ("dp", "seq"), scatter_dimension=0, tiled=True),
        lax.psum_scatter(grad_shift_one, ("dp", "seq"), scatter_dimension=0, tiled=True),
        lax.psum_scatter(grad_gain_two, ("dp", "seq"), scatter_dimension=0, tiled=True),
        lax.psum_scatter(grad_shift_two, ("dp", "seq"), scatter_dimension=0, tiled=True),
    )
    (
        sum_qkv_bias,
        sum_column,
        sum_up_bias,
        sum_gain_one,
        sum_shift_one,
        sum_gain_two,
        sum_shift_two,
    ) = small_sums
    return (
        output,
        input_grad,
        sum_qkv,
        sum_qkv_bias,
        sum_dense,
        sum_column,
        sum_up,
        sum_up_bias,
        sum_down,
        sum_column,
        sum_gain_one,
        sum_shift_one,
        sum_gain_two,
        sum_shift_two,
    )


def solution(mesh):
    placed = (
        P(("dp", "seq"), None),
        P("dp", None),
        P("dp", None),
        P("dp"),
        P("dp", None),
        P("dp"),
        P("dp", None),
        P("dp"),
        P("dp", None),
        P("dp"),
        P("dp"),
        P("dp"),
        P("dp"),
        P("dp"),
        P(("dp", "seq"), None),
    )
    return jax.shard_map(
        on_device,
        mesh=mesh,
        in_specs=placed,
        out_specs=(
            P(("dp", "seq"), None),
            P(("dp", "seq"), None),
            P("dp", "seq"),
            P(("dp", "seq")),
            P("seq", "dp"),
            P(("dp", "seq")),
            P("dp", "seq"),
            P(("dp", "seq")),
            P("seq", "dp"),
            P(("dp", "seq")),
            P(("dp", "seq")),
            P(("dp", "seq")),
            P(("dp", "seq")),
            P(("dp", "seq")),
        ),
        check_vma=False,
    )
```

profile of v0, /device:TPU:0, one launch (start us, length us, event | category | flops | bytes accessed | tf_op | source)
XLA Modules:
  0.0 1228.1 jit_solution(1152223384118208151)
XLA Ops:
  11.9 10.3 all-gather.5
  22.2 8.9 all-gather.4
  31.1 7.9 all-gather.1
  39.1 8.9 all-gather
  48.0 8.1 all-gather.2
  56.5 1.3 fusion.30
  57.9 9.3 all-gather.17.cloned.1.call-done
  67.2 6.3 convolution_convert_fusion
  74.3 4.6 all-to-all-start.2
  78.9 115.5 %all-gather.15.cloned.1.call-done = bf16[2048,6144]{1,0:T(8,128)(2,1)} async-done(((bf16[256,6144]{1,0:T(8,128)(2,1)}), bf16[2048,6144]{1,0:T(8,128)(2,1)}) %all-gather.15.cloned.1.call-update) | async-done | bytes 25165840 | tf_op jit(solution)/shard_map/all_gather | solution.py:86
  194.4 10.0 convolution_add_fusion.1
  206.3 2.1 pad_maximum_fusion
  208.4 4.6 all-to-all-start
  213.7 0.9 fusion.57
  215.7 34.7 %all-to-all-done = bf16[128,8,768]{2,0,1:T(8,128)(2,1)S(1)} async-done(((bf16[128,8,768]{2,0,1:T(8,128)(2,1)}), bf16[128,8,768]{2,0,1:T(8,128)(2,1)S(1)}, u32[]{:S(2)}, u32[]{:S(2)}) %all-to-all-start) | async-done | bytes 1572896 | tf_op jit(solution)/shard_map/all_to_all | solution.py:135
  251.9 0.8 multiply_reduce_fusion
  257.6 1.6 fusion.22
  259.2 5.1 copy.175
  264.3 4.5 all-to-all-start.3
  269.6 8.9 all_gather.54
  278.5 2.7 convolution_convert_fusion.1
  281.2 24.2 %all-to-all-done.3 = bf16[512,2,768]{2,1,0:T(2,128)(2,1)} async-done(((bf16[512,2,768]{2,1,0:T(2,128)(2,1)}), bf16[512,2,768]{2,1,0:T(2,128)(2,1)}, u32[]{:S(2)}, u32[]{:S(2)}) %all-to-all-start.3) | async-done | bytes 1572896 | tf_op jit(solution)/shard_map/all_to_all | solution.py:258
  305.4 2.7 copy.176
  308.1 2.1 copy.177
  310.2 1.6 convert_reduce_fusion.1
  312.4 44.8 %all-gather.19.cloned.1.call-done = bf16[2048,8192]{1,0:T(8,128)(2,1)} async-done(((bf16[256,8192]{1,0:T(8,128)(2,1)}), bf16[2048,8192]{1,0:T(8,128)(2,1)}) %all-gather.19.cloned.1.call-update) | async-done | bytes 33554448 | tf_op jit(solution)/shard_map/all_gather | solution.py:90
  357.2 18.9 %convolution_add_fusion = f32[128,8192]{1,0:T(8,128)} fusion(bf16[128,2048]{1,0:T(8,128)(2,1)S(1)} %copy-done.5, bf16[2048,8192]{1,0:T(8,128)(2,1)} %all-gather.19.cloned.1.call-done, f32[8192]{0:T(1024)S(1)} %convert_element_type.116), kind=kOutput, calls=%fused_computation | convolution fusion | flops 4296015872 | bytes 38305792 | tf_op jit(solution)/shard_map/dot_general | solution.py:176
  376.1 143.6 %all-gather.21.cloned.1.call-done = bf16[8192,2048]{1,0:T(8,128)(2,1)} async-done(((bf16[1024,2048]{1,0:T(8,128)(2,1)}), bf16[8192,2048]{1,0:T(8,128)(2,1)}) %all-gather.21.cloned.1.call-update) | async-done | bytes 33554448 | tf_op jit(solution)/shard_map/all_gather | solution.py:92
  519.8 26.9 %convert_reduce_fusion = (f32[8192]{0:T(1024)}, bf16[128,8192]{1,0:T(8,128)(2,1)}, f32[128,8192]{1,0:T(8,128)}) fusion(f32[128,8192]{1,0:T(8,128)} %convolution_add_fusion, bf16[128,2048]{1,0:T(8,128)(2,1)S(1)} %copy-done.7, bf16[8192,2048]{1,0:T(8,128)(2,1)} %all-gather.21.cloned.1.call-done), kind=kOutput, calls=%fused_computation.4 | convolution fusion | flops 4372553728 | bytes 44597248 | tf_op jit(solution)/shard_map/dot_general | solution.py:57
  546.7 16.5 %fusion.73 = f32[128,2048]{1,0:T(8,128)S(1)} fusion(bf16[128,8192]{1,0:T(8,128)(2,1)} %get-tuple-element.91, bf16[2048,8192]{1,0:T(8,128)(2,1)} %all-gather.19.cloned.1.call-done), kind=kOutput, calls=%fused_computation.146 | convolution fusion | flops 4294967296 | bytes 36700160 | tf_op jit(solution)/shard_map/dot_general | solution.py:57
  563.2 15.3 %fusion.69 = (f32[2048]{0:T(1024)}, f32[128]{0:T(128)S(1)}, f32[128]{0:T(128)S(1)}, f32[2048]{0:T(1024)}, f32[128,2048]{1,0:T(8,128)}) fusion(f32[2048]{0:T(1024)S(1)} %bitcast.124, f32[128]{0:T(128)S(1)} %copy-done.17, bf16[128,2048]{1,0:T(8,128)(2,1)S(1)} %copy-done, f32[128,2048]{1,0:T(8,128)S(1)} %fusion.73, f32[2048]{0:T(1024)S(1)} %bitcast.120, ...), kind=kOutput, calls=%fused_computation.143 | convolution fusion | flops 3223842816 | bytes 29394432 | tf_op jit(solution)/shard_map/dot_general | solution.py:57
  578.6 2.8 fusion.32
  581.4 3.3 convert_reduce_fusion.3
  584.8 4.8 fusion.75
  589.7 23.5 %all-gather.23.cloned.1.call-done = bf16[512,2048]{1,0:T(8,128)(2,1)} async-done(((bf16[128,2048]{1,0:T(8,128)(2,1)}), bf16[512,2048]{1,0:T(8,128)(2,1)}) %all-gather.23.cloned.1.call-update) | async-done | bytes 2097168 | tf_op jit(solution)/shard_map/all_gather | solution.py:199
  613.2 10.2 fusion.74
  623.5 1.6 copy-done.1
  625.1 1.5 copy.202
  626.5 3.9 all-to-all-start.4
  630.5 64.7 %all-gather.27.cloned.1.call-done = bf16[512,2048]{1,0:T(8,128)(2,1)} async-done(((bf16[128,2048]{1,0:T(8,128)(2,1)}), bf16[512,2048]{1,0:T(8,128)(2,1)}) %all-gather.27.cloned.1.call-update) | async-done | bytes 2097168 | tf_op jit(solution)/shard_map/all_gather | solution.py:200
  695.1 9.3 all-to-all-done.4
  704.4 9.8 fusion.76
  714.3 4.0 multiply_convert_fusion
  718.4 52.0 %all_to_all.104 = bf16[128,4,2048]{2,0,1:T(8,128)(2,1)S(1)} all-to-all(bf16[128,4,2048]{2,0,1:T(8,128)(2,1)S(1)} %bitcast.99), channel_id=1, replica_groups=mesh['dp'=8,'seq'=4] {'seq'}, dimensions={1} | all-to-all | bytes 4194304 | tf_op jit(solution)/shard_map/all_to_all | solution.py:204
  770.5 8.2 fusion.77
  778.7 1.1 copy.164
  779.8 3.5 all-to-all-start.1
  783.3 8.9 all-gather.6
  792.2 8.9 all-gather.3
  801.1 0.9 copy.165
  802.0 1.3 copy.166
  803.3 4.7 fusion.7
  808.0 13.9 %fusion.8 = bf16[128,2048]{1,0:T(8,128)(2,1)} fusion(f32[128,2048]{1,0:T(8,128)S(1)} %fusion.7, bf16[128,8192]{1,0:T(8,128)(2,1)S(1)} %multiply_convert_fusion, bf16[8192,2048]{1,0:T(8,128)(2,1)} %all-gather.21.cloned.1.call-done, f32[2048]{0:T(1024)S(1)} %bitcast.129), kind=kOutput, calls=%fused_computation.27 | convolution fusion | flops 4295753728 | bytes 37232640 | tf_op jit(solution)/shard_map/dot_general | solution.py:183
  821.9 5.1 all-reduce.10.cloned.1.call-done
  827.8 1.3 dynamic-slice.3
  829.0 1.3 dynamic-slice.4
  830.3 1.3 dynamic-slice.5
  831.6 1.3 dynamic-slice.6
  832.8 1.3 dynamic-slice
  834.1 1.3 dynamic-slice.2
  835.5 48.3 %reduce-scatter.7.cloned.1.call-done = f32[512,256]{1,0:T(8,128)} async-done(((f32[512,2048]{1,0:T(8,128)}), f32[512,256]{1,0:T(8,128)}) %reduce-scatter.7.cloned.1.call-update) | async-done | bytes 524304 | tf_op jit(solution)/shard_map/reduce_scatter | solution.py:265
  883.8 96.3 %reduce-scatter.5.cloned.1.call-done = f32[256,1536]{1,0:T(8,128)} async-done(((f32[2048,1536]{1,0:T(8,128)}), f32[256,1536]{1,0:T(8,128)}) %reduce-scatter.5.cloned.1.call-update) | async-done | bytes 1572880 | tf_op jit(solution)/shard_map/reduce_scatter | solution.py:264
  980.1 120.2 %reduce-scatter.9.cloned.1.call-done = f32[256,2048]{1,0:T(8,128)} async-done(((f32[2048,2048]{1,0:T(8,128)}), f32[256,2048]{1,0:T(8,128)}) %reduce-scatter.9.cloned.1.call-update) | async-done | bytes 2097168 | tf_op jit(solution)/shard_map/reduce_scatter | solution.py:210
  1100.3 120.0 %reduce-scatter.11.cloned.1.call-done = f32[2048,256]{1,0:T(8,128)} async-done(((f32[2048,2048]{1,0:T(8,128)}), f32[2048,256]{1,0:T(8,128)}) %reduce-scatter.11.cloned.1.call-update) | async-done | bytes 2097168 | tf_op jit(solution)/shard_map/reduce_scatter | solution.py:211
  (151 shorter events, 18.8 us)
Async XLA Ops:
  7.2 60.0 %all-gather.17.cloned.1.call-start = ((), (), s32[]{:S(2)}) async-start(), calls=%async_computation.11 | async-start | bytes 9437184 | tf_op jit(solution)/shard_map/all_gather | solution.py:88
  7.9 186.5 %all-gather.15.cloned.1.call-start = ((), (), s32[]{:S(2)}) async-start(), calls=%async_computation.10 | async-start | bytes 28311552 | tf_op jit(solution)/shard_map/all_gather | solution.py:86
  8.7 348.5 %all-gather.19.cloned.1.call-start = ((), (), s32[]{:S(2)}) async-start(), calls=%async_computation.12 | async-start | bytes 37748736 | tf_op jit(solution)/shard_map/all_gather | solution.py:90
  9.4 1.3 copy-start.24
  9.4 1.5 copy-start
  9.4 2.0 copy-start.25
  9.4 2.0 copy-start.26
  9.4 2.1 copy-start.27
  9.4 2.4 copy-start.28
  9.5 2.4 copy-start.21
  9.5 57.7 %copy-start.6 = (bf16[128,2048]{1,0:T(8,128)(2,1)S(1)}, bf16[128,2048]{1,0:T(8,128)(2,1)}, u32[]{:S(2)}) copy-start(bf16[128,2048]{1,0:T(8,128)(2,1)} %param.29) | copy-start | bytes 1572868
  9.5 510.3 %all-gather.21.cloned.1.call-start = ((), (), s32[]{:S(2)}) async-start(), calls=%async_computation.13 | async-start | bytes 37748736 | tf_op jit(solution)/shard_map/all_gather | solution.py:92
  10.1 574.7 %all-gather.25.cloned.1.call-start = ((), (), s32[]{:S(2)}) async-start(), calls=%async_computation.16 | async-start | bytes 2621440 | tf_op jit(solution)/shard_map/all_gather | solution.py:201
  11.0 62.4 %copy-start.16 = (f32[128]{0:T(128)}, f32[128]{0:T(128)S(1)}, u32[]{:S(2)}) copy-start(f32[128]{0:T(128)S(1)} %broadcast_multiply_fusion.2) | copy-start | bytes 1540
  11.3 0.5 copy-start.22
  11.3 62.1 %copy-start.18 = (f32[128]{0:T(128)}, f32[128]{0:T(128)S(1)}, u32[]{:S(2)}) copy-start(f32[128]{0:T(128)S(1)} %fusion.60) | copy-start | bytes 1540
  57.9 136.5 %copy-start.4 = (bf16[128,2048]{1,0:T(8,128)(2,1)}, bf16[128,2048]{1,0:T(8,128)(2,1)S(1)}, u32[]{:S(2)}) copy-start(bf16[128,2048]{1,0:T(8,128)(2,1)S(1)} %get-tuple-element.102) | copy-start | bytes 1572868
  74.3 134.1 %all-to-all-start.2 = ((bf16[128,8,256]{2,0,1:T(8,128)(2,1)}), bf16[128,8,256]{2,0,1:T(8,128)(2,1)S(1)}, u32[]{:S(2)}, u32[]{:S(2)}) async-start(bf16[128,8,256]{2,0,1:T(8,128)(2,1)} %bitcast.89), calls=%async_computation.2 | async-start | bytes 1048576 | tf_op jit(solution)/shard_map/all_to_all | solution.py:189
  208.4 42.0 %all-to-all-start = ((bf16[128,8,768]{2,0,1:T(8,128)(2,1)}), bf16[128,8,768]{2,0,1:T(8,128)(2,1)S(1)}, u32[]{:S(2)}, u32[]{:S(2)}) async-start(bf16[128,8,768]{2,0,1:T(8,128)(2,1)} %pad_maximum_fusion), calls=%async_computation | async-start | bytes 3145728 | tf_op jit(solution)/shard_map/all_to_all | solution.py:135
  213.0 400.3 %all-gather.23.cloned.1.call-start = ((), (), s32[]{:S(2)}) async-start(), calls=%async_computation.14 | async-start | bytes 2621440 | tf_op jit(solution)/shard_map/all_gather | solution.py:199
  250.5 3.5 copy-start.3
  250.5 1.4 copy-start.10
  251.1 1.7 copy-start.12
  251.6 1.8 copy-start.14
  253.4 1.1 copy-start.11
  259.2 10.4 copy-start.20
  259.2 19.2 %copy-start.13 = (f32[2,512]{1,0:T(2,128)S(1)}, f32[2,512]{1,0:T(2,128)}, u32[]{:S(2)}) copy-start(f32[2,512]{1,0:T(2,128)} %copy-done.12) | copy-start | bytes 12292
  259.2 19.3 %copy-start.15 = (f32[2,512]{1,0:T(2,128)S(1)}, f32[2,512]{1,0:T(2,128)}, u32[]{:S(2)}) copy-start(f32[2,512]{1,0:T(2,128)} %copy-done.14) | copy-start | bytes 12292
  264.3 41.0 %all-to-all-start.3 = ((bf16[512,2,768]{2,1,0:T(2,128)(2,1)}), bf16[512,2,768]{2,1,0:T(2,128)(2,1)}, u32[]{:S(2)}, u32[]{:S(2)}) async-start(bf16[512,2,768]{2,1,0:T(2,128)(2,1)} %copy.175), calls=%async_computation.3 | async-start | bytes 3145728 | tf_op jit(solution)/shard_map/all_to_all | solution.py:258
  268.8 426.3 %all-gather.27.cloned.1.call-start = ((), (), s32[]{:S(2)}) async-start(), calls=%async_computation.18 | async-start | bytes 2621440 | tf_op jit(solution)/shard_map/all_gather | solution.py:200
  269.5 557.5 %all-reduce.10.cloned.1.call-start = ((), (), s32[]{:S(2)}) async-start(), calls=%async_computation.21 | async-start | bytes 196608
  308.1 49.1 %copy-start.5 = (bf16[128,2048]{1,0:T(8,128)(2,1)S(1)}, bf16[128,2048]{1,0:T(8,128)(2,1)}, u32[]{:S(2)}) copy-start(bf16[128,2048]{1,0:T(8,128)(2,1)} %get-tuple-element.101) | copy-start | bytes 1572868
  312.4 207.4 %copy-start.7 = (bf16[128,2048]{1,0:T(8,128)(2,1)S(1)}, bf16[128,2048]{1,0:T(8,128)(2,1)}, u32[]{:S(2)}) copy-start(bf16[128,2048]{1,0:T(8,128)(2,1)} %param.29) | copy-start | bytes 1572868
  546.7 16.6 %copy-start.17 = (f32[128]{0:T(128)S(1)}, f32[128]{0:T(128)}, u32[]{:S(2)}) copy-start(f32[128]{0:T(128)} %copy-done.16) | copy-start | bytes 1540
  563.2 15.3 %copy-start.23 = (f32[128]{0:T(128)S(1)}, f32[128]{0:T(128)}, u32[]{:S(2)}) copy-start(f32[128]{0:T(128)} %copy-done.22) | copy-start | bytes 1540
  563.2 15.4 %copy-start.19 = (f32[128]{0:T(128)S(1)}, f32[128]{0:T(128)}, u32[]{:S(2)}) copy-start(f32[128]{0:T(128)} %copy-done.18) | copy-start | bytes 1540
  578.5 2.8 copy-start.2
  578.6 6.2 copy-start.9
  584.7 299.1 %reduce-scatter.7.cloned.1.call-start = ((), (), s32[]{:S(2)}) async-start(), calls=%async_computation.17 | async-start | bytes 4718592 | tf_op jit(solution)/shard_map/reduce_scatter | solution.py:265
  589.7 390.4 %reduce-scatter.5.cloned.1.call-start = ((), (), s32[]{:S(2)}) async-start(), calls=%async_computation.15 | async-start | bytes 14155776 | tf_op jit(solution)/shard_map/reduce_scatter | solution.py:264
  623.5 1.6 copy-start.1
  626.5 77.9 %all-to-all-start.4 = ((bf16[128,4,2048]{2,0,1:T(8,128)(2,1)}), bf16[128,4,2048]{2,0,1:T(8,128)(2,1)S(1)}, u32[]{:S(2)}, u32[]{:S(2)}) async-start(bf16[128,4,2048]{2,0,1:T(8,128)(2,1)} %bitcast.98), calls=%async_computation.6 | async-start | bytes 4194304 | tf_op jit(solution)/shard_map/all_to_all | solution.py:205
  630.4 469.9 %reduce-scatter.9.cloned.1.call-start = ((), (), s32[]{:S(2)}) async-start(), calls=%async_computation.19 | async-start | bytes 18874368 | tf_op jit(solution)/shard_map/reduce_scatter | solution.py:210
  714.3 506.0 %reduce-scatter.11.cloned.1.call-start = ((), (), s32[]{:S(2)}) async-start(), calls=%async_computation.20 | async-start | bytes 18874368 | tf_op jit(solution)/shard_map/reduce_scatter | solution.py:211
  718.4 52.0 %copy-start.8 = (bf16[512,2048]{1,0:T(8,128)(2,1)S(1)}, bf16[512,2048]{1,0:T(8,128)(2,1)}, u32[]{:S(2)}) copy-start(bf16[512,2048]{1,0:T(8,128)(2,1)} %all-gather.25.cloned.1.call-done) | copy-start | bytes 6291460
  778.7 4.6 copy-start.29
  778.7 4.6 copy-start.30
  779.8 21.3 %all-to-all-start.1 = ((bf16[512,2,256]{2,1,0:T(2,128)(2,1)}), bf16[512,2,256]{2,1,0:T(2,128)(2,1)S(1)}, u32[]{:S(2)}, u32[]{:S(2)}) async-start(bf16[512,2,256]{2,1,0:T(2,128)(2,1)} %copy.164), calls=%async_computation.1 | async-start | bytes 1048576 | tf_op jit(solution)/shard_map/all_to_all | solution.py:173
  827.8 393.0 %copy-start.31 = (f32[64]{0:T(128)}, f32[64]{0:T(128)S(1)}, u32[]{:S(2)}) copy-start(f32[64]{0:T(128)S(1)} %dynamic-slice.1) | copy-start | bytes 772
Sparse Core Ops, SparseCore 0:
  9.9 57.1 all-gather.16
  69.0 125.3 all-gather.14
  196.3 160.8 all-gather.18
  358.9 160.7 all-gather.20
  521.2 45.9 all-gather.24
  568.5 44.6 all-gather.22
  615.4 79.7 all-gather.26
  701.6 125.4 all-reduce.9
  831.3 52.4 reduce-scatter.6
  887.7 92.3 reduce-scatter.4
  984.3 115.9 reduce-scatter.8
  1104.3 115.9 reduce-scatter.10
where the time goes:
time: 1240 us; the launch traced here: 1230 us
  waiting for transfers between devices  864 us (70%)
  matrix products  152 us (12%)
  blocking collectives  123 us (10%)
  local copies, waits for them, and re-layouts  31.2 us (3%)
  starting transfers between devices  21.9 us (2%)
  other arithmetic  21 us (2%)
  between operations  15.3 us (1%)
    all_gather x1, waiting for transfers between devices, on_device(): lax.all_gather(down_weight, 'dp', axis=0, tiled=True)  144 us
    reduce_scatter x1, waiting for transfers between devices, on_device(): lax.psum_scatter(part_up, 'dp', scatter_dimension=0, tiled=True)  120 us
    reduce_scatter x1, waiting for transfers between devices, on_device(): lax.psum_scatter(part_down, 'dp', scatter_dimension=1, tiled=True)  120 us
    all_gather x1, waiting for transfers between devices, on_device(): lax.all_gather(qkv_weight, 'dp', axis=0, tiled=True)  116 us
    reduce_scatter x1, waiting for transfers between devices, on_device(): lax.psum_scatter(part_qkv, 'dp', scatter_dimension=0, tiled=True)  96.3 us
    dot_general x4, matrix products, times_transposed(): lax.dot_general(left, right, (((1,), (1,)), ((), ())), preferred_element_...  65 us
    all_gather x1, waiting for transfers between devices, on_device(): lax.all_gather(normed_two, 'seq', axis=0, tiled=True)  64.7 us
    all_to_all x1, blocking collectives, on_device(): lax.all_to_all(activated, 'seq', split_axis=1, concat_axis=0, tiled=True)  52 us
  transfers between devices with their start and end apart: 17, of which 14 were waited for; matrix products, arithmetic and copies ran while one was open for 16% of the time, Pallas kernels for 0%

commit v1 on v0

v1 whole, which is shorter than its diff:
```python
import jax
import jax.numpy as jnp
from jax import lax
from jax.sharding import PartitionSpec as P

H = 8
HS = 256
ROT = 64
F32 = jnp.float32
BF16 = jnp.bfloat16


def matmul(left, right):
    return jnp.dot(left, right, preferred_element_type=F32)


def times_transposed(left, right):
    return lax.dot_general(left, right, (((1,), (1,)), ((), ())), preferred_element_type=F32)


def left_transposed(left, right):
    return lax.dot_general(left, right, (((0,), (0,)), ((), ())), preferred_element_type=F32)


def doc_layout(lengths_row, places):
    starts = jnp.cumsum(lengths_row) - lengths_row
    after = places[:, None] >= starts[None, :]
    doc_ids = jnp.sum(after.astype(jnp.int32), axis=1)
    begins = jnp.max(jnp.where(after, starts[None, :], 0), axis=1)
    return (doc_ids, places - begins)


def turn_tables(positions, rot_dims):
    half_rot = rot_dims // 2
    inverse = 10000.0 ** (-(jnp.arange(half_rot, dtype=F32) * 2.0 / rot_dims))
    angles = positions.astype(F32)[:, None] * inverse[None, :]
    angles = jnp.concatenate([angles, angles], axis=1)
    return (jnp.cos(angles), jnp.sin(angles))


def rotate(values, cosine, sine_table):
    half_rot = ROT // 2
    leading = values[..., :ROT]
    swapped = jnp.concatenate([-leading[..., half_rot:], leading[..., :half_rot]], axis=-1)
    turned = leading * cosine[..., None, :] + swapped * sine_table[..., None, :]
    return jnp.concatenate([turned, values[..., ROT:]], axis=-1)


def unrotate(gradient, cosine, sine_table):
    half_rot = ROT // 2
    leading = gradient[..., :ROT]
    scaled = leading * sine_table[..., None, :]
    moved = jnp.concatenate([scaled[..., half_rot:], -scaled[..., :half_rot]], axis=-1)
    return jnp.concatenate(
        [leading * cosine[..., None, :] + moved, gradient[..., ROT:]], axis=-1
    )


class Place:
    def __init__(self):
        self.n_dp = lax.axis_size("dp")
        self.n_seq = lax.axis_size("seq")
        assert self.n_dp == 2 * self.n_seq
        self.split = 2 if H % (2 * self.n_seq) == 0 else 1
        self.blocks = self.n_dp // self.split
        self.dp = lax.axis_index("dp")
        self.z = lax.axis_index("seq")
        self.block = self.dp // self.split
        self.part = self.dp % self.split
        self.masks = [1 << k for k in range(self.blocks.bit_length() - 1)]
        self.order = [k ^ (k >> 1) for k in range(self.blocks)]

    def swap(self, value, mask):
        return lax.ppermute(value, "dp", [(i, i ^ mask) for i in range(self.n_dp)])

    def to_relative(self, value, axis):
        size = value.shape[axis] // self.blocks
        return jnp.concatenate(
            [
                lax.dynamic_slice_in_dim(value, (self.block ^ off) * size, size, axis)
                for off in self.order
            ],
            axis=axis,
        )

    def to_natural(self, value, axis):
        size = value.shape[axis] // self.blocks
        table = [0] * self.blocks
        for position, off in enumerate(self.order):
            table[off] = position
        table = jnp.array(table, jnp.int32)
        return jnp.concatenate(
            [
                lax.dynamic_slice_in_dim(value, table[self.block ^ k] * size, size, axis)
                for k in range(self.blocks)
            ],
            axis=axis,
        )

    def pair(self, own, other, axis):
        return jnp.where(
            self.part == 0,
            jnp.concatenate([own, other], axis=axis),
            jnp.concatenate([other, own], axis=axis),
        )

    def gather(self, piece):
        half = piece.shape[0] // 2
        gathered = []
        for rows, masks in ((piece[:half], self.masks), (piece[half:], self.masks[::-1])):
            have = {0: rows}
            for mask in masks:
                offs = list(have)
                sent = jnp.concatenate([have[o] for o in offs], 0) if len(offs) > 1 else have[offs[0]]
                got = self.swap(sent, mask * self.split)
                for k, o in enumerate(offs):
                    have[o ^ mask] = got[k * half : (k + 1) * half]
            gathered.append(have)
        return gathered

    def spread(self, piece):
        chips = self.n_dp // 2
        masks = [1 << k for k in range(chips.bit_length() - 1)]
        offset = (self.dp // 2) ^ self.z
        half = piece.shape[0] // 2
        result = []
        for rows, order in ((piece[:half], masks), (piece[half:], masks[::-1])):
            held = [0]
            for mask in order:
                pairs = [
                    (
                        (2 * (z ^ o) + c) * self.n_seq + z,
                        (2 * (z ^ o ^ mask) + c) * self.n_seq + z,
                    )
                    for z in range(self.n_seq)
                    for o in held
                    for c in range(2)
                ]
                got = lax.ppermute(rows, ("dp", "seq"), pairs)
                takes = jnp.zeros((), jnp.bool_)
                for o in held:
                    takes = takes | (offset == (o ^ mask))
                rows = jnp.where(takes, got, rows)
                held = held + [o ^ mask for o in held]
            result.append(rows)
        return jnp.concatenate(result, axis=0)

    def scatter_sum(self, product, halves):
        out = []
        for half, masks in zip(halves, (self.masks, self.masks[::-1])):
            live = list(range(self.blocks))
            extra = {}

            def total(offs):
                whole = product(half, offs)
                if all(o not in extra for o in offs):
                    return whole
                axis, size = whole.ndim and product.axis, whole.shape[product.axis] // len(offs)
                parts = []
                for k, o in enumerate(offs):
                    value = lax.slice_in_dim(whole, k * size, (k + 1) * size, axis=axis)
                    for more in extra.get(o, ()):
                        value = value + more.astype(F32)
                    parts.append(value)
                return parts[0] if len(parts) == 1 else jnp.concatenate(parts, axis=axis)

            for mask in masks:
                away = [o for o in self.order if o in live and o & mask]
                sent = total(away).astype(BF16)
                got = self.swap(sent, mask * self.split)
                size = got.shape[product.axis] // len(away)
                for k, o in enumerate(away):
                    extra.setdefault(o ^ mask, []).append(
                        lax.slice_in_dim(got, k * size, (k + 1) * size, axis=product.axis)
                    )
                live = [o for o in live if not o & mask]
            out.append(total([0]))
        return out


class Product:
    def __init__(self, place, by_block, other, axis):
        self.place, self.by_block, self.other, self.axis = place, by_block, other, axis
        self.size = by_block.shape[1] // place.blocks

    def __call__(self, half, offs):
        where = [self.place.order.index(o) for o in offs]
        if where == list(range(where[0], where[0] + len(where))):
            blocks = self.by_block[:, where[0] * self.size : (where[-1] + 1) * self.size]
        else:
            blocks = jnp.concatenate(
                [self.by_block[:, w * self.size : (w + 1) * self.size] for w in where], axis=1
            )
        width = self.other.shape[1] // 2
        others = self.other[:, half * width : (half + 1) * width]
        if self.axis == 0:
            return left_transposed(blocks, others)
        return left_transposed(others, blocks)


def on_device(
    tokens,
    doc_lengths,
    qkv_weight,
    qkv_bias,
    dense_weight,
    dense_bias,
    up_weight,
    up_bias,
    down_weight,
    down_bias,
    norm1_gain,
    norm1_shift,
    norm2_gain,
    norm2_shift,
    cotangent,
):
    here = Place()
    n_dp, n_seq, split, blocks = here.n_dp, here.n_seq, here.split, here.blocks
    z, part = here.z, here.part
    rows_here, width = tokens.shape
    seq_len = rows_here * n_seq
    hidden_rows = down_weight.shape[0]
    slice_rows = hidden_rows // n_seq
    heads_here = H // (n_seq * split)
    head_cols = heads_here * 3 * HS

    tokens_rel = here.to_relative(tokens, 1)
    x_stream = lax.all_gather(tokens_rel, "seq", axis=0, tiled=True)
    g_stream = lax.all_gather(cotangent, "seq", axis=0, tiled=True)
    if split == 2:
        x_all = jnp.concatenate([x_stream, here.swap(x_stream, 1)], axis=0)
        g_all = jnp.concatenate([g_stream, here.swap(g_stream, 1)], axis=0)
        lengths = jnp.concatenate([doc_lengths, here.swap(doc_lengths, 1)], axis=0)
    else:
        x_all, g_all, lengths = x_stream, g_stream, doc_lengths
    g_rel = here.to_relative(g_all, 1)

    def up_columns(core):
        return jnp.concatenate(
            [
                lax.dynamic_slice_in_dim(
                    up_weight, (k * split + core) * hidden_rows + z * slice_rows, slice_rows, 1
                )
                for k in range(blocks)
            ],
            axis=1,
        )

    def qkv_columns(core):
        return lax.dynamic_slice_in_dim(qkv_weight, (z * split + core) * head_cols, head_cols, 1)

    def rows_of_d(columns):
        piece = columns(part)
        if split == 2:
            piece = here.pair(piece, here.swap(columns(1 - part), 1), 0)
        gathered = here.gather(piece)
        return jnp.concatenate(
            [half[o] for o in here.order for half in gathered], axis=0
        )

    w_up = rows_of_d(up_columns)
    down_piece = lax.dynamic_slice_in_dim(down_weight, z * slice_rows, slice_rows, 0)
    down_halves = here.gather(down_piece)
    w_down = jnp.zeros((blocks * slice_rows, width), BF16)
    half_rows = slice_rows // 2
    for index, half in enumerate(down_halves):
        for o in range(blocks):
            w_down = lax.dynamic_update_slice_in_dim(
                w_down, half[o], (here.block ^ o) * slice_rows + index * half_rows, 0
            )
    w_qkv = rows_of_d(qkv_columns)
    w_dense = here.spread(dense_weight)
    if split == 1:
        other = here.swap(w_dense, 1)
        w_dense = jnp.where(
            here.dp % 2 == 0,
            jnp.concatenate([w_dense, other], 0),
            jnp.concatenate([other, w_dense], 0),
        )

    small = (qkv_bias, up_bias, dense_bias, down_bias, norm1_gain, norm1_shift, norm2_gain, norm2_shift)
    packed_small = lax.all_gather(jnp.concatenate(small)[None], "dp", axis=0, tiled=True)
    spans, first = [], 0
    for value in small:
        spans.append(packed_small[:, first : first + value.shape[0]].astype(F32))
        first += value.shape[0]
    b_qkv, b_up, b_dense, b_down, gain_one, shift_one, gain_two, shift_two = spans
    b_qkv = lax.dynamic_slice_in_dim(b_qkv.reshape(-1), (z * split + part) * head_cols, head_cols, 0)
    b_up = lax.dynamic_slice_in_dim(b_up, z * slice_rows, slice_rows, 1).reshape(
        blocks, split, slice_rows
    )
    b_up = lax.dynamic_index_in_dim(b_up, part, 1, keepdims=False).reshape(-1)
    b_out = (b_dense + b_down).reshape(-1)
    gain_one, shift_one, gain_two, shift_two = (
        here.to_relative(v.reshape(-1), 0) for v in (gain_one, shift_one, gain_two, shift_two)
    )

    def standardize(values):
        values = values.astype(F32)
        average = jnp.mean(values, axis=-1, keepdims=True)
        centred = values - average
        variance = jnp.mean(centred * centred, axis=-1, keepdims=True)
        inverse = lax.rsqrt(variance + 1e-05)
        return centred * inverse, inverse

    xhat, _ = standardize(x_all)
    normed_one = (xhat * gain_one + shift_one).astype(BF16)
    normed_two = (xhat * gain_two + shift_two).astype(BF16)

    hidden = matmul(normed_two, w_up) + b_up
    cdf = 0.5 + 0.5 * lax.erf(hidden * (0.5**0.5))
    activated = (hidden * cdf).astype(BF16)
    slope = cdf + hidden * (jnp.exp(-0.5 * hidden * hidden) * 0.3989422804014327)
    sum_down = here.scatter_sum(Product(here, g_rel, activated, 1), (0, 1))
    branches = matmul(activated, w_down)
    grad_hidden = (times_transposed(g_all, w_down) * slope).astype(BF16)
    grad_up_bias = jnp.sum(grad_hidden.astype(F32), axis=0)
    sum_up = here.scatter_sum(Product(here, normed_two, grad_hidden, 0), (0, 1))
    grad_two = times_transposed(grad_hidden, w_up)

    places = jnp.arange(seq_len, dtype=jnp.int32)
    doc_ids, positions = jax.vmap(lambda row: doc_layout(row, places))(lengths)
    cosine, sine = jax.vmap(lambda p: turn_tables(p, ROT))(positions)
    allowed = (doc_ids[:, :, None] == doc_ids[:, None, :]) & (
        places[None, None, :] <= places[None, :, None]
    )
    allowed = allowed[:, None]
    projected = (matmul(normed_one, w_qkv) + b_qkv).reshape(split, seq_len, heads_here, 3 * HS)
    queries = rotate(projected[..., :HS], cosine, sine).astype(BF16)
    keys = rotate(projected[..., HS : 2 * HS], cosine, sine).astype(BF16)
    values = projected[..., 2 * HS :].astype(BF16)
    scale = HS ** (-0.5)
    scores = jnp.einsum("bqhd,bkhd->bhqk", queries, keys, preferred_element_type=F32) * scale
    masked = jnp.where(allowed, scores, -1e30)
    largest = jnp.max(masked, axis=-1, keepdims=True)
    exponent = jnp.exp(masked - largest)
    probs = exponent / jnp.sum(exponent, axis=-1, keepdims=True)
    probs_low = probs.astype(BF16)
    attended = jnp.einsum("bhqk,bkhd->bqhd", probs_low, values, preferred_element_type=F32)
    attended = attended.astype(BF16).reshape(split * seq_len, heads_here * HS)
    sum_dense = here.scatter_sum(Product(here, g_rel, attended, 1), (0, 1))
    branches = branches + matmul(attended, w_dense)
    grad_attended = times_transposed(g_all, w_dense).astype(BF16)
    grad_attended = grad_attended.reshape(split, seq_len, heads_here, HS)
    grad_probs = jnp.einsum("bqhd,bkhd->bhqk", grad_attended, values, preferred_element_type=F32)
    inner = jnp.sum(probs * grad_probs, axis=-1, keepdims=True)
    grad_scores = (probs * (grad_probs - inner)).astype(BF16)
    grad_queries = jnp.einsum("bhqk,bkhd->bqhd", grad_scores, keys, preferred_element_type=F32)
    grad_keys = jnp.einsum("bhqk,bqhd->bkhd", grad_scores, queries, preferred_element_type=F32)
    grad_values = jnp.einsum("bhqk,bqhd->bkhd", probs_low, grad_attended, preferred_element_type=F32)
    grad_projected = jnp.concatenate(
        [
            unrotate(grad_queries * scale, cosine, sine),
            unrotate(grad_keys * scale, cosine, sine),
            grad_values,
        ],
        axis=-1,
    ).astype(BF16)
    grad_projected = grad_projected.reshape(split * seq_len, head_cols)
    grad_qkv_bias = jnp.sum(grad_projected.astype(F32), axis=0)
    sum_qkv = here.scatter_sum(Product(here, normed_one, grad_projected, 0), (0, 1))
    grad_one = times_transposed(grad_projected, w_qkv)

    def join(partial_sum):
        own = partial_sum[:seq_len]
        if split == 2:
            own = own + here.swap(partial_sum[seq_len:].astype(BF16), 1).astype(F32)
        return lax.psum_scatter(own.astype(BF16), "seq", scatter_dimension=0, tiled=True).astype(F32)

    branch_rows = join(branches)
    term_rows = join(grad_one * gain_one + grad_two * gain_two)
    output = (tokens.astype(F32) + branch_rows + b_out).astype(BF16)
    xhat_here, inverse_here = standardize(tokens_rel)
    term = (
        term_rows
        - jnp.mean(term_rows, axis=-1, keepdims=True)
        - xhat_here * jnp.mean(term_rows * xhat_here, axis=-1, keepdims=True)
    ) * inverse_here
    cotan_rows = cotangent.astype(F32)
    input_grad = (cotan_rows + here.to_natural(term, 1)).astype(BF16)

    norm_sums = [
        jnp.sum(grad_one * xhat, axis=0),
        jnp.sum(grad_one, axis=0),
        jnp.sum(grad_two * xhat, axis=0),
        jnp.sum(grad_two, axis=0),
    ]
    norm_sums = [here.to_natural(v, 0) for v in norm_sums]
    wide_qkv = lax.dynamic_update_slice_in_dim(
        jnp.zeros((H * 3 * HS,), F32), grad_qkv_bias, (z * split + part) * head_cols, 0
    )
    wide_up = lax.dynamic_update_slice(
        jnp.zeros((blocks, split, n_seq, slice_rows), F32),
        grad_up_bias.reshape(blocks, 1, 1, slice_rows),
        (0, part, z, 0),
    )
    column_total = jnp.sum(cotan_rows, axis=0)
    devices = n_dp * n_seq
    wide = [wide_qkv, wide_up, column_total] + norm_sums
    wide = [v.reshape(devices, -1) for v in wide]
    sizes = [v.shape[1] for v in wide]
    swapped = lax.all_to_all(
        jnp.concatenate(wide, axis=1), ("dp", "seq"), split_axis=0, concat_axis=0, tiled=True
    )
    total = jnp.sum(swapped, axis=0)
    sums, first = [], 0
    for size in sizes:
        sums.append(total[first : first + size])
        first += size
    sum_qkv_bias, sum_up_bias, sum_column, sum_gain_one, sum_shift_one, sum_gain_two, sum_shift_two = sums

    def to_plane(halves, axis):
        whole = jnp.concatenate(halves, axis=axis).astype(BF16)
        moved = lax.all_to_all(whole, "seq", split_axis=axis, concat_axis=axis, tiled=True)
        if split == 1:
            per = moved.shape[axis] // (n_seq * 2)
            if axis == 0:
                moved = moved.reshape(n_seq, 2, per, -1).transpose(1, 0, 2, 3).reshape(moved.shape)
            else:
                moved = moved.reshape(-1, n_seq, 2, per).transpose(0, 2, 1, 3).reshape(moved.shape)
        return moved

    def to_cores(value, axis):
        if split == 1:
            return value.astype(F32)
        size = value.shape[axis] // 2
        mine = lax.dynamic_slice_in_dim(value, part * size, size, axis)
        other = lax.dynamic_slice_in_dim(value, (1 - part) * size, size, axis)
        return here.pair(mine, here.swap(other, 1), 1 - axis).astype(F32)

    grad_up = to_cores(to_plane(sum_up, 1), 0)
    grad_down = to_cores(to_plane(sum_down, 0), 1)
    grad_qkv = to_cores(jnp.concatenate(sum_qkv, axis=1), 0)
    grad_dense = to_cores(jnp.concatenate(sum_dense, axis=0), 1)
    return (
        output,
        input_grad,
        grad_qkv,
        sum_qkv_bias,
        grad_dense,
        sum_column,
        grad_up,
        sum_up_bias,
        grad_down,
        sum_column,
        sum_gain_one,
        sum_shift_one,
        sum_gain_two,
        sum_shift_two,
    )


def solution(mesh):
    rows = P(("dp", "seq"), None)
    flat = P(("dp", "seq"))
    placed = (rows,) + (P("dp", None),) * 2 + (P("dp"), P("dp", None)) * 3 + (P("dp"),) * 5 + (rows,)
    return jax.shard_map(
        on_device,
        mesh=mesh,
        in_specs=placed,
        out_specs=(
            rows,
            rows,
            P("dp", "seq"),
            flat,
            P("seq", "dp"),
            flat,
            P("dp", "seq"),
            flat,
            P("seq", "dp"),
            flat,
            flat,
            flat,
            flat,
            flat,
        ),
        check_vma=False,
    )
```

time: 1240 us -> 563 us (0.45)
  waiting for transfers between devices: 864 us -> 177 us
  blocking collectives: 123 us -> 17.1 us
  other arithmetic: 21 us -> 79.4 us
  local copies, waits for them, and re-layouts: 31.2 us -> 81.4 us
  starting transfers between devices: 21.9 us -> 61.4 us
  matrix products: 152 us -> 120 us
    all_gather x7 -> x2, waiting for transfers between devices: 401 us -> 0.01 us  [the longest x1 0.01 us: on_device(): x_stream = lax.all_gather(tokens_rel, 'seq', axis=0, tiled=True)]
    reduce_scatter x4 -> x2, waiting for transfers between devices: 385 us -> 0.02 us  [join(): lax.psum_scatter(own.astype(BF16), 'seq', scatter_dimension=0, tiled=True)]
    ppermute x0 -> x43, waiting for transfers between devices: none -> 126 us  [the longest x39 99.6 us: swap(): return lax.ppermute(value, 'dp', [(i, i ^ mask) for i in range(self.n_dp)])]
    all_gather x8 -> x1, blocking collectives: 70.8 us -> 17.1 us  [on_device(): lax.all_gather(jnp.concatenate(small)[None], 'dp', axis=0, tiled=True)]
    all_to_all x1 -> x0, blocking collectives: 52 us -> none  [on_device(): lax.all_to_all(activated, 'seq', split_axis=1, concat_axis=0, tiled=True)]
    ppermute x0 -> x43, starting transfers between devices: none -> 49.5 us  [the longest x39 38.9 us: swap(): return lax.ppermute(value, 'dp', [(i, i ^ mask) for i in range(self.n_dp)])]
    dot_general x4, matrix products: 65 us -> 24.8 us  [times_transposed(): lax.dot_general(left, right, (((1,), (1,)), ((), ())), preferred_element_...]
    dot_general x4 -> x24, matrix products: 33.1 us -> 52.9 us  [left_transposed(): lax.dot_general(left, right, (((0,), (0,)), ((), ())), preferred_element_...]
  transfers between devices with their start and end apart: 17 -> 50, of which waited for: 14 -> 17; matrix products, arithmetic and copies ran while one was open for 16% -> 32% of each run, Pallas kernels for 0% -> 0%
where the time goes in v1:
time: 563 us; the launch traced here: 554 us
  waiting for transfers between devices  177 us (31%)
  matrix products  120 us (21%)
  local copies, waits for them, and re-layouts  81.4 us (14%)
  other arithmetic  79.4 us (14%)
  starting transfers between devices  61.4 us (11%)
  between operations  18.2 us (3%)
  blocking collectives  17.1 us (3%)
    ppermute x39, waiting for transfers between devices, swap(): return lax.ppermute(value, 'dp', [(i, i ^ mask) for i in range(self.n_dp)])  99.6 us
    dot_general x24, matrix products, left_transposed(): lax.dot_general(left, right, (((0,), (0,)), ((), ())), preferred_element_...  52.9 us
    all_to_all x2, waiting for transfers between devices, to_plane(): lax.all_to_all(whole, 'seq', split_axis=axis, concat_axis=axis, tiled=True)  44.3 us
    ppermute x39, starting transfers between devices, swap(): return lax.ppermute(value, 'dp', [(i, i ^ mask) for i in range(self.n_dp)])  38.9 us
    dot_general x4, matrix products, matmul(): return jnp.dot(left, right, preferred_element_type=F32)  30.8 us
    ppermute x4, waiting for transfers between devices, spread(): got = lax.ppermute(rows, ('dp', 'seq'), pairs)  26.6 us
    unnamed x189, local copies, waits for them, and re-layouts  26.6 us
    dot_general x4, matrix products, times_transposed(): lax.dot_general(left, right, (((1,), (1,)), ((), ())), preferred_element_...  24.8 us
  transfers between devices with their start and end apart: 50, of which 17 were waited for; matrix products, arithmetic and copies ran while one was open for 32% of the time, Pallas kernels for 0%

profile of v1, /device:TPU:0, one launch (start us, length us, event | category | flops | bytes accessed | tf_op | source)
XLA Modules:
  0.0 553.9 jit_solution(15644868435766295127)
XLA Ops:
  12.6 2.5 broadcast_in_dim.22
  17.1 2.5 collective-permute-start.6
  23.1 2.7 collective-permute-start.16
  31.2 17.1 %all-gather.1 = bf16[8,1,3328]{2,1,0:T(2,128)(2,1)S(1)} all-gather(bf16[1,1,3328]{2,1,0:T(2,128)(2,1)S(1)} %reshape.499), channel_id=2, replica_groups=mesh['dp'=8,'seq'=4] {'dp'}, dimensions={0}, use_global_device_ids=true | all-gather | bytes 59904 | tf_op jit(solution)/shard_map/all_gather | solution.py:283
  79.6 7.7 %constant_dynamic-update-slice_fusion.2 = (bf16[2048,1024]{1,0:T(8,128)(2,1)}, bf16[512,1024]{1,0:T(8,128)(2,1)S(1)}) fusion(bf16[256,256]{1,0:T(8,128)(2,1)S(1)} %get-tuple-element.98, bf16[256,256]{1,0:T(8,128)(2,1)S(1)} %get-tuple-element.99, bf16[256,256]{1,0:T(8,128)(2,1)S(1)} %get-tuple-element.100, bf16[256,256]{1,0:T(8,128)(2,1)S(1)} %get-tuple-element.101, ...), kind=kLoop, calls=%fused_computation.247 | loop fusion | flops 11010047 | bytes 3145729
  88.1 2.1 collective-permute-start.3
  91.3 2.4 collective-permute-done.12
  95.6 4.1 collective-permute-start.17
  99.8 5.1 collective-permute-done.3
  105.0 2.5 collective-permute-start.14
  109.5 2.1 collective-permute-done.19
  111.6 2.5 collective-permute-start.4
  114.1 24.5 %collective-permute-done.17 = bf16[128,2048]{1,0:T(8,128)(2,1)S(1)} collective-permute-done((bf16[128,2048]{1,0:T(8,128)(2,1)S(1)}, bf16[128,2048]{1,0:T(8,128)(2,1)S(1)}, u32[]{:S(2)}, u32[]{:S(2)}) %collective-permute-start.17) | collective-permute-done | bytes 524320 | tf_op jit(solution)/shard_map/ppermute | solution.py:139
  138.7 2.5 collective-permute-start.5
  145.7 9.8 %collective-permute-done.14 = bf16[512,768]{1,0:T(8,128)(2,1)S(1)} collective-permute-done((bf16[512,768]{1,0:T(8,128)(2,1)S(1)}, bf16[512,768]{1,0:T(8,128)(2,1)S(1)}, u32[]{:S(2)}, u32[]{:S(2)}) %collective-permute-start.14) | collective-permute-done | bytes 786464 | tf_op jit(solution)/shard_map/ppermute | solution.py:74
  155.7 33.3 %collective-permute-done.8 = bf16[128,2048]{1,0:T(8,128)(2,1)S(1)} collective-permute-done((bf16[128,2048]{1,0:T(8,128)(2,1)S(1)}, bf16[128,2048]{1,0:T(8,128)(2,1)S(1)}, u32[]{:S(2)}, u32[]{:S(2)}) %collective-permute-start.8) | collective-permute-done | bytes 524320 | tf_op jit(solution)/shard_map/ppermute | solution.py:74
  198.9 16.3 %collective-permute-done.9 = bf16[256,2048]{1,0:T(8,128)(2,1)S(1)} collective-permute-done((bf16[256,2048]{1,0:T(8,128)(2,1)}, bf16[256,2048]{1,0:T(8,128)(2,1)S(1)}, u32[]{:S(2)}, u32[]{:S(2)}) %collective-permute-start.9) | collective-permute-done | bytes 1048608 | tf_op jit(solution)/shard_map/ppermute | solution.py:74
  221.2 2.2 convert_reduce_fusion
  223.4 3.0 fusion.13
  228.6 5.6 %fusion.8 = (bf16[1024,2048]{1,0:T(8,128)(2,1)S(1)}, bf16[1024,2048]{1,0:T(8,128)(2,1)S(1)}) fusion(f32[2048]{0:T(1024)S(1)} %copy-done.62, f32[2048]{0:T(1024)S(1)} %pad_maximum_fusion.43, f32[1024]{0:T(1024)S(1)} %add_rsqrt_fusion, f32[1024]{0:T(1024)S(1)} %broadcast_multiply_fusion, bf16[512,2048]{1,0:T(8,128)(2,1)} %collective-permute-done, ...), kind=kLoop, calls=%fused_computation.10 | loop fusion | flops 25165824 | bytes 12623872 | tf_op jit(solution)/shard_map/convert_element_type | solution.py:309
  234.3 11.3 %multiply_convert_fusion = (bf16[1024,1024]{1,0:T(8,128)(2,1)}, f32[1024,1024]{1,0:T(8,128)S(1)}) fusion(f32[1024]{0:T(1024)S(1)} %bitcast.140, bf16[1024,2048]{1,0:T(8,128)(2,1)S(1)} %get-tuple-element.91, bf16[2048,1024]{1,0:T(8,128)(2,1)} %constant_dynamic-update-slice_fusion), kind=kOutput, calls=%fused_computation.32 | convolution fusion | flops 4301258752 | bytes 14684160 | tf_op jit(solution)/shard_map/dot_general | solution.py:14
  245.5 8.5 %convert_reduce_fusion.1 = (f32[1024]{0:T(1024)}, bf16[1024,1024]{1,0:T(8,128)(2,1)S(1)}) fusion(f32[1024,1024]{1,0:T(8,128)S(1)} %get-tuple-element.200, f32[1024]{0:T(1024)S(1)} %bitcast.141, bf16[1024,2048]{1,0:T(8,128)(2,1)S(1)} %constant_dynamic-update-slice_fusion.6, bf16[1024,2048]{1,0:T(8,128)(2,1)} %slice_dynamic-update-slice_fusion), kind=kOutput, calls=%fused_computation.31 | convolution fusion | flops 4308597760 | bytes 14688256 | tf_op jit(solution)/shard_map/dot_general | solution.py:18
  254.0 2.3 fusion.30
  258.1 2.3 fusion.33
  262.7 3.4 convolution_add_fusion.1
  268.1 3.5 fusion.152
  271.6 4.0 fusion.199
  275.6 3.2 fusion.54
  293.4 3.9 fusion.39
  297.4 2.8 fusion.146
  300.2 4.1 concatenate.325
  304.3 3.9 fusion.36
  309.5 5.9 %fusion.136 = f32[1024,2048]{1,0:T(8,128)} fusion(bf16[1024,256]{1,0:T(8,128)(2,1)S(1)} %bitcast.94, bf16[128,2048]{1,0:T(8,128)(2,1)} %copy-done.29, bf16[128,2048]{1,0:T(8,128)(2,1)} %broadcast_select_fusion.3), kind=kOutput, calls=%fused_computation.176 | convolution fusion | flops 1075838976 | bytes 9961472 | tf_op jit(solution)/shard_map/dot_general | solution.py:14
  317.1 2.2 convolution_convert_fusion
  319.4 2.2 convolution_convert_fusion.1
  321.9 2.5 collective-permute-start.40
  326.2 3.4 fusion.200
  329.6 11.6 %fusion.182 = (f32[2048]{0:T(1024)S(1)}, f32[2048]{0:T(1024)S(1)}, f32[1024,2048]{1,0:T(8,128)}, f32[2048]{0:T(1024)}, f32[2048]{0:T(1024)S(1)}) fusion(f32[1024]{0:T(1024)S(1)} %add_rsqrt_fusion, f32[1024]{0:T(1024)S(1)} %broadcast_multiply_fusion, bf16[512,2048]{1,0:T(8,128)(2,1)} %collective-permute-done, bf16[512,2048]{1,0:T(8,128)(2,1)S(1)} %copy-done, ...), kind=kOutput, calls=%fused_computation.332 | convolution fusion | flops 4326416384 | bytes 27320320 | tf_op jit(solution)/shard_map/dot_general | solution.py:18
  342.0 3.8 slice.648
  347.7 10.1 %convolution_add_fusion = f32[1024,2048]{1,0:T(8,128)S(1)} fusion(f32[1024,2048]{1,0:T(8,128)} %fusion.136, bf16[1024,1024]{1,0:T(8,128)(2,1)} %get-tuple-element.199, bf16[1024,2048]{1,0:T(8,128)(2,1)} %slice_dynamic-update-slice_fusion), kind=kOutput, calls=%fused_computation.34 | convolution fusion | flops 4297064448 | bytes 23068672 | tf_op jit(solution)/shard_map/dot_general | solution.py:14
  358.4 2.9 copy-done.12
  368.3 3.7 fusion.20
  375.9 3.3 collective-permute-done.31
  379.3 2.5 collective-permute-start.35
  381.8 2.3 fusion.59
  384.0 2.9 collective-permute-done.25
  388.7 3.0 fusion.89
  393.8 2.1 collective-permute-start.29
  398.0 2.6 fusion.81
  400.6 8.8 %collective-permute-done.35 = bf16[1024,512]{0,1:T(8,128)(2,1)S(1)} collective-permute-done((bf16[1024,512]{0,1:T(8,128)(2,1)}, bf16[1024,512]{0,1:T(8,128)(2,1)S(1)}, u32[]{:S(2)}, u32[]{:S(2)}) %collective-permute-start.35) | collective-permute-done | bytes 1048608 | tf_op jit(solution)/shard_map/ppermute | solution.py:74
  412.6 10.4 %collective-permute-done.39 = bf16[512,512]{1,0:T(8,128)(2,1)S(1)} collective-permute-done((bf16[512,512]{1,0:T(8,128)(2,1)S(1)}, bf16[512,512]{1,0:T(8,128)(2,1)S(1)}, u32[]{:S(2)}, u32[]{:S(2)}) %collective-permute-start.39) | collective-permute-done | bytes 524320 | tf_op jit(solution)/shard_map/ppermute | solution.py:74
  431.3 3.6 all-to-all-start.2
  436.8 3.2 fusion.97
  443.2 4.9 collective-permute-done.36
  448.4 4.9 fusion.21
  454.4 5.5 all-to-all-done.2
  459.9 3.5 all-to-all-start.1
  463.5 2.8 fusion.116
  466.3 2.6 fusion.119
  477.3 38.8 %all-to-all-done.1 = bf16[512,4,256]{0,2,1:T(8,128)(2,1)S(1)} async-done(((bf16[512,4,256]{0,2,1:T(8,128)(2,1)}), bf16[512,4,256]{0,2,1:T(8,128)(2,1)S(1)}, u32[]{:S(2)}, u32[]{:S(2)}) %all-to-all-start.1) | async-done | bytes 1048608 | tf_op jit(solution)/shard_map/all_to_all | solution.py:415
  521.5 2.8 fusion.101
  524.3 2.9 fusion.100
  532.2 4.3 all-to-all-start
  538.6 5.9 %all-to-all-done = f32[32,1,768]{2,1,0:T(1,128)S(1)} async-done(((f32[32,1,768]{2,1,0:T(1,128)}), f32[32,1,768]{2,1,0:T(1,128)S(1)}, u32[]{:S(2)}, u32[]{:S(2)}) %all-to-all-start) | async-done | bytes 98336 | tf_op jit(solution)/shard_map/all_to_all | solution.py:403
  (410 shorter events, 159.8 us)
Async XLA Ops:
  7.2 184.7 %all-gather.5.cloned.1.call-start = ((), (), s32[]{:S(2)}) async-start(), calls=%async_computation.5 | async-start | bytes 2621440 | tf_op jit(solution)/shard_map/all_gather | solution.py:229
  9.8 188.6 %all-gather.7.cloned.1.call-start = ((), (), s32[]{:S(2)}) async-start(), calls=%async_computation.7 | async-start | bytes 2621440 | tf_op jit(solution)/shard_map/all_gather | solution.py:230
  12.1 66.0 %collective-permute-start.1 = (bf16[256,1024]{1,0:T(8,128)(2,1)}, bf16[256,1024]{1,0:T(8,128)(2,1)}, u32[]{:S(2)}, u32[]{:S(2)}) collective-permute-start(bf16[256,1024]{1,0:T(8,128)(2,1)} %pad_maximum_fusion.27), channel_id=1, source_target_pairs={{0,4},{4,0},{8,12},{12,8},{16,20},{20,16},{24,28},{28,24},{1,5},{5... | collective-permute-start | bytes 1572872 | tf_op jit(solution)/shard_map/ppermute | solution.py:74
  15.1 50.9 %copy-start.1 = (bf16[128,2048]{1,0:T(8,128)(2,1)S(1)}, bf16[128,2048]{1,0:T(8,128)(2,1)}, u32[]{:S(2)}) copy-start(bf16[128,2048]{1,0:T(8,128)(2,1)} %get-tuple-element.79) | copy-start | bytes 1572868
  17.1 70.2 %collective-permute-start.6 = (bf16[128,2048]{1,0:T(8,128)(2,1)S(1)}, bf16[128,2048]{1,0:T(8,128)(2,1)S(1)}, u32[]{:S(2)}, u32[]{:S(2)}) collective-permute-start(bf16[128,2048]{1,0:T(8,128)(2,1)S(1)} %get-tuple-element.83), channel_id=1, source_target_pairs={{0,8},{4,12},{8,0},{12,4},{16,24},{20,28},{24,16},{28,20},{1,9},{5... | collective-permute-start | bytes 1572872 | tf_op jit(solution)/shard_map/ppermute | solution.py:74
  21.6 55.2 %collective-permute-start.10 = (bf16[256,768]{1,0:T(8,128)(2,1)}, bf16[256,768]{1,0:T(8,128)(2,1)}, u32[]{:S(2)}, u32[]{:S(2)}) collective-permute-start(bf16[256,768]{1,0:T(8,128)(2,1)} %get-tuple-element.110), channel_id=1, source_target_pairs={{0,4},{4,0},{8,12},{12,8},{16,20},{20,16},{24,28},{28,24},{1,5},{5... | collective-permute-start | bytes 1179656 | tf_op jit(solution)/shard_map/ppermute | solution.py:74
  21.8 49.8 %collective-permute-start.15 = (s32[1,4]{1,0:T(1,128)}, s32[1,4]{1,0:T(1,128)}, u32[]{:S(2)}, u32[]{:S(2)}) collective-permute-start(s32[1,4]{1,0:T(1,128)} %param.21), channel_id=1, source_target_pairs={{0,4},{4,0},{8,12},{12,8},{16,20},{20,16},{24,28},{28,24},{1,5},{5... | collective-permute-start | bytes 56 | tf_op jit(solution)/shard_map/ppermute | solution.py:74
  23.1 65.0 %collective-permute-start.16 = (bf16[128,2048]{1,0:T(8,128)(2,1)}, bf16[128,2048]{1,0:T(8,128)(2,1)}, u32[]{:S(2)}, u32[]{:S(2)}) collective-permute-start(bf16[128,2048]{1,0:T(8,128)(2,1)} %get-tuple-element.128), channel_id=1, source_target_pairs={{0,8},{4,12},{9,1},{13,5},{18,26},{22,30},{27,19},{31,23}} | collective-permute-start | bytes 1572872 | tf_op jit(solution)/shard_map/ppermute | solution.py:139
  25.8 501.4 %reduce-scatter.5.cloned.1.call-start = ((), (), s32[]{:S(2)}) async-start(), calls=%async_computation.8 | async-start | bytes 2621440 | tf_op jit(solution)/shard_map/reduce_scatter | solution.py:369
  71.6 18.6 %collective-permute-start.18 = (bf16[128,2048]{1,0:T(8,128)(2,1)}, bf16[128,2048]{1,0:T(8,128)(2,1)}, u32[]{:S(2)}, u32[]{:S(2)}) collective-permute-start(bf16[128,2048]{1,0:T(8,128)(2,1)} %get-tuple-element.129), channel_id=1, source_target_pairs={{0,16},{4,20},{9,25},{13,29},{18,2},{22,6},{27,11},{31,15}} | collective-permute-start | bytes 1572872 | tf_op jit(solution)/shard_map/ppermute | solution.py:139
  78.1 17.5 %collective-permute-start.11 = (bf16[256,768]{1,0:T(8,128)(2,1)S(1)}, bf16[256,768]{1,0:T(8,128)(2,1)S(1)}, u32[]{:S(2)}, u32[]{:S(2)}) collective-permute-start(bf16[256,768]{1,0:T(8,128)(2,1)S(1)} %get-tuple-element.131), channel_id=1, source_target_pairs={{0,8},{4,12},{8,0},{12,4},{16,24},{20,28},{24,16},{28,20},{1,9},{5... | collective-permute-start | bytes 1179656 | tf_op jit(solution)/shard_map/ppermute | solution.py:74
  78.2 15.5 %collective-permute-start.12 = (bf16[256,768]{1,0:T(8,128)(2,1)S(1)}, bf16[256,768]{1,0:T(8,128)(2,1)S(1)}, u32[]{:S(2)}, u32[]{:S(2)}) collective-permute-start(bf16[256,768]{1,0:T(8,128)(2,1)S(1)} %get-tuple-element.130), channel_id=1, source_target_pairs={{0,16},{4,20},{8,24},{12,28},{16,0},{20,4},{24,8},{28,12},{1,17},{... | collective-permute-start | bytes 1179656 | tf_op jit(solution)/shard_map/ppermute | solution.py:74
  87.4 17.7 %collective-permute-start.2 = (bf16[256,1024]{1,0:T(8,128)(2,1)S(1)}, bf16[256,1024]{1,0:T(8,128)(2,1)S(1)}, u32[]{:S(2)}, u32[]{:S(2)}) collective-permute-start(bf16[256,1024]{1,0:T(8,128)(2,1)S(1)} %get-tuple-element.125), channel_id=1, source_target_pairs={{0,8},{4,12},{8,0},{12,4},{16,24},{20,28},{24,16},{28,20},{1,9},{5... | collective-permute-start | bytes 1572872 | tf_op jit(solution)/shard_map/ppermute | solution.py:74
  88.1 16.8 %collective-permute-start.3 = (bf16[256,1024]{1,0:T(8,128)(2,1)S(1)}, bf16[256,1024]{1,0:T(8,128)(2,1)S(1)}, u32[]{:S(2)}, u32[]{:S(2)}) collective-permute-start(bf16[256,1024]{1,0:T(8,128)(2,1)S(1)} %get-tuple-element.124), channel_id=1, source_target_pairs={{0,16},{4,20},{8,24},{12,28},{16,0},{20,4},{24,8},{28,12},{1,17},{... | collective-permute-start | bytes 1572872 | tf_op jit(solution)/shard_map/ppermute | solution.py:74
  90.2 51.8 %collective-permute-start.7 = (bf16[256,2048]{1,0:T(8,128)(2,1)S(1)}, bf16[256,2048]{1,0:T(8,128)(2,1)S(1)}, u32[]{:S(2)}, u32[]{:S(2)}) collective-permute-start(bf16[256,2048]{1,0:T(8,128)(2,1)S(1)} %pad_maximum_fusion.13), channel_id=1, source_target_pairs={{0,16},{4,20},{8,24},{12,28},{16,0},{20,4},{24,8},{28,12},{1,17},{... | collective-permute-start | bytes 3145736 | tf_op jit(solution)/shard_map/ppermute | solution.py:74
  93.7 17.9 %collective-permute-start.19 = (bf16[128,2048]{1,0:T(8,128)(2,1)S(1)}, bf16[128,2048]{1,0:T(8,128)(2,1)S(1)}, u32[]{:S(2)}, u32[]{:S(2)}) collective-permute-start(bf16[128,2048]{1,0:T(8,128)(2,1)S(1)} %get-tuple-element.127), channel_id=1, source_target_pairs={{0,8},{4,12},{16,24},{20,28},{9,1},{13,5},{25,17},{29,21},{18,26},... | collective-permute-start | bytes 1572872 | tf_op jit(solution)/shard_map/ppermute | solution.py:139
  95.6 43.0 %collective-permute-start.17 = (bf16[128,2048]{1,0:T(8,128)(2,1)S(1)}, bf16[128,2048]{1,0:T(8,128)(2,1)S(1)}, u32[]{:S(2)}, u32[]{:S(2)}) collective-permute-start(bf16[128,2048]{1,0:T(8,128)(2,1)S(1)} %get-tuple-element.126), channel_id=1, source_target_pairs={{0,16},{4,20},{8,24},{12,28},{9,25},{13,29},{1,17},{5,21},{18,2},{... | collective-permute-start | bytes 1572872 | tf_op jit(solution)/shard_map/ppermute | solution.py:139
  105.0 40.8 %collective-permute-start.13 = (bf16[512,768]{1,0:T(8,128)(2,1)S(1)}, bf16[512,768]{1,0:T(8,128)(2,1)S(1)}, u32[]{:S(2)}, u32[]{:S(2)}) collective-permute-start(bf16[512,768]{1,0:T(8,128)(2,1)S(1)} %pad_maximum_fusion.22), channel_id=1, source_target_pairs={{0,8},{4,12},{8,0},{12,4},{16,24},{20,28},{24,16},{28,20},{1,9},{5... | collective-permute-start | bytes 2359304 | tf_op jit(solution)/shard_map/ppermute | solution.py:74
  105.0 50.5 %collective-permute-start.14 = (bf16[512,768]{1,0:T(8,128)(2,1)S(1)}, bf16[512,768]{1,0:T(8,128)(2,1)S(1)}, u32[]{:S(2)}, u32[]{:S(2)}) collective-permute-start(bf16[512,768]{1,0:T(8,128)(2,1)S(1)} %pad_maximum_fusion.23), channel_id=1, source_target_pairs={{0,16},{4,20},{8,24},{12,28},{16,0},{20,4},{24,8},{28,12},{1,17},{... | collective-permute-start | bytes 2359304 | tf_op jit(solution)/shard_map/ppermute | solution.py:74
  111.6 78.5 %collective-permute-start.4 = (bf16[512,1024]{1,0:T(8,128)(2,1)S(1)}, bf16[512,1024]{1,0:T(8,128)(2,1)S(1)}, u32[]{:S(2)}, u32[]{:S(2)}) collective-permute-start(bf16[512,1024]{1,0:T(8,128)(2,1)S(1)} %pad_maximum_fusion.11), channel_id=1, source_target_pairs={{0,8},{4,12},{8,0},{12,4},{16,24},{20,28},{24,16},{28,20},{1,9},{5... | collective-permute-start | bytes 3145736 | tf_op jit(solution)/shard_map/ppermute | solution.py:74
  114.1 164.7 %copy-start.29 = (bf16[128,2048]{1,0:T(8,128)(2,1)}, bf16[128,2048]{1,0:T(8,128)(2,1)S(1)}, u32[]{:S(2)}) copy-start(bf16[128,2048]{1,0:T(8,128)(2,1)S(1)} %broadcast_select_fusion.1) | copy-start | bytes 1572868
  138.7 53.2 %collective-permute-start.5 = (bf16[512,1024]{1,0:T(8,128)(2,1)}, bf16[512,1024]{1,0:T(8,128)(2,1)}, u32[]{:S(2)}, u32[]{:S(2)}) collective-permute-start(bf16[512,1024]{1,0:T(8,128)(2,1)} %pad_maximum_fusion.12), channel_id=1, source_target_pairs={{0,16},{4,20},{8,24},{12,28},{16,0},{20,4},{24,8},{28,12},{1,17},{... | collective-permute-start | bytes 3145736 | tf_op jit(solution)/shard_map/ppermute | solution.py:74
  145.7 43.3 %collective-permute-start.8 = (bf16[128,2048]{1,0:T(8,128)(2,1)S(1)}, bf16[128,2048]{1,0:T(8,128)(2,1)S(1)}, u32[]{:S(2)}, u32[]{:S(2)}) collective-permute-start(bf16[128,2048]{1,0:T(8,128)(2,1)S(1)} %get-tuple-element.81), channel_id=1, source_target_pairs={{0,16},{4,20},{8,24},{12,28},{16,0},{20,4},{24,8},{28,12},{1,17},{... | collective-permute-start | bytes 1572872 | tf_op jit(solution)/shard_map/ppermute | solution.py:74
  155.7 34.4 %copy-start.55 = (bf16[2048,768]{1,0:T(8,128)(2,1)}, bf16[2048,768]{1,0:T(8,128)(2,1)S(1)}, u32[]{:S(2)}) copy-start(bf16[2048,768]{1,0:T(8,128)(2,1)S(1)} %constant_dynamic-update-slice_fusion.3) | copy-start | bytes 9437188
  190.1 25.1 %collective-permute-start.9 = (bf16[256,2048]{1,0:T(8,128)(2,1)}, bf16[256,2048]{1,0:T(8,128)(2,1)S(1)}, u32[]{:S(2)}, u32[]{:S(2)}) collective-permute-start(bf16[256,2048]{1,0:T(8,128)(2,1)} %pad_maximum_fusion.14), channel_id=1, source_target_pairs={{0,8},{4,12},{8,0},{12,4},{16,24},{20,28},{24,16},{28,20},{1,9},{5... | collective-permute-start | bytes 3145736 | tf_op jit(solution)/shard_map/ppermute | solution.py:74
  191.9 29.3 %collective-permute-start = (bf16[512,2048]{1,0:T(8,128)(2,1)}, bf16[512,2048]{1,0:T(8,128)(2,1)}, u32[]{:S(2)}, u32[]{:S(2)}) collective-permute-start(bf16[512,2048]{1,0:T(8,128)(2,1)} %all-gather.5.cloned.1.call-done), channel_id=1, source_target_pairs={{0,4},{4,0},{8,12},{12,8},{16,20},{20,16},{24,28},{28,24},{1,5},{5... | collective-permute-start | bytes 6291464 | tf_op jit(solution)/shard_map/ppermute | solution.py:74
  198.4 22.6 %copy-start.31 = (bf16[512,2048]{1,0:T(8,128)(2,1)S(1)}, bf16[512,2048]{1,0:T(8,128)(2,1)}, u32[]{:S(2)}) copy-start(bf16[512,2048]{1,0:T(8,128)(2,1)} %all-gather.7.cloned.1.call-done) | copy-start | bytes 6291460
  198.4 28.0 %collective-permute-start.21 = (bf16[512,2048]{1,0:T(8,128)(2,1)}, bf16[512,2048]{1,0:T(8,128)(2,1)S(1)}, u32[]{:S(2)}, u32[]{:S(2)}) collective-permute-start(bf16[512,2048]{1,0:T(8,128)(2,1)} %all-gather.7.cloned.1.call-done), channel_id=1, source_target_pairs={{0,4},{4,0},{8,12},{12,8},{16,20},{20,16},{24,28},{28,24},{1,5},{5... | collective-permute-start | bytes 6291464 | tf_op jit(solution)/shard_map/ppermute | solution.py:74
  226.7 18.9 %copy-start.3 = (bf16[1024,2048]{1,0:T(8,128)(2,1)}, bf16[1024,2048]{1,0:T(8,128)(2,1)S(1)}, u32[]{:S(2)}) copy-start(bf16[1024,2048]{1,0:T(8,128)(2,1)S(1)} %constant_dynamic-update-slice_fusion.6) | copy-start | bytes 12582916
  234.2 26.2 %copy-start.20 = (bf16[1024,2048]{1,0:T(8,128)(2,1)}, bf16[1024,2048]{1,0:T(8,128)(2,1)S(1)}, u32[]{:S(2)}) copy-start(bf16[1024,2048]{1,0:T(8,128)(2,1)S(1)} %get-tuple-element.91) | copy-start | bytes 12582916
  234.3 27.9 %copy-start.19 = (bf16[1024,2048]{1,0:T(8,128)(2,1)}, bf16[1024,2048]{1,0:T(8,128)(2,1)S(1)}, u32[]{:S(2)}) copy-start(bf16[1024,2048]{1,0:T(8,128)(2,1)S(1)} %get-tuple-element.92) | copy-start | bytes 12582916
  321.6 70.1 %collective-permute-start.38 = (bf16[512,1024]{1,0:T(8,128)(2,1)}, bf16[512,1024]{1,0:T(8,128)(2,1)}, u32[]{:S(2)}, u32[]{:S(2)}) collective-permute-start(bf16[512,1024]{1,0:T(8,128)(2,1)} %convolution_convert_fusion.1), channel_id=1, source_target_pairs={{0,8},{4,12},{8,0},{12,4},{16,24},{20,28},{24,16},{28,20},{1,9},{5... | collective-permute-start | bytes 3145736 | tf_op jit(solution)/shard_map/ppermute | solution.py:74
  321.9 71.9 %collective-permute-start.40 = (bf16[512,1024]{1,0:T(8,128)(2,1)}, bf16[512,1024]{1,0:T(8,128)(2,1)}, u32[]{:S(2)}, u32[]{:S(2)}) collective-permute-start(bf16[512,1024]{1,0:T(8,128)(2,1)} %convolution_convert_fusion), channel_id=1, source_target_pairs={{0,16},{4,20},{8,24},{12,28},{16,0},{20,4},{24,8},{28,12},{1,17},{... | collective-permute-start | bytes 3145736 | tf_op jit(solution)/shard_map/ppermute | solution.py:74
  324.4 73.3 %collective-permute-start.33 = (bf16[1024,512]{0,1:T(8,128)(2,1)}, bf16[1024,512]{0,1:T(8,128)(2,1)}, u32[]{:S(2)}, u32[]{:S(2)}) collective-permute-start(bf16[1024,512]{0,1:T(8,128)(2,1)} %fusion.30), channel_id=1, source_target_pairs={{0,8},{4,12},{8,0},{12,4},{16,24},{20,28},{24,16},{28,20},{1,9},{5... | collective-permute-start | bytes 3145736 | tf_op jit(solution)/shard_map/ppermute | solution.py:74
  326.2 38.0 %collective-permute-start.30 = (bf16[128,1024]{1,0:T(8,128)(2,1)}, bf16[128,1024]{1,0:T(8,128)(2,1)}, u32[]{:S(2)}, u32[]{:S(2)}) collective-permute-start(bf16[128,1024]{1,0:T(8,128)(2,1)} %fusion.57), channel_id=1, source_target_pairs={{0,16},{4,20},{8,24},{12,28},{16,0},{20,4},{24,8},{28,12},{1,17},{... | collective-permute-start | bytes 786440 | tf_op jit(solution)/shard_map/ppermute | solution.py:74
  345.8 20.6 %collective-permute-start.22 = (bf16[512,2048]{1,0:T(8,128)(2,1)}, bf16[512,2048]{1,0:T(8,128)(2,1)}, u32[]{:S(2)}, u32[]{:S(2)}) collective-permute-start(bf16[512,2048]{1,0:T(8,128)(2,1)} %slice.648), channel_id=1, source_target_pairs={{0,4},{4,0},{8,12},{12,8},{16,20},{20,16},{24,28},{28,24},{1,5},{5... | collective-permute-start | bytes 6291464 | tf_op jit(solution)/shard_map/ppermute | solution.py:74
  346.8 21.6 %slice-start = ((s8[8388608]{0:T(1024)(128)(4,1)}), s8[4194304]{0:T(1024)(128)(4,1)S(1)}, s32[]{:S(2)}) async-start(s8[8388608]{0:T(1024)(128)(4,1)} %bitcast.101), calls=%async_computation.9 | async-start | bytes 8388608
  347.6 20.7 %slice-start.1 = ((s8[8388608]{0:T(1024)(128)(4,1)}), s8[4194304]{0:T(1024)(128)(4,1)S(1)}, s32[]{:S(2)}) async-start(s8[8388608]{0:T(1024)(128)(4,1)} %bitcast.101), calls=%async_computation.10 | async-start | bytes 8388608
  364.1 9.9 %collective-permute-start.28 = (bf16[128,1024]{1,0:T(8,128)(2,1)}, bf16[128,1024]{1,0:T(8,128)(2,1)}, u32[]{:S(2)}, u32[]{:S(2)}) collective-permute-start(bf16[128,1024]{1,0:T(8,128)(2,1)} %fusion.56), channel_id=1, source_target_pairs={{0,8},{4,12},{8,0},{12,4},{16,24},{20,28},{24,16},{28,20},{1,9},{5... | collective-permute-start | bytes 786440 | tf_op jit(solution)/shard_map/ppermute | solution.py:74
  366.3 20.7 %collective-permute-start.25 = (bf16[1024,384]{0,1:T(8,128)(2,1)}, bf16[1024,384]{0,1:T(8,128)(2,1)}, u32[]{:S(2)}, u32[]{:S(2)}) collective-permute-start(bf16[1024,384]{0,1:T(8,128)(2,1)} %fusion.39), channel_id=1, source_target_pairs={{0,16},{4,20},{8,24},{12,28},{16,0},{20,4},{24,8},{28,12},{1,17},{... | collective-permute-start | bytes 2359304 | tf_op jit(solution)/shard_map/ppermute | solution.py:74
  372.1 16.7 %copy-start.25 = (bf16[2,512,1,192]{3,1,0,2:T(8,128)(2,1)S(1)}, bf16[2,512,1,192]{3,1,0,2:T(8,128)(2,1)}, u32[]{:S(2)}) copy-start(bf16[2,512,1,192]{3,1,0,2:T(8,128)(2,1)} %slice.650) | copy-start | bytes 1179652
  372.1 16.7 %copy-start.28 = (bf16[2,512,1,256]{3,1,0,2:T(8,128)(2,1)S(1)}, bf16[2,512,1,256]{3,1,0,2:T(8,128)(2,1)}, u32[]{:S(2)}) copy-start(bf16[2,512,1,256]{3,1,0,2:T(8,128)(2,1)} %copy.109) | copy-start | bytes 1572868
  374.1 5.2 collective-permute-start.31
  375.9 15.9 %copy-start.77 = (bf16[1024,1024]{1,0:T(8,128)(2,1)S(1)}, bf16[1024,1024]{1,0:T(8,128)(2,1)}, u32[]{:S(2)}) copy-start(bf16[1024,1024]{1,0:T(8,128)(2,1)} %get-tuple-element.199) | copy-start | bytes 6291460
  379.3 30.1 %collective-permute-start.35 = (bf16[1024,512]{0,1:T(8,128)(2,1)}, bf16[1024,512]{0,1:T(8,128)(2,1)S(1)}, u32[]{:S(2)}, u32[]{:S(2)}) collective-permute-start(bf16[1024,512]{0,1:T(8,128)(2,1)} %fusion.33), channel_id=1, source_target_pairs={{0,16},{4,20},{8,24},{12,28},{16,0},{20,4},{24,8},{28,12},{1,17},{... | collective-permute-start | bytes 3145736 | tf_op jit(solution)/shard_map/ppermute | solution.py:74
  387.0 48.2 %collective-permute-start.23 = (bf16[1024,384]{0,1:T(8,128)(2,1)}, bf16[1024,384]{0,1:T(8,128)(2,1)}, u32[]{:S(2)}, u32[]{:S(2)}) collective-permute-start(bf16[1024,384]{0,1:T(8,128)(2,1)} %fusion.36), channel_id=1, source_target_pairs={{0,8},{4,12},{8,0},{12,4},{16,24},{20,28},{24,16},{28,20},{1,9},{5... | collective-permute-start | bytes 2359304 | tf_op jit(solution)/shard_map/ppermute | solution.py:74
  391.8 56.6 %collective-permute-start.20 = (bf16[512,2048]{1,0:T(8,128)(2,1)}, bf16[512,2048]{1,0:T(8,128)(2,1)}, u32[]{:S(2)}, u32[]{:S(2)}) collective-permute-start(bf16[512,2048]{1,0:T(8,128)(2,1)} %slice.649), channel_id=1, source_target_pairs={{0,4},{4,0},{8,12},{12,8},{16,20},{20,16},{24,28},{28,24},{1,5},{5... | collective-permute-start | bytes 6291464 | tf_op jit(solution)/shard_map/ppermute | solution.py:74
  393.8 76.2 %collective-permute-start.29 = (bf16[128,512]{1,0:T(8,128)(2,1)S(1)}, bf16[128,512]{1,0:T(8,128)(2,1)}, u32[]{:S(2)}, u32[]{:S(2)}) collective-permute-start(bf16[128,512]{1,0:T(8,128)(2,1)S(1)} %fusion.61), channel_id=1, source_target_pairs={{0,16},{4,20},{8,24},{12,28},{16,0},{20,4},{24,8},{28,12},{1,17},{... | collective-permute-start | bytes 393224 | tf_op jit(solution)/shard_map/ppermute | solution.py:74
  397.7 25.3 %collective-permute-start.39 = (bf16[512,512]{1,0:T(8,128)(2,1)S(1)}, bf16[512,512]{1,0:T(8,128)(2,1)S(1)}, u32[]{:S(2)}, u32[]{:S(2)}) collective-permute-start(bf16[512,512]{1,0:T(8,128)(2,1)S(1)} %fusion.48), channel_id=1, source_target_pairs={{0,16},{4,20},{8,24},{12,28},{16,0},{20,4},{24,8},{28,12},{1,17},{... | collective-permute-start | bytes 1572872 | tf_op jit(solution)/shard_map/ppermute | solution.py:74
  400.6 24.2 %copy-start.5 = (bf16[1024,2048]{1,0:T(8,128)(2,1)S(1)}, bf16[1024,2048]{1,0:T(8,128)(2,1)}, u32[]{:S(2)}) copy-start(bf16[1024,2048]{1,0:T(8,128)(2,1)} %copy-done.3) | copy-start | bytes 12582916
  409.3 17.2 %copy-start.52 = (bf16[1024,512]{0,1:T(8,128)(2,1)}, bf16[1024,512]{0,1:T(8,128)(2,1)S(1)}, u32[]{:S(2)}) copy-start(bf16[1024,512]{0,1:T(8,128)(2,1)S(1)} %collective-permute-done.35) | copy-start | bytes 3145732
  409.3 17.2 %collective-permute-start.41 = (bf16[512,512]{1,0:T(8,128)(2,1)S(1)}, bf16[512,512]{1,0:T(8,128)(2,1)S(1)}, u32[]{:S(2)}, u32[]{:S(2)}) collective-permute-start(bf16[512,512]{1,0:T(8,128)(2,1)S(1)} %fusion.49), channel_id=1, source_target_pairs={{0,8},{4,12},{8,0},{12,4},{16,24},{20,28},{24,16},{28,20},{1,9},{5... | collective-permute-start | bytes 1572872 | tf_op jit(solution)/shard_map/ppermute | solution.py:74
  423.0 40.5 %collective-permute-start.26 = (bf16[512,384]{0,1:T(8,128)(2,1)}, bf16[512,384]{0,1:T(8,128)(2,1)}, u32[]{:S(2)}, u32[]{:S(2)}) collective-permute-start(bf16[512,384]{0,1:T(8,128)(2,1)} %fusion.89), channel_id=1, source_target_pairs={{0,8},{4,12},{8,0},{12,4},{16,24},{20,28},{24,16},{28,20},{1,9},{5... | collective-permute-start | bytes 1179656 | tf_op jit(solution)/shard_map/ppermute | solution.py:74
  426.6 13.6 %collective-permute-start.34 = (bf16[512,512]{0,1:T(8,128)(2,1)}, bf16[512,512]{0,1:T(8,128)(2,1)}, u32[]{:S(2)}, u32[]{:S(2)}) collective-permute-start(bf16[512,512]{0,1:T(8,128)(2,1)} %fusion.81), channel_id=1, source_target_pairs={{0,16},{4,20},{8,24},{12,28},{16,0},{20,4},{24,8},{28,12},{1,17},{... | collective-permute-start | bytes 1572872 | tf_op jit(solution)/shard_map/ppermute | solution.py:74
  431.3 28.7 %all-to-all-start.2 = ((bf16[4,256,512]{2,1,0:T(8,128)(2,1)}), bf16[4,256,512]{2,1,0:T(8,128)(2,1)S(1)}, u32[]{:S(2)}, u32[]{:S(2)}) async-start(bf16[4,256,512]{2,1,0:T(8,128)(2,1)} %bitcast.33), calls=%async_computation.4 | async-start | bytes 2097152 | tf_op jit(solution)/shard_map/all_to_all | solution.py:415
  434.9 101.7 %reduce-scatter.3.cloned.1.call-start = ((), (), s32[]{:S(2)}) async-start(), calls=%async_computation.6 | async-start | bytes 2621440 | tf_op jit(solution)/shard_map/reduce_scatter | solution.py:369
  435.2 13.0 %collective-permute-start.36 = (bf16[512,512]{0,1:T(8,128)(2,1)}, bf16[512,512]{0,1:T(8,128)(2,1)S(1)}, u32[]{:S(2)}, u32[]{:S(2)}) collective-permute-start(bf16[512,512]{0,1:T(8,128)(2,1)} %fusion.73), channel_id=1, source_target_pairs={{0,8},{4,12},{8,0},{12,4},{16,24},{20,28},{24,16},{28,20},{1,9},{5... | collective-permute-start | bytes 1572872 | tf_op jit(solution)/shard_map/ppermute | solution.py:74
  440.2 26.0 %collective-permute-start.24 = (bf16[512,384]{0,1:T(8,128)(2,1)}, bf16[512,384]{0,1:T(8,128)(2,1)}, u32[]{:S(2)}, u32[]{:S(2)}) collective-permute-start(bf16[512,384]{0,1:T(8,128)(2,1)} %fusion.97), channel_id=1, source_target_pairs={{0,16},{4,20},{8,24},{12,28},{16,0},{20,4},{24,8},{28,12},{1,17},{... | collective-permute-start | bytes 1179656 | tf_op jit(solution)/shard_map/ppermute | solution.py:74
  459.9 56.2 %all-to-all-start.1 = ((bf16[512,4,256]{0,2,1:T(8,128)(2,1)}), bf16[512,4,256]{0,2,1:T(8,128)(2,1)S(1)}, u32[]{:S(2)}, u32[]{:S(2)}) async-start(bf16[512,4,256]{0,2,1:T(8,128)(2,1)} %pad_maximum_fusion.16), calls=%async_computation.3 | async-start | bytes 2097152 | tf_op jit(solution)/shard_map/all_to_all | solution.py:415
  469.9 48.0 %collective-permute-start.27 = (f32[256,768]{0,1:T(8,128)}, f32[256,768]{0,1:T(8,128)}, u32[]{:S(2)}, u32[]{:S(2)}) collective-permute-start(f32[256,768]{0,1:T(8,128)} %get-tuple-element.113), channel_id=1, source_target_pairs={{0,4},{4,0},{8,12},{12,8},{16,20},{20,16},{24,28},{28,24},{1,5},{5... | collective-permute-start | bytes 2359304 | tf_op jit(solution)/shard_map/ppermute | solution.py:74
  471.7 3.8 collective-permute-start.32
  475.4 46.0 %collective-permute-start.42 = (bf16[1024,256]{1,0:T(8,128)(2,1)}, bf16[1024,256]{1,0:T(8,128)(2,1)}, u32[]{:S(2)}, u32[]{:S(2)}) collective-permute-start(bf16[1024,256]{1,0:T(8,128)(2,1)} %get-tuple-element.117), channel_id=1, source_target_pairs={{0,4},{4,0},{8,12},{12,8},{16,20},{20,16},{24,28},{28,24},{1,5},{5... | collective-permute-start | bytes 1572872 | tf_op jit(solution)/shard_map/ppermute | solution.py:74
  518.0 6.3 %collective-permute-start.37 = (bf16[256,1024]{1,0:T(8,128)(2,1)}, bf16[256,1024]{1,0:T(8,128)(2,1)}, u32[]{:S(2)}, u32[]{:S(2)}) collective-permute-start(bf16[256,1024]{1,0:T(8,128)(2,1)} %copy.141), channel_id=1, source_target_pairs={{0,4},{4,0},{8,12},{12,8},{16,20},{20,16},{24,28},{28,24},{1,5},{5... | collective-permute-start | bytes 1572872 | tf_op jit(solution)/shard_map/ppermute | solution.py:74
  532.2 12.3 %all-to-all-start = ((f32[32,1,768]{2,1,0:T(1,128)}), f32[32,1,768]{2,1,0:T(1,128)S(1)}, u32[]{:S(2)}, u32[]{:S(2)}) async-start(f32[32,1,768]{2,1,0:T(1,128)} %all_to_all.18), calls=%async_computation.2 | async-start | bytes 196608 | tf_op jit(solution)/shard_map/all_to_all | solution.py:403
  (66 other events, 305.4 us)
Sparse Core Ops, SparseCore 0:
  10.2 48.6 all-gather.4
  60.4 44.6 all-gather.6
  372.2 44.3 reduce-scatter.4
  453.5 62.8 reduce-scatter.2

commit v2 on v1

v2 whole, which is shorter than its diff:
```python
import jax
import jax.numpy as jnp
from jax import lax
from jax.experimental import pallas as pl
from jax.experimental.pallas import tpu as pltpu
from jax.sharding import PartitionSpec as P

H = 8
HS = 256
ROT = 64
HINT = 0.05
F32 = jnp.float32
BF16 = jnp.bfloat16


def matmul(left, right):
    return jnp.dot(left, right, preferred_element_type=F32)


def times_transposed(left, right):
    return lax.dot_general(left, right, (((1,), (1,)), ((), ())), preferred_element_type=F32)


def left_transposed(left, right):
    return lax.dot_general(left, right, (((0,), (0,)), ((), ())), preferred_element_type=F32)


def doc_layout(lengths_row, places):
    starts = jnp.cumsum(lengths_row) - lengths_row
    after = places[:, None] >= starts[None, :]
    doc_ids = jnp.sum(after.astype(jnp.int32), axis=1)
    begins = jnp.max(jnp.where(after, starts[None, :], 0), axis=1)
    return (doc_ids, places - begins)


def turn_tables(positions, rot_dims):
    half_rot = rot_dims // 2
    inverse = 10000.0 ** (-(jnp.arange(half_rot, dtype=F32) * 2.0 / rot_dims))
    angles = positions.astype(F32)[:, None] * inverse[None, :]
    angles = jnp.concatenate([angles, angles], axis=1)
    return (jnp.cos(angles), jnp.sin(angles))


def cost(flops, reads, writes, transcendentals=0):
    return pl.CostEstimate(
        flops=int(flops * HINT),
        bytes_accessed=int((reads + writes) * HINT),
        transcendentals=int(transcendentals * HINT),
    )


VMEM = pl.BlockSpec(memory_space=pltpu.VMEM)
SMEM = pl.BlockSpec(memory_space=pltpu.SMEM)


def on_chip(body, name, arrays, shapes, estimate, scalars=()):
    return pl.pallas_call(
        body,
        in_specs=[SMEM] * len(scalars) + [VMEM] * len(arrays),
        out_specs=[VMEM] * len(shapes),
        out_shape=[jax.ShapeDtypeStruct(*shape) for shape in shapes],
        compiler_params=pltpu.CompilerParams(vmem_limit_bytes=16 * 1024 * 1024),
        cost_estimate=estimate,
        name=name,
    )(*scalars, *arrays)


def chunks(total, size):
    return [(at, min(size, total - at)) for at in range(0, total, size)]


def two_norms(arrays, scales):
    rows, width = arrays[0].shape
    total = rows * len(arrays)
    tile = 32

    def body(scales_ref, *refs):
        one_ref, two_ref, stats_ref = refs[-3:]
        for k in range(len(arrays)):

            @pl.loop(0, rows // tile)
            def _(i, k=k):
                values = refs[k][pl.ds(pl.multiple_of(i * tile, tile), tile), :].astype(F32)
                average = jnp.mean(values, axis=-1, keepdims=True)
                centred = values - average
                variance = jnp.mean(centred * centred, axis=-1, keepdims=True)
                inverse = lax.rsqrt(variance + 1e-05)
                xhat = centred * inverse
                span = pl.ds(pl.multiple_of(k * rows + i * tile, tile), tile)
                one_ref[span, :] = (xhat * scales_ref[0:1, :] + scales_ref[1:2, :]).astype(BF16)
                two_ref[span, :] = (xhat * scales_ref[2:3, :] + scales_ref[3:4, :]).astype(BF16)
                stats_ref[span, :] = jnp.concatenate([average, inverse], axis=1)

    return on_chip(
        body,
        "two_norms",
        [scales, *arrays],
        [((total, width), BF16), ((total, width), BF16), ((total, 2), F32)],
        cost(total * width * 24, total * width * 2, total * width * 4),
    )


class Pieces:
    def __init__(self, arrays, tiles, size, blocks=None):
        self.arrays, self.tiles, self.size, self.blocks = arrays, tiles, size, blocks

    def runs(self):
        found = []
        for k, tile in enumerate(self.tiles):
            at = 0
            for which, first, count in tile:
                last = found[-1] if found else None
                joins = last and self.blocks is None and last[0] == which and last[1] + last[2] == first
                if joins:
                    found[-1] = (which, last[1], last[2] + count, last[3], last[4])
                else:
                    found.append((which, first, count, k, at))
                at += count
        return found


def feed_up(x, pieces, b):
    rows, width = x.shape
    units = pieces.arrays[0].shape[1]

    def body(x_ref, b_ref, *refs):
        w_refs, (act_ref, slope_ref) = refs[:-2], refs[-2:]
        for col, cols in chunks(units, 512):
            for row, count in chunks(rows, 256):
                at = (pl.ds(row, count), pl.ds(col, cols))
                hidden = b_ref[:, at[1]]
                for which, first, depth, k, place in pieces.runs():
                    start = k * pieces.size + place
                    hidden = hidden + matmul(
                        x_ref[at[0], start : start + depth], w_refs[which][first : first + depth, at[1]]
                    )
                cdf = 0.5 + 0.5 * lax.erf(hidden * (0.5**0.5))
                act_ref[at] = (hidden * cdf).astype(BF16)
                slope_ref[at] = cdf + hidden * (jnp.exp(-0.5 * hidden * hidden) * 0.3989422804014327)

    return on_chip(
        body,
        "feed_up",
        [x, b, *pieces.arrays],
        [((rows, units), BF16), ((rows, units), F32)],
        cost(4 * rows * width * units, 2 * (rows + units) * width, 6 * rows * units, 2 * rows * units),
    )


def hidden_grad(g, pieces, slope):
    rows, width = g.shape
    units = slope.shape[1]

    def body(blocks_ref, g_ref, slope_ref, *refs):
        w_refs, (out_ref, sum_ref) = refs[:-2], refs[-2:]
        for which, first, count, k, place in pieces.runs():
            columns = pl.ds(pl.multiple_of(blocks_ref[k] * pieces.size + place, 128), count)
            total = jnp.zeros((1, count), F32)
            for row, size in chunks(rows, 256):
                span = pl.ds(row, size)
                value = times_transposed(g_ref[span, :], w_refs[which][first : first + count, :])
                value = (value * slope_ref[span, columns]).astype(BF16)
                out_ref[span, columns] = value
                total = total + jnp.sum(value.astype(F32), axis=0, keepdims=True)
            sum_ref[:, columns] = total

    return on_chip(
        body,
        "hidden_grad",
        [g, slope, *pieces.arrays],
        [((rows, units), BF16), ((1, units), F32)],
        cost(4 * rows * width * units, 2 * (rows + units) * width + 4 * rows * units, 2 * rows * units),
        [pieces.blocks],
    )


def turn(values, cosine, before, after, sign):
    lanes = cosine.shape[1]
    half = ROT // 2
    first = values[:, :lanes]
    first = first * cosine + sign * (
        pltpu.roll(first, lanes - half, 1) * before + pltpu.roll(first, half, 1) * after
    )
    return jnp.concatenate([first, values[:, lanes:]], axis=1)


def attention_forward(x, pieces, bias, tables, begins):
    count, size, width = x.shape
    columns = bias.shape[1]

    def body(x_ref, b_ref, cos_ref, before_ref, after_ref, begin_ref, *refs):
        w_refs, (qkv_ref, probs_ref, out_ref) = refs[:-3], refs[-3:]
        for n in range(count):
            turns = (cos_ref[n], before_ref[n], after_ref[n])
            projected = b_ref[...]
            for which, first, rows, k, place in pieces.runs():
                start = k * pieces.size + place
                projected = projected + matmul(
                    x_ref[n, :, start : start + rows], w_refs[which][first : first + rows, :]
                )
            queries = turn(projected[:, :HS], *turns, 1.0).astype(BF16)
            keys = turn(projected[:, HS : 2 * HS], *turns, 1.0).astype(BF16)
            values = projected[:, 2 * HS :].astype(BF16)
            qkv_ref[n, :, :HS] = queries
            qkv_ref[n, :, HS : 2 * HS] = keys
            qkv_ref[n, :, 2 * HS :] = values
            for row, tile in chunks(size, 256):
                rows = slice(row, row + tile)
                scores = times_transposed(queries[rows], keys) * (HS**-0.5)
                places = lax.broadcasted_iota(jnp.int32, (tile, size), 1)
                here = lax.broadcasted_iota(jnp.int32, (tile, size), 0) + row
                allowed = (places >= begin_ref[n, rows, :]) & (places <= here)
                masked = jnp.where(allowed, scores, -1e30)
                exponent = jnp.exp(masked - jnp.max(masked, axis=-1, keepdims=True))
                probs = exponent / jnp.sum(exponent, axis=-1, keepdims=True)
                probs_ref[n, rows, :] = probs
                out_ref[n, rows, :] = matmul(probs.astype(BF16), values).astype(BF16)

    return on_chip(
        body,
        "attention_forward",
        [x, bias, *tables, begins, *pieces.arrays],
        [
            ((count, size, columns), BF16),
            ((count, size, size), F32),
            ((count, size, HS), BF16),
        ],
        cost(
            count * size * (size * HS * 8 + 4 * width * columns),
            count * size * width * 2,
            count * size * (columns * 2 + size * 4),
            count * size * size,
        ),
    )


def attention_backward(qkv, probs, g, w_dense, tables):
    count, size, columns = qkv.shape
    scale = HS**-0.5

    def body(qkv_ref, probs_ref, g_ref, w_ref, cos_ref, before_ref, after_ref, out_ref, sum_ref):
        total = jnp.zeros((1, columns), F32)
        for n in range(count):
            turns = (cos_ref[n], before_ref[n], after_ref[n])
            queries = qkv_ref[n, :, :HS]
            keys = qkv_ref[n, :, HS : 2 * HS]
            values = qkv_ref[n, :, 2 * HS :]
            grad = times_transposed(g_ref[n], w_ref[...]).astype(BF16)
            probs_now = probs_ref[n]
            grad_probs = times_transposed(grad, values)
            inner = jnp.sum(probs_now * grad_probs, axis=-1, keepdims=True)
            grad_scores = (probs_now * (grad_probs - inner)).astype(BF16)
            grad_queries = turn(matmul(grad_scores, keys) * scale, *turns, -1.0).astype(BF16)
            grad_keys = turn(left_transposed(grad_scores, queries) * scale, *turns, -1.0).astype(BF16)
            grad_values = left_transposed(probs_now.astype(BF16), grad).astype(BF16)
            whole = jnp.concatenate([grad_queries, grad_keys, grad_values], axis=1)
            out_ref[n] = whole
            total = total + jnp.sum(whole.astype(F32), axis=0, keepdims=True)
        sum_ref[...] = total

    return on_chip(
        body,
        "attention_backward",
        [qkv, probs, g, w_dense, *tables],
        [((count, size, columns), BF16), ((1, columns), F32)],
        cost(
            count * size * (size * HS * 16 + 4 * HS * g.shape[2]),
            count * size * (columns * 4 + size * 4),
            count * size * columns * 2,
        ),
    )


def branch_rows_of(attended, w_dense, activated, pieces, first, count, extra=None):
    width = w_dense.shape[1]
    inner, units = attended.shape[1], activated.shape[1]
    arrays = [attended, w_dense, activated] + ([] if extra is None else [extra])

    def body(blocks_ref, a_ref, wa_ref, b_ref, *refs):
        if extra is not None:
            extra_ref, *refs = refs
        for row, rows in chunks(count, 256):
            span = pl.ds(first * count + row, rows)
            for col, cols in chunks(width, 512):
                at = pl.ds(col, cols)
                value = matmul(a_ref[span, :], wa_ref[:, at])
                for which, start, depth, k, place in pieces.runs():
                    columns = pl.ds(pl.multiple_of(blocks_ref[k] * pieces.size + place, 128), depth)
                    value = value + matmul(b_ref[span, columns], refs[which][start : start + depth, at])
                if extra is not None:
                    value = value + extra_ref[pl.ds(row, rows), at].astype(F32)
                refs[-1][pl.ds(row, rows), at] = value.astype(BF16)

    return on_chip(
        body,
        "branch_rows",
        arrays + pieces.arrays,
        [((count, width), BF16)],
        cost(4 * count * (inner + units) * width, 2 * (inner + units) * (width + count), 2 * count * width),
        [pieces.blocks],
    )[0]


def input_terms(grad_proj, qkv_pieces, grad_hid, up_pieces, x, stats, scales, first, extra=None):
    count, width = x.shape
    tile = up_pieces.size
    columns, units = grad_proj.shape[1], grad_hid.shape[1]
    weights = qkv_pieces.arrays + up_pieces.arrays
    arrays = [grad_proj, grad_hid, x, stats, scales] + ([] if extra is None else [extra])

    def body(gp_ref, gh_ref, x_ref, stats_ref, scales_ref, *refs):
        if extra is not None:
            extra_ref, *refs = refs
        out_ref, sums_ref = refs[-2:]
        split = len(qkv_pieces.arrays)
        for k, (qkv_tile, up_tile) in enumerate(zip(qkv_pieces.tiles, up_pieces.tiles)):
            (which, start, _), = qkv_tile
            wq = refs[which][start : start + tile, :]
            (which, start, _), = up_tile
            wu = refs[split + which][start : start + tile, :]
            at = pl.ds(k * tile, tile)
            sums = [jnp.zeros((1, tile), F32)] * 4
            for row, rows in chunks(count, 256):
                span = pl.ds(row, rows)
                there = pl.ds(first * count + row, rows)
                one = times_transposed(gp_ref[there, :], wq)
                two = times_transposed(gh_ref[there, :], wu)
                xhat = (x_ref[span, at].astype(F32) - stats_ref[there, 0:1]) * stats_ref[there, 1:2]
                value = one * scales_ref[0:1, at] + two * scales_ref[2:3, at]
                if extra is not None:
                    value = value + extra_ref[span, at].astype(F32)
                out_ref[span, at] = value.astype(BF16)
                for n, term in enumerate((one * xhat, one, two * xhat, two)):
                    sums[n] = sums[n] + jnp.sum(term, axis=0, keepdims=True)
            sums_ref[:, at] = jnp.concatenate(sums, axis=0)

    return on_chip(
        body,
        "input_terms",
        arrays + weights,
        [((count, width), BF16), ((4, width), F32)],
        cost(
            4 * count * (columns + units) * width,
            2 * (columns + units) * (width + count) + 2 * count * width,
            2 * count * width,
        ),
    )


def weight_grad(left, right, left_at, right_block, rows, cols, extras=(), halves=False, kind=BF16):
    depth = left.shape[0]

    def body(block_ref, l_ref, r_ref, *refs):
        extra_refs, outs = refs[: len(extras)], refs[len(extras) :]
        where = pl.ds(pl.multiple_of(block_ref[0] * cols, 128), cols)
        tile = min(256, rows // 2)
        for row, size in chunks(rows, tile):
            value = left_transposed(l_ref[:, pl.ds(left_at + row, size)], r_ref[:, where])
            for ref, (array, first) in zip(extra_refs, extras):
                if first <= row < first + array.shape[0]:
                    value = value + ref[pl.ds(row - first, size), :].astype(F32)
            if halves:
                half = rows // 2
                outs[row // half][pl.ds(row % half, size), :] = value.astype(kind)
            else:
                outs[0][pl.ds(row, size), :] = value.astype(kind)

    shapes = [((rows // 2, cols), kind)] * 2 if halves else [((rows, cols), kind)]
    found = on_chip(
        body,
        "weight_grad",
        [left, right, *[e[0] for e in extras]],
        shapes,
        cost(4 * depth * rows * cols, 2 * depth * (rows + cols), rows * cols * 2),
        [jnp.reshape(right_block, (1,)).astype(jnp.int32)],
    )
    return found if halves else found[0]


class Place:
    def __init__(self):
        self.n_dp = lax.axis_size("dp")
        self.n_seq = lax.axis_size("seq")
        assert self.n_dp == 2 * self.n_seq
        self.split = 2 if H % (2 * self.n_seq) == 0 else 1
        self.blocks = self.n_dp // self.split
        self.dp = lax.axis_index("dp")
        self.z = lax.axis_index("seq")
        self.block = self.dp // self.split
        self.part = self.dp % self.split
        self.masks = [1 << k for k in range(self.blocks.bit_length() - 1)]
        self.order = list(range(self.blocks))
        self.paired = self.split == 2 and self.blocks == 4

    def swap(self, value, mask):
        return lax.ppermute(value, "dp", [(i, i ^ mask) for i in range(self.n_dp)])

    def to_relative(self, value, axis):
        size = value.shape[axis] // self.blocks
        return jnp.concatenate(
            [
                lax.dynamic_slice_in_dim(value, (self.block ^ off) * size, size, axis)
                for off in self.order
            ],
            axis=axis,
        )

    def to_natural(self, value, axis):
        return self.to_relative(value, axis)

    def pair(self, own, other, axis):
        return jnp.where(
            self.part == 0,
            jnp.concatenate([own, other], axis=axis),
            jnp.concatenate([other, own], axis=axis),
        )

    def gather(self, piece):
        half = piece.shape[0] // 2
        gathered = []
        for rows, masks in ((piece[:half], self.masks), (piece[half:], self.masks[::-1])):
            have = {0: rows}
            for mask in masks:
                offs = list(have)
                sent = jnp.concatenate([have[o] for o in offs], 0) if len(offs) > 1 else have[offs[0]]
                got = self.swap(sent, mask * self.split)
                for k, o in enumerate(offs):
                    have[o ^ mask] = got[k * half : (k + 1) * half]
            gathered.append(have)
        return gathered

    def spread(self, piece, chain):
        chips = self.n_dp // 2
        masks = [1 << k for k in range(chips.bit_length() - 1)]
        offset = (self.dp // 2) ^ self.z
        half = piece.shape[0] // 2
        states = [(piece[:half], masks, [0]), (piece[half:], masks[::-1], [0])]
        for step in range(len(masks)):
            got = []
            for rows, order, held in states:
                pairs = [
                    (
                        (2 * (z ^ o) + c) * self.n_seq + z,
                        (2 * (z ^ o ^ order[step]) + c) * self.n_seq + z,
                    )
                    for z in range(self.n_seq)
                    for o in held
                    for c in range(2)
                ]
                got.append(lax.ppermute(rows, ("dp", "seq"), pairs))
            yield
            got = chain(*got)
            after = []
            for new, (rows, order, held) in zip(got, states):
                takes = jnp.zeros((), jnp.bool_)
                for o in held:
                    takes = takes | (offset == (o ^ order[step]))
                after.append(
                    (jnp.where(takes, new, rows), order, held + [o ^ order[step] for o in held])
                )
            states = after
            chain.done(tuple(state[0] for state in states))
        self.spread_rows = jnp.concatenate([state[0] for state in states], axis=0)
        yield

    def scatter_sum(self, product, halves):
        out = []
        for half, masks in zip(halves, (self.masks, self.masks[::-1])):
            live = list(range(self.blocks))
            extra = {}

            def total(offs):
                whole = product(half, offs)
                if all(o not in extra for o in offs):
                    return whole
                axis, size = whole.ndim and product.axis, whole.shape[product.axis] // len(offs)
                parts = []
                for k, o in enumerate(offs):
                    value = lax.slice_in_dim(whole, k * size, (k + 1) * size, axis=axis)
                    for more in extra.get(o, ()):
                        value = value + more.astype(F32)
                    parts.append(value)
                return parts[0] if len(parts) == 1 else jnp.concatenate(parts, axis=axis)

            for mask in masks:
                away = [o for o in self.order if o in live and o & mask]
                sent = total(away).astype(BF16)
                got = self.swap(sent, mask * self.split)
                size = got.shape[product.axis] // len(away)
                for k, o in enumerate(away):
                    extra.setdefault(o ^ mask, []).append(
                        lax.slice_in_dim(got, k * size, (k + 1) * size, axis=product.axis)
                    )
                live = [o for o in live if not o & mask]
            out.append(total([0]))
        return out


class Product:
    def __init__(self, place, by_block, other, axis):
        self.place, self.by_block, self.other, self.axis = place, by_block, other, axis
        self.size = by_block.shape[1] // place.blocks

    def __call__(self, half, offs):
        where = [self.place.order.index(o) for o in offs]
        if where == list(range(where[0], where[0] + len(where))):
            blocks = self.by_block[:, where[0] * self.size : (where[-1] + 1) * self.size]
        else:
            blocks = jnp.concatenate(
                [self.by_block[:, w * self.size : (w + 1) * self.size] for w in where], axis=1
            )
        width = self.other.shape[1] // 2
        others = self.other[:, half * width : (half + 1) * width]
        if self.axis == 0:
            return left_transposed(blocks, others)
        return left_transposed(others, blocks)


class Chain:
    def __init__(self):
        self.last = None

    def __call__(self, *values):
        if self.last is not None:
            values = tuple(lax.optimization_barrier((values, self.last))[0])
        return values if len(values) > 1 else values[0]

    def done(self, value):
        self.last = value
        return value


class Gathered:
    def __init__(self, here, piece):
        self.here, self.piece = here, piece
        self.half = piece.shape[0] // 2
        if here.paired:
            self.by_x, self.by_y = here.swap(piece, 2), here.swap(piece, 4)

    def hand_on(self, chain):
        if self.here.paired:
            by_x, by_y = chain(self.by_x, self.by_y)
            first, second = by_x[: self.half], by_y[self.half :]
            chain.done((first, second))
            self.handed = (self.here.swap(first, 4), self.here.swap(second, 2))

    def rows(self, size, moving):
        here, block = self.here, self.piece.shape[0]
        if here.paired:
            arrays = [self.piece, self.by_x, self.by_y, *self.handed]
            parts = [(k, r, block) for k in range(3) for r in (0,)] + [(3, 0, self.half), (4, 0, self.half)]
            tiles, now, left = [], [], size
            for which, first, count in parts:
                while count:
                    take = min(left, count)
                    now.append((which, first, take))
                    first, count, left = first + take, count - take, left - take
                    if not left:
                        tiles.append(now)
                        now, left = [], size
            blocks = None
            if moving:
                assert size == block
                blocks = here.block ^ jnp.arange(here.blocks, dtype=jnp.int32)
            return Pieces(arrays, tiles, size, blocks)
        halves = here.gather(self.piece)
        order = [here.block ^ k for k in range(here.blocks)] if moving else None
        whole = jnp.concatenate([half[o] for o in range(here.blocks) for half in halves], axis=0)
        if moving:
            whole = here.to_natural(whole, 0)
        count = whole.shape[0] // size
        blocks = jnp.arange(count, dtype=jnp.int32) if moving else None
        return Pieces([whole], [[(0, k * size, size)] for k in range(count)], size, blocks)


class Scattered:
    def __init__(self, here, left, right, axis):
        self.here, self.left, self.right, self.axis = here, left, right, axis
        self.size = (left if axis == 0 else right).shape[1] // here.blocks

    def part(self, off, **more):
        if self.axis == 0:
            return weight_grad(
                self.left, self.right, off * self.size, jnp.int32(0), self.size, self.right.shape[1], **more
            )
        return weight_grad(
            self.left, self.right, 0, self.here.block ^ off, self.left.shape[1], self.size, **more
        )

    def first(self, chain):
        if self.here.paired:
            self.left, self.right = chain(self.left, self.right)
            one, two = chain.done(self.part(3, halves=True))
            self.by_x, self.by_y = self.here.swap(one, 2), self.here.swap(two, 4)

    def second(self, chain):
        if self.here.paired:
            by_x, by_y = chain(self.by_x, self.by_y)
            half = by_x.shape[0]
            to_x = self.part(1, extras=((by_y, half),))
            to_y = self.part(2, extras=((by_x, 0),))
            chain.done((to_x, to_y))
            self.by_x, self.by_y = self.here.swap(to_x, 2), self.here.swap(to_y, 4)

    def last(self, chain, kind):
        if self.here.paired:
            by_x, by_y = chain(self.by_x, self.by_y)
            return chain.done(self.part(0, extras=((by_x, 0), (by_y, 0)), kind=kind))
        right = self.right
        if self.axis == 1:
            right = self.here.to_relative(right, 1)
            product = Product(self.here, right, self.left, 1)
        else:
            product = Product(self.here, self.left, right, 0)
        halves = self.here.scatter_sum(product, (0, 1))
        return jnp.concatenate(halves, axis=1 - self.axis).astype(kind)


def on_device(
    tokens,
    doc_lengths,
    qkv_weight,
    qkv_bias,
    dense_weight,
    dense_bias,
    up_weight,
    up_bias,
    down_weight,
    down_bias,
    norm1_gain,
    norm1_shift,
    norm2_gain,
    norm2_shift,
    cotangent,
):
    here = Place()
    chain = Chain()
    n_dp, n_seq, split, blocks = here.n_dp, here.n_seq, here.split, here.blocks
    z, part = here.z, here.part
    rows_here, width = tokens.shape
    seq_len = rows_here * n_seq
    hidden_rows = down_weight.shape[0]
    slice_rows = hidden_rows // n_seq
    assert H == n_seq * split
    head_cols = 3 * HS

    tokens_rel = chain.done(here.to_relative(tokens, 1))
    x_own = lax.all_gather(tokens_rel, "seq", axis=0, tiled=True)

    def up_columns(weight, core):
        return jnp.concatenate(
            [
                lax.dynamic_slice_in_dim(
                    weight, (k * split + core) * hidden_rows + z * slice_rows, slice_rows, 1
                )
                for k in range(blocks)
            ],
            axis=1,
        )

    def qkv_columns(weight, core):
        return lax.dynamic_slice_in_dim(weight, (z * split + core) * head_cols, head_cols, 1)

    def first_exchange(columns, weight):
        if split == 2:
            return here.swap(chain.done(columns(chain(weight), 1 - part)), 1)
        return None

    def chip_rows(columns, weight, got):
        own = columns(chain(weight), part)
        return chain.done(own if got is None else here.pair(own, got, 0))

    up_got = first_exchange(up_columns, up_weight)
    qkv_got = first_exchange(qkv_columns, qkv_weight)
    dense_steps = here.spread(dense_weight, chain)
    next(dense_steps)
    up_rows = Gathered(here, chip_rows(up_columns, up_weight, up_got))
    qkv_rows = Gathered(here, chip_rows(qkv_columns, qkv_weight, qkv_got))
    g_own = lax.all_gather(chain(cotangent), "seq", axis=0, tiled=True)
    down_piece = chain.done(
        lax.dynamic_slice_in_dim(chain(down_weight), z * slice_rows, slice_rows, 0)
    )

    small = (qkv_bias, up_bias, dense_bias, down_bias, norm1_gain, norm1_shift, norm2_gain, norm2_shift)
    packed_small = jnp.concatenate(chain(*small))
    packed_small = chain.done(jnp.broadcast_to(packed_small[None], (n_dp,) + packed_small.shape))
    packed_small = lax.all_to_all(packed_small, "dp", 0, 0, tiled=True)
    lengths = chain(doc_lengths)
    if split == 2:
        lengths = jnp.concatenate([lengths, here.swap(lengths, 1)], axis=0)

    places = jnp.arange(seq_len, dtype=jnp.int32)
    _, positions = jax.vmap(lambda row: doc_layout(row, places))(lengths)
    cosine, sine = jax.vmap(lambda p: turn_tables(p, ROT))(positions)
    lanes = 128
    rest = ((0, 0), (0, 0), (0, lanes - ROT))
    half_rot = ROT // 2
    tables = (
        jnp.pad(cosine, rest, constant_values=1.0),
        jnp.pad(-sine[..., :half_rot], ((0, 0), (0, 0), (0, lanes - half_rot))),
        jnp.pad(sine[..., half_rot:], ((0, 0), (0, 0), (half_rot, lanes - ROT))),
    )
    begins = (places[None] - positions)[..., None]

    spans, first = [], 0
    for value in small:
        spans.append(packed_small[:, first : first + value.shape[0]].astype(F32))
        first += value.shape[0]
    b_qkv, b_up, b_dense, b_down = spans[:4]
    b_qkv = lax.dynamic_slice_in_dim(b_qkv.reshape(-1), (z * split + part) * head_cols, head_cols, 0)
    b_up = lax.dynamic_slice_in_dim(b_up, z * slice_rows, slice_rows, 1).reshape(
        blocks, split, slice_rows
    )
    b_up = lax.dynamic_index_in_dim(b_up, part, 1, keepdims=False).reshape(-1)
    b_out = (b_dense + b_down).reshape(-1)
    scales = here.to_relative(jnp.stack([v.reshape(-1) for v in spans[4:]]), 1)
    if here.paired:
        (b_qkv, b_up, scales, begins) = chain(b_qkv, b_up, scales, begins)
        tables = chain(*tables)
        chain.done((b_qkv, b_up, scales, tables, begins))

    next(dense_steps)
    up_rows.hand_on(chain)
    down_rows = Gathered(here, chain(down_piece))
    x_own = chain(x_own)
    streams = [x_own] + ([here.swap(x_own, 1)] if split == 2 else [])
    for _ in dense_steps:
        pass
    w_dense = here.spread_rows
    if split == 1:
        other = here.swap(w_dense, 1)
        w_dense = jnp.where(
            here.dp % 2 == 0,
            jnp.concatenate([w_dense, other], 0),
            jnp.concatenate([other, w_dense], 0),
        )
    qkv_rows.hand_on(chain)
    normed_one, normed_two, stats = chain.done(two_norms(chain(*streams) if split == 2 else streams, scales))
    up_pieces = up_rows.rows(256, False)
    activated, slope = chain.done(feed_up(chain(normed_two), up_pieces, b_up[None]))
    qkv_pieces = qkv_rows.rows(256, False)
    qkv, probs, attended = chain.done(
        attention_forward(
            chain(normed_one).reshape(split, seq_len, width), qkv_pieces, b_qkv[None], tables, begins
        )
    )
    attended = attended.reshape(split * seq_len, HS)

    g_own = chain(g_own)
    g_all = jnp.concatenate([g_own, here.swap(g_own, 1)], axis=0) if split == 2 else g_own
    down_rows.hand_on(chain)
    sum_down = Scattered(here, activated, g_all, 1)
    sum_dense = Scattered(here, attended, g_all, 1)
    sum_down.first(chain)
    sum_dense.first(chain)
    grad_projected, grad_qkv_bias = chain.done(
        attention_backward(chain(qkv), probs, g_all.reshape(split, seq_len, width), w_dense, tables)
    )
    grad_projected = grad_projected.reshape(split * seq_len, head_cols)
    sum_qkv = Scattered(here, normed_one, grad_projected, 0)
    sum_qkv.first(chain)
    sum_down.second(chain)
    down_pieces = down_rows.rows(down_piece.shape[0] if here.paired else 256, True)

    def join(value):
        return lax.psum_scatter(value, "seq", scatter_dimension=0, tiled=True).astype(F32)

    def branches(first, extra=None):
        return chain.done(
            branch_rows_of(chain(attended), w_dense, activated, down_pieces, first, seq_len, extra)
        )

    def terms(first, extra=None):
        return chain.done(
            input_terms(
                chain(grad_projected),
                qkv_pieces,
                grad_hidden,
                up_pieces,
                streams[first],
                stats,
                scales,
                first,
                extra,
            )
        )

    branch_other = here.swap(branches(1), 1) if split == 2 else None
    grad_hidden, grad_up_bias = chain.done(hidden_grad(chain(g_all), down_pieces, slope))
    sum_up = Scattered(here, normed_two, grad_hidden, 0)
    branch_rows = join(branches(0, branch_other))
    sum_up.first(chain)
    if split == 2:
        term_other, norm_sums = terms(1)
        term_other = here.swap(term_other, 1)
        sum_dense.second(chain)
        term_own, more_sums = terms(0, term_other)
        norm_sums = norm_sums + more_sums
    else:
        term_own, norm_sums = terms(0)
    term_rows = join(term_own)
    sum_up.second(chain)
    output = chain.done((chain(branch_rows) + tokens.astype(F32) + b_out).astype(BF16))
    sum_qkv.second(chain)

    norm_sums = here.to_natural(chain(norm_sums), 1)
    wide_qkv = lax.dynamic_update_slice_in_dim(
        jnp.zeros((H * head_cols,), F32), grad_qkv_bias.reshape(-1), (z * split + part) * head_cols, 0
    )
    wide_up = lax.dynamic_update_slice(
        jnp.zeros((blocks, split, n_seq, slice_rows), F32),
        grad_up_bias.reshape(blocks, 1, 1, slice_rows),
        (0, part, z, 0),
    )
    cotan_rows = cotangent.astype(F32)
    column_total = jnp.sum(cotan_rows, axis=0)
    devices = n_dp * n_seq
    wide = [wide_qkv, wide_up, column_total] + [norm_sums[k] for k in range(4)]
    wide = [v.reshape(devices, -1) for v in wide]
    sizes = [v.shape[1] for v in wide]
    swapped = lax.all_to_all(
        chain.done(jnp.concatenate(wide, axis=1)), ("dp", "seq"), split_axis=0, concat_axis=0, tiled=True
    )
    total = jnp.sum(swapped, axis=0)
    sums, first = [], 0
    for size in sizes:
        sums.append(total[first : first + size])
        first += size
    sum_qkv_bias, sum_up_bias, sum_column, sum_gain_one, sum_shift_one, sum_gain_two, sum_shift_two = sums

    def to_plane(whole, axis):
        moved = lax.all_to_all(whole, "seq", split_axis=axis, concat_axis=axis, tiled=True)
        if split == 1:
            per = moved.shape[axis] // (n_seq * 2)
            if axis == 0:
                moved = moved.reshape(n_seq, 2, per, -1).transpose(1, 0, 2, 3).reshape(moved.shape)
            else:
                moved = moved.reshape(-1, n_seq, 2, per).transpose(0, 2, 1, 3).reshape(moved.shape)
        return moved

    def to_cores(value, axis):
        if split == 1:
            return value.astype(F32)
        size = value.shape[axis] // 2
        mine = lax.dynamic_slice_in_dim(value, part * size, size, axis)
        other = lax.dynamic_slice_in_dim(value, (1 - part) * size, size, axis)
        return here.pair(mine, here.swap(other, 1), 1 - axis).astype(F32)

    grad_down = to_cores(to_plane(sum_down.last(chain, BF16), 0), 1)
    grad_dense = to_cores(sum_dense.last(chain, F32), 1)
    grad_up = to_cores(to_plane(sum_up.last(chain, BF16), 1), 0)
    grad_qkv = to_cores(sum_qkv.last(chain, F32), 0)

    values = tokens_rel.astype(F32)
    centred = values - jnp.mean(values, axis=-1, keepdims=True)
    inverse = lax.rsqrt(jnp.mean(centred * centred, axis=-1, keepdims=True) + 1e-05)
    xhat = centred * inverse
    term = (
        term_rows
        - jnp.mean(term_rows, axis=-1, keepdims=True)
        - xhat * jnp.mean(term_rows * xhat, axis=-1, keepdims=True)
    ) * inverse
    input_grad = (cotan_rows + here.to_natural(term, 1)).astype(BF16)
    return (
        output,
        input_grad,
        grad_qkv,
        sum_qkv_bias,
        grad_dense,
        sum_column,
        grad_up,
        sum_up_bias,
        grad_down,
        sum_column,
        sum_gain_one,
        sum_shift_one,
        sum_gain_two,
        sum_shift_two,
    )


def solution(mesh):
    rows = P(("dp", "seq"), None)
    flat = P(("dp", "seq"))
    placed = (rows,) + (P("dp", None),) * 2 + (P("dp"), P("dp", None)) * 3 + (P("dp"),) * 5 + (rows,)
    return jax.shard_map(
        on_device,
        mesh=mesh,
        in_specs=placed,
        out_specs=(
            rows,
            rows,
            P("dp", "seq"),
            flat,
            P("seq", "dp"),
            flat,
            P("dp", "seq"),
            flat,
            P("seq", "dp"),
            flat,
            flat,
            flat,
            flat,
            flat,
        ),
        check_vma=False,
    )
```

time: 563 us -> 413 us (0.73)
  matrix products: 120 us -> 0 us
  Pallas kernels: 0 us -> 89.6 us
  waiting for transfers between devices: 177 us -> 122 us
  other arithmetic: 79.4 us -> 32.3 us
  blocking collectives: 17.1 us -> 0 us
    dot_general x37 -> x0, matrix products: 116 us -> none  [the longest x24 52.9 us: left_transposed(): lax.dot_general(left, right, (((0,), (0,)), ((), ())), preferred_element_...]
    pallas_call x0 -> x25, Pallas kernels: none -> 89.6 us  [on_chip(): pl.pallas_call(body, in_specs=[SMEM] * len(scalars) + [VMEM] * len(arrays...]
    ppermute x39, waiting for transfers between devices: 99.6 us -> 53.5 us  [swap(): return lax.ppermute(value, 'dp', [(i, i ^ mask) for i in range(self.n_dp)])]
    unnamed x189 -> x209, local copies, waits for them, and re-layouts: 26.6 us -> 46.1 us
    all_gather x1 -> x0, blocking collectives: 17.1 us -> none  [on_device(): lax.all_gather(jnp.concatenate(small)[None], 'dp', axis=0, tiled=True)]
    ppermute x4, waiting for transfers between devices: 26.6 us -> 9.6 us  [spread(): got.append(lax.ppermute(rows, ('dp', 'seq'), pairs))]
    reduce_scatter x2, waiting for transfers between devices: 0.02 us -> 15 us  [join(): lax.psum_scatter(value, 'seq', scatter_dimension=0, tiled=True).astype(F32)]
    convert_element_type x5 -> x2, other arithmetic: 16.8 us -> 2.2 us  [the longest x1 1.26 us: join(): lax.psum_scatter(value, 'seq', scatter_dimension=0, tiled=True).astype(F32)]
  transfers between devices with their start and end apart: 50 -> 51, of which waited for: 17 -> 15; matrix products, arithmetic and copies ran while one was open for 32% -> 17% of each run, Pallas kernels for 0% -> 20%
where the time goes in v2:
time: 413 us; the launch traced here: 406 us
  waiting for transfers between devices  122 us (30%)
  Pallas kernels  89.6 us (22%)
  local copies, waits for them, and re-layouts  82.4 us (20%)
  starting transfers between devices  64.2 us (16%)
  other arithmetic  32.3 us (8%)
  between operations  15.4 us (4%)
    pallas_call x25, Pallas kernels, on_chip(): pl.pallas_call(body, in_specs=[SMEM] * len(scalars) + [VMEM] * len(arrays...  89.6 us
    ppermute x39, waiting for transfers between devices, swap(): return lax.ppermute(value, 'dp', [(i, i ^ mask) for i in range(self.n_dp)])  53.5 us
    unnamed x209, local copies, waits for them, and re-layouts  46.1 us
    all_to_all x2, waiting for transfers between devices, to_plane(): lax.all_to_all(whole, 'seq', split_axis=axis, concat_axis=axis, tiled=True)  33.9 us
    ppermute x39, starting transfers between devices, swap(): return lax.ppermute(value, 'dp', [(i, i ^ mask) for i in range(self.n_dp)])  30.6 us
    ppermute x4, starting transfers between devices, spread(): got.append(lax.ppermute(rows, ('dp', 'seq'), pairs))  16.3 us
    reduce_scatter x2, waiting for transfers between devices, join(): lax.psum_scatter(value, 'seq', scatter_dimension=0, tiled=True).astype(F32)  15 us
    all_to_all x1, waiting for transfers between devices, on_device(): packed_small = lax.all_to_all(packed_small, 'dp', 0, 0, tiled=True)  9.63 us
  transfers between devices with their start and end apart: 51, of which 15 were waited for; matrix products, arithmetic and copies ran while one was open for 17% of the time, Pallas kernels for 20%

profile of v2, /device:TPU:0, one launch (start us, length us, event | category | flops | bytes accessed | tf_op | source)
XLA Modules:
  0.0 405.8 jit_solution(16453689678533491816)
XLA Ops:
  12.8 2.3 fusion.14
  15.1 5.7 %collective-permute-start.5 = (bf16[128,2048]{1,0:T(8,128)(2,1)}, bf16[128,2048]{1,0:T(8,128)(2,1)}, u32[]{:S(2)}, u32[]{:S(2)}) collective-permute-start(bf16[128,2048]{1,0:T(8,128)(2,1)} %get-tuple-element.261), channel_id=1, source_target_pairs={{0,8},{4,12},{9,1},{13,5},{18,26},{22,30},{27,19},{31,23}} | collective-permute-start | bytes 1572872 | tf_op jit(solution)/shard_map/ppermute | solution.py:450
  20.8 2.1 collective-permute-start.6
  22.9 1.8 constant_dynamic-slice_fusion.27
  24.7 2.7 maximum_select_fusion.1.refs_0_.refs_5_.refs_6_
  29.1 2.6 constant_dynamic-slice_fusion.22.refs_0_.refs_1_
  35.4 4.7 %all-to-all-start = ((bf16[8,2,1664]{2,1,0:T(2,128)(2,1)}), bf16[8,2,1664]{2,1,0:T(2,128)(2,1)S(1)}, u32[]{:S(2)}, u32[]{:S(2)}) async-start(bf16[8,2,1664]{2,1,0:T(2,128)(2,1)} %reshape.196), calls=%async_computation | async-start | bytes 106496 | tf_op jit(solution)/shard_map/all_to_all | solution.py:687
  41.9 2.2 fusion.10
  47.0 9.6 %all-to-all-done = bf16[8,2,1664]{2,1,0:T(2,128)(2,1)S(1)} async-done(((bf16[8,2,1664]{2,1,0:T(2,128)(2,1)}), bf16[8,2,1664]{2,1,0:T(2,128)(2,1)S(1)}, u32[]{:S(2)}, u32[]{:S(2)}) %all-to-all-start) | async-done | bytes 53280 | tf_op jit(solution)/shard_map/all_to_all | solution.py:687
  58.0 1.9 slice.97
  59.9 1.9 slice.98
  61.8 6.4 %collective-permute-start.10 = (bf16[128,2048]{1,0:T(8,128)(2,1)}, bf16[128,2048]{1,0:T(8,128)(2,1)}, u32[]{:S(2)}, u32[]{:S(2)}) collective-permute-start(bf16[128,2048]{1,0:T(8,128)(2,1)} %get-tuple-element.259), channel_id=1, source_target_pairs={{0,16},{4,20},{8,24},{12,28},{9,25},{13,29},{1,17},{5,21},{18,2},{... | collective-permute-start | bytes 1572872 | tf_op jit(solution)/shard_map/ppermute | solution.py:450
  68.2 2.1 collective-permute-start.11
  70.3 9.6 %collective-permute-done.10 = bf16[128,2048]{1,0:T(8,128)(2,1)} collective-permute-done((bf16[128,2048]{1,0:T(8,128)(2,1)}, bf16[128,2048]{1,0:T(8,128)(2,1)}, u32[]{:S(2)}, u32[]{:S(2)}) %collective-permute-start.10) | collective-permute-done | bytes 524320 | tf_op jit(solution)/shard_map/ppermute | solution.py:450
  79.9 2.5 collective-permute-start.12
  82.4 1.9 collective-permute-start.13
  84.3 2.2 broadcast_select_fusion
  86.4 12.1 %collective-permute-done.8.refs_1_.refs_2_ = bf16[512,768]{1,0:T(8,128)(2,1)S(1)} collective-permute-done((bf16[512,768]{1,0:T(8,128)(2,1)S(1)}, bf16[512,768]{1,0:T(8,128)(2,1)S(1)}, u32[]{:S(2)}, u32[]{:S(2)}) %collective-permute-start.8) | collective-permute-done | bytes 786464 | tf_op jit(solution)/shard_map/ppermute | solution.py:396
  100.7 1.9 collective-permute-start.15
  105.3 10.3 %two_norms.1 = (bf16[1024,2048]{1,0:T(8,128)(2,1)S(1)}, bf16[1024,2048]{1,0:T(8,128)(2,1)S(1)}, f32[1024,2]{1,0:T(8,128)S(1)}) custom-call(f32[4,2048]{1,0:T(4,128)S(1)} %pad_maximum_fusion.4.scales_ref, bf16[512,2048]{1,0:T(8,128)(2,1)S(1)} %copy-done.33, bf16[512,2048]{1,0:T(8,128)(2,1)} %collective-permute-done.7.refs_1_.x_ref), custom_call_target="tpu_custom_call" | custom-call | flops 2516582 | bytes 629145 | tf_op jit(solution)/shard_map/two_norms/pallas_call | solution.py:57
  116.5 11.1 %feed_up.1 = (bf16[1024,1024]{1,0:T(8,128)(2,1)S(1)}, f32[1024,1024]{1,0:T(8,128)S(1)}) custom-call(bf16[1024,2048]{1,0:T(8,128)(2,1)S(1)} %get-tuple-element.178.x_ref.l_ref, f32[1,1024]{1,0:T(1,128)S(1)} %bitcast.57, bf16[512,1024]{1,0:T(8,128)(2,1)} %maximum_select_fusion.1.refs_0_.refs_5_.refs_6_, ...), custom_call_target="tpu_custom_call" | custom-call | flops 429496736 | bytes 734003 | tf_op jit(solution)/shard_map/feed_up/pallas_call | solution.py:57
  127.7 2.0 copy-done.42
  129.7 7.6 %attention_forward.1 = (bf16[2,512,768]{2,1,0:T(8,128)(2,1)S(1)}, f32[2,512,512]{2,1,0:T(8,128)S(1)}, bf16[2,512,256]{2,1,0:T(8,128)(2,1)S(1)}) custom-call(bf16[2,512,2048]{2,1,0:T(8,128)(2,1)S(1)} %bitcast.43, f32[1,768]{1,0:T(1,128)S(1)} %broadcast_in_dim.49.b_ref, f32[2,512,128]{2,1,0:T(8,128)S(1)} %copy-done.40, f32[2,512,128]{2,1,0:T(8,128)S(1)} %copy-done.36, ...), custom_call_target="tpu_custom_call" | custom-call | flops 375809632 | bytes 393216 | tf_op jit(solution)/shard_map/attention_forward/pallas_call | solution.py:57
  139.9 2.0 collective-permute-start.18
  141.9 23.7 %collective-permute-done.17.refs_1_.refs_2_ = bf16[256,2048]{1,0:T(8,128)(2,1)S(1)} collective-permute-done((bf16[256,2048]{1,0:T(8,128)(2,1)}, bf16[256,2048]{1,0:T(8,128)(2,1)S(1)}, u32[]{:S(2)}, u32[]{:S(2)}) %collective-permute-start.17) | collective-permute-done | bytes 1048608 | tf_op jit(solution)/shard_map/ppermute | solution.py:396
  167.8 1.8 collective-permute-start.19
  169.6 1.7 collective-permute-start.20
  174.5 4.4 %attention_backward.1 = (bf16[2,512,768]{2,1,0:T(8,128)(2,1)S(1)}, f32[1,768]{1,0:T(1,128)S(1)}) custom-call(bf16[2,512,768]{2,1,0:T(8,128)(2,1)S(1)} %copy-done.53, f32[2,512,512]{2,1,0:T(8,128)S(1)} %copy-done.45, bf16[2,512,2048]{2,1,0:T(8,128)(2,1)S(1)} %bitcast.42, bf16[256,2048]{1,0:T(8,128)(2,1)S(1)} %pad_maximum_fusion.w_ref.wa_ref, ...), custom_call_target="tpu_custom_call" | custom-call | flops 214748368 | bytes 340787 | tf_op jit(solution)/shard_map/attention_backward/pallas_call | solution.py:57
  180.0 2.6 collective-permute-done.19.refs_0_
  182.7 1.8 collective-permute-done.20.refs_0_
  188.2 6.0 %collective-permute-done.21.refs_3_.refs_4_ = bf16[128,2048]{1,0:T(8,128)(2,1)S(1)} collective-permute-done((bf16[128,2048]{1,0:T(8,128)(2,1)S(1)}, bf16[128,2048]{1,0:T(8,128)(2,1)S(1)}, u32[]{:S(2)}, u32[]{:S(2)}) %collective-permute-start.21) | collective-permute-done | bytes 524320 | tf_op jit(solution)/shard_map/ppermute | solution.py:396
  194.2 4.0 branch_rows.2
  198.3 6.5 %hidden_grad.1 = (bf16[1024,1024]{1,0:T(8,128)(2,1)S(1)}, f32[1,1024]{1,0:T(1,128)S(1)}) custom-call(s32[4]{0:T(128)S(1)} %iota_xor_fusion.blocks_ref, bf16[1024,2048]{1,0:T(8,128)(2,1)S(1)} %constant_dynamic-update-slice_fusion.1.r_ref.g_ref, f32[1024,1024]{1,0:T(8,128)S(1)} %copy-done.43, bf16[256,2048]{1,0:T(8,128)(2,1)S(1)} %copy-done.23, ...), custom_call_target="tpu_custom_call" | custom-call | flops 429496736 | bytes 734003 | tf_op jit(solution)/shard_map/hidden_grad/pallas_call | solution.py:57
  206.1 4.1 %branch_rows.3 = bf16[512,2048]{1,0:T(8,128)(2,1)S(1)} custom-call(s32[4]{0:T(128)S(1)} %iota_xor_fusion.blocks_ref, bf16[1024,256]{1,0:T(8,128)(2,1)S(1)} %bitcast.52, bf16[256,2048]{1,0:T(8,128)(2,1)S(1)} %pad_maximum_fusion.w_ref.wa_ref, bf16[1024,1024]{1,0:T(8,128)(2,1)S(1)} %get-tuple-element.156.l_ref.b_ref, ...), custom_call_target="tpu_custom_call" | custom-call | flops 268435456 | bytes 432537 | tf_op jit(solution)/shard_map/branch_rows/pallas_call | solution.py:57
  211.6 2.2 copy-done.11
  219.7 7.7 %input_terms.2 = (bf16[512,2048]{1,0:T(8,128)(2,1)S(1)}, f32[4,2048]{1,0:T(4,128)S(1)}) custom-call(bf16[1024,768]{1,0:T(8,128)(2,1)S(1)} %bitcast.45, bf16[1024,1024]{1,0:T(8,128)(2,1)S(1)} %copy-done.16, bf16[512,2048]{1,0:T(8,128)(2,1)} %collective-permute-done.7.refs_1_.x_ref, f32[1024,2]{1,0:T(8,128)S(1)} %copy-done.51, ...), custom_call_target="tpu_custom_call" | custom-call | flops 375809632 | bytes 668467 | tf_op jit(solution)/shard_map/input_terms/pallas_call | solution.py:57
  229.8 3.7 collective-permute-done.26.refs_0_
  236.5 7.2 %input_terms.3 = (bf16[512,2048]{1,0:T(8,128)(2,1)S(1)}, f32[4,2048]{1,0:T(4,128)S(1)}) custom-call(bf16[1024,768]{1,0:T(8,128)(2,1)S(1)} %bitcast.46, bf16[1024,1024]{1,0:T(8,128)(2,1)S(1)} %copy-done.16, bf16[512,2048]{1,0:T(8,128)(2,1)S(1)} %copy-done.34, f32[1024,2]{1,0:T(8,128)S(1)} %copy-done.51, f32[4,2048]{1,0:T(4,128)S(1)} %pad_maximum_fusion.4.scales_ref, ...), custom_call_target="tpu_custom_call" | custom-call | flops 375809632 | bytes 668467 | tf_op jit(solution)/shard_map/input_terms/pallas_call | solution.py:57
  245.6 1.6 collective-permute-start.24
  252.8 1.6 dynamic_update_slice.6
  255.8 1.6 collective-permute-start.37
  264.8 2.2 copy-done.12
  268.6 3.4 weight_grad.24
  272.0 2.3 weight_grad.25
  276.5 1.6 collective-permute-start.33
  278.7 2.2 copy-done.8
  280.9 3.0 weight_grad.26
  286.2 15.0 %reduce-scatter.5.cloned.1.call-done = bf16[128,2048]{1,0:T(8,128)(2,1)} async-done(((bf16[512,2048]{1,0:T(8,128)(2,1)}), bf16[128,2048]{1,0:T(8,128)(2,1)}) %reduce-scatter.5.cloned.1.call-update) | async-done | bytes 524304 | tf_op jit(solution)/shard_map/reduce_scatter | solution.py:766
  302.9 1.7 fusion.4
  308.1 3.0 all-to-all-start.1
  311.1 2.2 copy-done.4
  313.3 4.1 %weight_grad.28 = bf16[1024,512]{1,0:T(8,128)(2,1)} custom-call(s32[1]{0:T(128)} %bitcast.10.block_ref, bf16[1024,1024]{1,0:T(8,128)(2,1)S(1)} %get-tuple-element.156.l_ref.b_ref, bf16[1024,2048]{1,0:T(8,128)(2,1)S(1)} %copy-done.4, bf16[1024,512]{1,0:T(8,128)(2,1)} %collective-permute-done.37.refs_0_, bf16[1024,512]{1,0:T(8,128)(2,1)} %collective-permute-done.38.refs_1_), custom_call_target="tpu_custom_call" | custom-call | flops 107374184 | bytes 209715 | tf_op jit(solution)/shard_map/weight_grad/pallas_call | solution.py:57
  317.4 2.6 collective-permute-done.36.refs_1_
  322.2 2.9 weight_grad.30
  326.2 5.0 %all-to-all-start.2 = ((bf16[512,4,256]{2,0,1:T(8,128)(2,1)}), bf16[512,4,256]{2,0,1:T(8,128)(2,1)}, u32[]{:S(2)}, u32[]{:S(2)}) async-start(bf16[512,4,256]{2,0,1:T(8,128)(2,1)} %bitcast.40), calls=%async_computation.4 | async-start | bytes 2097152 | tf_op jit(solution)/shard_map/all_to_all | solution.py:832
  333.0 22.7 %all-to-all-done.2 = bf16[512,4,256]{2,0,1:T(8,128)(2,1)} async-done(((bf16[512,4,256]{2,0,1:T(8,128)(2,1)}), bf16[512,4,256]{2,0,1:T(8,128)(2,1)}, u32[]{:S(2)}, u32[]{:S(2)}) %all-to-all-start.2) | async-done | bytes 1048608 | tf_op jit(solution)/shard_map/all_to_all | solution.py:832
  355.7 4.5 %all-to-all-start.3 = ((bf16[4,256,512]{2,1,0:T(8,128)(2,1)}), bf16[4,256,512]{2,1,0:T(8,128)(2,1)}, u32[]{:S(2)}, u32[]{:S(2)}) async-start(bf16[4,256,512]{2,1,0:T(8,128)(2,1)} %bitcast.14), calls=%async_computation.5 | async-start | bytes 2097152 | tf_op jit(solution)/shard_map/all_to_all | solution.py:832
  362.0 2.2 copy-done.9
  372.9 1.9 maximum_select_fusion.5
  374.9 11.2 %all-to-all-done.3 = bf16[4,256,512]{2,1,0:T(8,128)(2,1)} async-done(((bf16[4,256,512]{2,1,0:T(8,128)(2,1)}), bf16[4,256,512]{2,1,0:T(8,128)(2,1)}, u32[]{:S(2)}, u32[]{:S(2)}) %all-to-all-start.3) | async-done | bytes 1048608 | tf_op jit(solution)/shard_map/all_to_all | solution.py:832
  386.1 2.2 constant_dynamic-slice_fusion.1
  389.7 2.7 fusion.8
  392.4 3.0 copy.46
  395.5 3.1 fusion.9
  (371 shorter events, 94.4 us)
Async XLA Ops:
  7.2 54.6 %all-gather.3.cloned.1.call-start = ((), (), s32[]{:S(2)}) async-start(), calls=%async_computation.6 | async-start | bytes 2621440 | tf_op jit(solution)/shard_map/all_gather | solution.py:648
  11.5 13.2 %collective-permute-start = (bf16[256,1024]{1,0:T(8,128)(2,1)}, bf16[256,1024]{1,0:T(8,128)(2,1)}, u32[]{:S(2)}, u32[]{:S(2)}) collective-permute-start(bf16[256,1024]{1,0:T(8,128)(2,1)} %pad_maximum_fusion.2), channel_id=1, source_target_pairs={{0,4},{4,0},{8,12},{12,8},{16,20},{20,16},{24,28},{28,24},{1,5},{5... | collective-permute-start | bytes 1572872 | tf_op jit(solution)/shard_map/ppermute | solution.py:396
  12.7 15.0 %collective-permute-start.1 = (bf16[256,768]{1,0:T(8,128)(2,1)}, bf16[256,768]{1,0:T(8,128)(2,1)}, u32[]{:S(2)}, u32[]{:S(2)}) collective-permute-start(bf16[256,768]{1,0:T(8,128)(2,1)} %constant_dynamic-slice_fusion.28), channel_id=1, source_target_pairs={{0,4},{4,0},{8,12},{12,8},{16,20},{20,16},{24,28},{28,24},{1,5},{5... | collective-permute-start | bytes 1179656 | tf_op jit(solution)/shard_map/ppermute | solution.py:396
  15.1 42.0 %collective-permute-start.5 = (bf16[128,2048]{1,0:T(8,128)(2,1)}, bf16[128,2048]{1,0:T(8,128)(2,1)}, u32[]{:S(2)}, u32[]{:S(2)}) collective-permute-start(bf16[128,2048]{1,0:T(8,128)(2,1)} %get-tuple-element.261), channel_id=1, source_target_pairs={{0,8},{4,12},{9,1},{13,5},{18,26},{22,30},{27,19},{31,23}} | collective-permute-start | bytes 1572872 | tf_op jit(solution)/shard_map/ppermute | solution.py:450
  20.8 36.3 %collective-permute-start.6 = (bf16[128,2048]{1,0:T(8,128)(2,1)}, bf16[128,2048]{1,0:T(8,128)(2,1)}, u32[]{:S(2)}, u32[]{:S(2)}) collective-permute-start(bf16[128,2048]{1,0:T(8,128)(2,1)} %get-tuple-element.260), channel_id=1, source_target_pairs={{0,16},{4,20},{9,25},{13,29},{18,2},{22,6},{27,11},{31,15}} | collective-permute-start | bytes 1572872 | tf_op jit(solution)/shard_map/ppermute | solution.py:450
  27.5 30.5 %collective-permute-start.3 = (bf16[512,1024]{1,0:T(8,128)(2,1)}, bf16[512,1024]{1,0:T(8,128)(2,1)}, u32[]{:S(2)}, u32[]{:S(2)}) collective-permute-start(bf16[512,1024]{1,0:T(8,128)(2,1)} %maximum_select_fusion.1.refs_0_.refs_5_.refs_6_), channel_id=1, source_target_pairs={{0,8},{4,12},{8,0},{12,4},{16,24},{20,28},{24,16},{28,20},{1,9},{5... | collective-permute-start | bytes 3145736 | tf_op jit(solution)/shard_map/ppermute | solution.py:396
  27.6 30.4 %collective-permute-start.4 = (bf16[512,1024]{1,0:T(8,128)(2,1)}, bf16[512,1024]{1,0:T(8,128)(2,1)}, u32[]{:S(2)}, u32[]{:S(2)}) collective-permute-start(bf16[512,1024]{1,0:T(8,128)(2,1)} %maximum_select_fusion.1.refs_0_.refs_5_.refs_6_), channel_id=1, source_target_pairs={{0,16},{4,20},{8,24},{12,28},{16,0},{20,4},{24,8},{28,12},{1,17},{... | collective-permute-start | bytes 3145736 | tf_op jit(solution)/shard_map/ppermute | solution.py:396
  29.1 41.2 %copy-start.24 = (bf16[512,768]{1,0:T(8,128)(2,1)}, bf16[512,768]{1,0:T(8,128)(2,1)S(1)}, u32[]{:S(2)}) copy-start(bf16[512,768]{1,0:T(8,128)(2,1)S(1)} %maximum_select_fusion.4.refs_0_.refs_1_) | copy-start | bytes 2359300
  35.4 21.3 %all-to-all-start = ((bf16[8,2,1664]{2,1,0:T(2,128)(2,1)}), bf16[8,2,1664]{2,1,0:T(2,128)(2,1)S(1)}, u32[]{:S(2)}, u32[]{:S(2)}) async-start(bf16[8,2,1664]{2,1,0:T(2,128)(2,1)} %reshape.196), calls=%async_computation | async-start | bytes 106496 | tf_op jit(solution)/shard_map/all_to_all | solution.py:687
  40.0 99.7 %all-gather.5.cloned.1.call-start = ((), (), s32[]{:S(2)}) async-start(), calls=%async_computation.7 | async-start | bytes 2621440 | tf_op jit(solution)/shard_map/all_gather | solution.py:679
  40.1 1.3 collective-permute-start.2
  40.8 233.5 %reduce-scatter.3.cloned.1.call-start = ((), (), s32[]{:S(2)}) async-start(), calls=%async_computation.8 | async-start | bytes 2621440 | tf_op jit(solution)/shard_map/reduce_scatter | solution.py:766
  61.7 41.9 %collective-permute-start.7 = (bf16[512,2048]{1,0:T(8,128)(2,1)}, bf16[512,2048]{1,0:T(8,128)(2,1)}, u32[]{:S(2)}, u32[]{:S(2)}) collective-permute-start(bf16[512,2048]{1,0:T(8,128)(2,1)} %all-gather.3.cloned.1.call-done.refs_0_.x_ref), channel_id=1, source_target_pairs={{0,4},{4,0},{8,12},{12,8},{16,20},{20,16},{24,28},{28,24},{1,5},{5... | collective-permute-start | bytes 6291464 | tf_op jit(solution)/shard_map/ppermute | solution.py:396
  61.8 18.1 %collective-permute-start.10 = (bf16[128,2048]{1,0:T(8,128)(2,1)}, bf16[128,2048]{1,0:T(8,128)(2,1)}, u32[]{:S(2)}, u32[]{:S(2)}) collective-permute-start(bf16[128,2048]{1,0:T(8,128)(2,1)} %get-tuple-element.259), channel_id=1, source_target_pairs={{0,16},{4,20},{8,24},{12,28},{9,25},{13,29},{1,17},{5,21},{18,2},{... | collective-permute-start | bytes 1572872 | tf_op jit(solution)/shard_map/ppermute | solution.py:450
  68.2 14.2 %collective-permute-start.11 = (bf16[128,2048]{1,0:T(8,128)(2,1)S(1)}, bf16[128,2048]{1,0:T(8,128)(2,1)}, u32[]{:S(2)}, u32[]{:S(2)}) collective-permute-start(bf16[128,2048]{1,0:T(8,128)(2,1)S(1)} %get-tuple-element.258), channel_id=1, source_target_pairs={{0,8},{4,12},{16,24},{20,28},{9,1},{13,5},{25,17},{29,21},{18,26},... | collective-permute-start | bytes 1572872 | tf_op jit(solution)/shard_map/ppermute | solution.py:450
  70.3 28.3 %collective-permute-start.8 = (bf16[512,768]{1,0:T(8,128)(2,1)S(1)}, bf16[512,768]{1,0:T(8,128)(2,1)S(1)}, u32[]{:S(2)}, u32[]{:S(2)}) collective-permute-start(bf16[512,768]{1,0:T(8,128)(2,1)S(1)} %maximum_select_fusion.4.refs_0_.refs_1_), channel_id=1, source_target_pairs={{0,8},{4,12},{8,0},{12,4},{16,24},{20,28},{24,16},{28,20},{1,9},{5... | collective-permute-start | bytes 2359304 | tf_op jit(solution)/shard_map/ppermute | solution.py:396
  70.3 28.3 %collective-permute-start.9 = (bf16[512,768]{1,0:T(8,128)(2,1)S(1)}, bf16[512,768]{1,0:T(8,128)(2,1)S(1)}, u32[]{:S(2)}, u32[]{:S(2)}) collective-permute-start(bf16[512,768]{1,0:T(8,128)(2,1)S(1)} %maximum_select_fusion.4.refs_0_.refs_1_), channel_id=1, source_target_pairs={{0,16},{4,20},{8,24},{12,28},{16,0},{20,4},{24,8},{28,12},{1,17},{... | collective-permute-start | bytes 2359304 | tf_op jit(solution)/shard_map/ppermute | solution.py:396
  79.9 36.6 %collective-permute-start.12 = (bf16[256,1024]{1,0:T(8,128)(2,1)}, bf16[256,1024]{1,0:T(8,128)(2,1)}, u32[]{:S(2)}, u32[]{:S(2)}) collective-permute-start(bf16[256,1024]{1,0:T(8,128)(2,1)} %slice.97), channel_id=1, source_target_pairs={{0,16},{4,20},{8,24},{12,28},{16,0},{20,4},{24,8},{28,12},{1,17},{... | collective-permute-start | bytes 1572872 | tf_op jit(solution)/shard_map/ppermute | solution.py:396
  82.4 34.1 %collective-permute-start.13 = (bf16[256,1024]{1,0:T(8,128)(2,1)}, bf16[256,1024]{1,0:T(8,128)(2,1)}, u32[]{:S(2)}, u32[]{:S(2)}) collective-permute-start(bf16[256,1024]{1,0:T(8,128)(2,1)} %slice.98), channel_id=1, source_target_pairs={{0,8},{4,12},{8,0},{12,4},{16,24},{20,28},{24,16},{28,20},{1,9},{5... | collective-permute-start | bytes 1572872 | tf_op jit(solution)/shard_map/ppermute | solution.py:396
  100.2 29.5 %collective-permute-start.14 = (bf16[256,768]{1,0:T(8,128)(2,1)}, bf16[256,768]{1,0:T(8,128)(2,1)S(1)}, u32[]{:S(2)}, u32[]{:S(2)}) collective-permute-start(bf16[256,768]{1,0:T(8,128)(2,1)} %slice.99), channel_id=1, source_target_pairs={{0,16},{4,20},{8,24},{12,28},{16,0},{20,4},{24,8},{28,12},{1,17},{... | collective-permute-start | bytes 1179656 | tf_op jit(solution)/shard_map/ppermute | solution.py:396
  100.7 28.9 %collective-permute-start.15 = (bf16[256,768]{1,0:T(8,128)(2,1)}, bf16[256,768]{1,0:T(8,128)(2,1)}, u32[]{:S(2)}, u32[]{:S(2)}) collective-permute-start(bf16[256,768]{1,0:T(8,128)(2,1)} %slice.100), channel_id=1, source_target_pairs={{0,8},{4,12},{8,0},{12,4},{16,24},{20,28},{24,16},{28,20},{1,9},{5... | collective-permute-start | bytes 1179656 | tf_op jit(solution)/shard_map/ppermute | solution.py:396
  116.4 13.2 %copy-start.6 = (bf16[1024,2048]{1,0:T(8,128)(2,1)}, bf16[1024,2048]{1,0:T(8,128)(2,1)S(1)}, u32[]{:S(2)}) copy-start(bf16[1024,2048]{1,0:T(8,128)(2,1)S(1)} %get-tuple-element.167.l_ref) | copy-start | bytes 12582916
  116.5 13.2 %copy-start.25 = (bf16[512,768]{1,0:T(8,128)(2,1)S(1)}, bf16[512,768]{1,0:T(8,128)(2,1)}, u32[]{:S(2)}) copy-start(bf16[512,768]{1,0:T(8,128)(2,1)} %copy-done.24) | copy-start | bytes 2359300
  116.5 13.2 %copy-start.28 = (bf16[512,768]{1,0:T(8,128)(2,1)S(1)}, bf16[512,768]{1,0:T(8,128)(2,1)}, u32[]{:S(2)}) copy-start(bf16[512,768]{1,0:T(8,128)(2,1)} %copy-done.27) | copy-start | bytes 2359300
  116.5 13.2 %copy-start.31 = (bf16[512,768]{1,0:T(8,128)(2,1)S(1)}, bf16[512,768]{1,0:T(8,128)(2,1)}, u32[]{:S(2)}) copy-start(bf16[512,768]{1,0:T(8,128)(2,1)} %copy-done.30) | copy-start | bytes 2359300
  139.8 26.2 %copy-start.74 = (bf16[512,2048]{1,0:T(8,128)(2,1)S(1)}, bf16[512,2048]{1,0:T(8,128)(2,1)}, u32[]{:S(2)}) copy-start(bf16[512,2048]{1,0:T(8,128)(2,1)} %all-gather.5.cloned.1.call-done) | copy-start | bytes 6291460
  139.8 26.5 %collective-permute-start.16 = (bf16[512,2048]{1,0:T(8,128)(2,1)}, bf16[512,2048]{1,0:T(8,128)(2,1)S(1)}, u32[]{:S(2)}, u32[]{:S(2)}) collective-permute-start(bf16[512,2048]{1,0:T(8,128)(2,1)} %all-gather.5.cloned.1.call-done), channel_id=1, source_target_pairs={{0,4},{4,0},{8,12},{12,8},{16,20},{20,16},{24,28},{28,24},{1,5},{5... | collective-permute-start | bytes 6291464 | tf_op jit(solution)/shard_map/ppermute | solution.py:396
  139.8 25.8 %collective-permute-start.17 = (bf16[256,2048]{1,0:T(8,128)(2,1)}, bf16[256,2048]{1,0:T(8,128)(2,1)S(1)}, u32[]{:S(2)}, u32[]{:S(2)}) collective-permute-start(bf16[256,2048]{1,0:T(8,128)(2,1)} %constant_dynamic-slice_fusion.22.refs_0_.refs_1_), channel_id=1, source_target_pairs={{0,8},{4,12},{8,0},{12,4},{16,24},{20,28},{24,16},{28,20},{1,9},{5... | collective-permute-start | bytes 3145736 | tf_op jit(solution)/shard_map/ppermute | solution.py:396
  139.9 26.0 %collective-permute-start.18 = (bf16[256,2048]{1,0:T(8,128)(2,1)}, bf16[256,2048]{1,0:T(8,128)(2,1)S(1)}, u32[]{:S(2)}, u32[]{:S(2)}) collective-permute-start(bf16[256,2048]{1,0:T(8,128)(2,1)} %constant_dynamic-slice_fusion.22.refs_0_.refs_1_), channel_id=1, source_target_pairs={{0,16},{4,20},{8,24},{12,28},{16,0},{20,4},{24,8},{28,12},{1,17},{... | collective-permute-start | bytes 3145736 | tf_op jit(solution)/shard_map/ppermute | solution.py:396
  166.5 31.8 %copy-start.2 = (bf16[1024,2048]{1,0:T(8,128)(2,1)}, bf16[1024,2048]{1,0:T(8,128)(2,1)S(1)}, u32[]{:S(2)}) copy-start(bf16[1024,2048]{1,0:T(8,128)(2,1)S(1)} %constant_dynamic-update-slice_fusion.1.r_ref.g_ref) | copy-start | bytes 12582916
  167.8 14.9 %collective-permute-start.19 = (bf16[512,512]{1,0:T(8,128)(2,1)S(1)}, bf16[512,512]{1,0:T(8,128)(2,1)S(1)}, u32[]{:S(2)}, u32[]{:S(2)}) collective-permute-start(bf16[512,512]{1,0:T(8,128)(2,1)S(1)} %get-tuple-element.158), channel_id=1, source_target_pairs={{0,8},{4,12},{8,0},{12,4},{16,24},{20,28},{24,16},{28,20},{1,9},{5... | collective-permute-start | bytes 1572872 | tf_op jit(solution)/shard_map/ppermute | solution.py:396
  169.6 14.9 %collective-permute-start.20 = (bf16[512,512]{1,0:T(8,128)(2,1)S(1)}, bf16[512,512]{1,0:T(8,128)(2,1)S(1)}, u32[]{:S(2)}, u32[]{:S(2)}) collective-permute-start(bf16[512,512]{1,0:T(8,128)(2,1)S(1)} %get-tuple-element.159), channel_id=1, source_target_pairs={{0,16},{4,20},{8,24},{12,28},{16,0},{20,4},{24,8},{28,12},{1,17},{... | collective-permute-start | bytes 1572872 | tf_op jit(solution)/shard_map/ppermute | solution.py:396
  171.3 22.8 %collective-permute-start.21 = (bf16[128,2048]{1,0:T(8,128)(2,1)S(1)}, bf16[128,2048]{1,0:T(8,128)(2,1)S(1)}, u32[]{:S(2)}, u32[]{:S(2)}) collective-permute-start(bf16[128,2048]{1,0:T(8,128)(2,1)S(1)} %slice.101), channel_id=1, source_target_pairs={{0,16},{4,20},{8,24},{12,28},{16,0},{20,4},{24,8},{28,12},{1,17},{... | collective-permute-start | bytes 1572872 | tf_op jit(solution)/shard_map/ppermute | solution.py:396
  171.7 22.5 %collective-permute-start.22 = (bf16[128,2048]{1,0:T(8,128)(2,1)S(1)}, bf16[128,2048]{1,0:T(8,128)(2,1)S(1)}, u32[]{:S(2)}, u32[]{:S(2)}) collective-permute-start(bf16[128,2048]{1,0:T(8,128)(2,1)S(1)} %slice.102), channel_id=1, source_target_pairs={{0,8},{4,12},{8,0},{12,4},{16,24},{20,28},{24,16},{28,20},{1,9},{5... | collective-permute-start | bytes 1572872 | tf_op jit(solution)/shard_map/ppermute | solution.py:396
  198.2 7.9 %collective-permute-start.23 = (bf16[512,2048]{1,0:T(8,128)(2,1)S(1)}, bf16[512,2048]{1,0:T(8,128)(2,1)S(1)}, u32[]{:S(2)}, u32[]{:S(2)}) collective-permute-start(bf16[512,2048]{1,0:T(8,128)(2,1)S(1)} %branch_rows.2), channel_id=1, source_target_pairs={{0,4},{4,0},{8,12},{12,8},{16,20},{20,16},{24,28},{28,24},{1,5},{5... | collective-permute-start | bytes 6291464 | tf_op jit(solution)/shard_map/ppermute | solution.py:396
  211.5 89.7 %reduce-scatter.5.cloned.1.call-start = ((), (), s32[]{:S(2)}) async-start(), calls=%async_computation.9 | async-start | bytes 2621440 | tf_op jit(solution)/shard_map/reduce_scatter | solution.py:766
  219.7 13.8 %copy-start.3 = (bf16[1024,2048]{1,0:T(8,128)(2,1)S(1)}, bf16[1024,2048]{1,0:T(8,128)(2,1)}, u32[]{:S(2)}) copy-start(bf16[1024,2048]{1,0:T(8,128)(2,1)} %copy-done.2) | copy-start | bytes 12582916
  227.4 8.5 %collective-permute-start.28 = (bf16[512,2048]{1,0:T(8,128)(2,1)S(1)}, bf16[512,2048]{1,0:T(8,128)(2,1)S(1)}, u32[]{:S(2)}, u32[]{:S(2)}) collective-permute-start(bf16[512,2048]{1,0:T(8,128)(2,1)S(1)} %get-tuple-element.183), channel_id=1, source_target_pairs={{0,4},{4,0},{8,12},{12,8},{16,20},{20,16},{24,28},{28,24},{1,5},{5... | collective-permute-start | bytes 6291464 | tf_op jit(solution)/shard_map/ppermute | solution.py:396
  228.0 5.5 %collective-permute-start.26 = (bf16[128,512]{1,0:T(8,128)(2,1)S(1)}, bf16[128,512]{1,0:T(8,128)(2,1)S(1)}, u32[]{:S(2)}, u32[]{:S(2)}) collective-permute-start(bf16[128,512]{1,0:T(8,128)(2,1)S(1)} %get-tuple-element.162), channel_id=1, source_target_pairs={{0,8},{4,12},{8,0},{12,4},{16,24},{20,28},{24,16},{28,20},{1,9},{5... | collective-permute-start | bytes 393224 | tf_op jit(solution)/shard_map/ppermute | solution.py:396
  228.2 5.3 %collective-permute-start.27 = (bf16[128,512]{1,0:T(8,128)(2,1)S(1)}, bf16[128,512]{1,0:T(8,128)(2,1)S(1)}, u32[]{:S(2)}, u32[]{:S(2)}) collective-permute-start(bf16[128,512]{1,0:T(8,128)(2,1)S(1)} %get-tuple-element.163), channel_id=1, source_target_pairs={{0,16},{4,20},{8,24},{12,28},{16,0},{20,4},{24,8},{28,12},{1,17},{... | collective-permute-start | bytes 393224 | tf_op jit(solution)/shard_map/ppermute | solution.py:396
  245.6 16.6 %collective-permute-start.24 = (bf16[256,1024]{1,0:T(8,128)(2,1)}, bf16[256,1024]{1,0:T(8,128)(2,1)S(1)}, u32[]{:S(2)}, u32[]{:S(2)}) collective-permute-start(bf16[256,1024]{1,0:T(8,128)(2,1)} %copy-done.69), channel_id=1, source_target_pairs={{0,8},{4,12},{8,0},{12,4},{16,24},{20,28},{24,16},{28,20},{1,9},{5... | collective-permute-start | bytes 1572872 | tf_op jit(solution)/shard_map/ppermute | solution.py:396
  247.2 17.2 %collective-permute-start.25 = (bf16[256,1024]{1,0:T(8,128)(2,1)}, bf16[256,1024]{1,0:T(8,128)(2,1)}, u32[]{:S(2)}, u32[]{:S(2)}) collective-permute-start(bf16[256,1024]{1,0:T(8,128)(2,1)} %copy-done.68), channel_id=1, source_target_pairs={{0,16},{4,20},{8,24},{12,28},{16,0},{20,4},{24,8},{28,12},{1,17},{... | collective-permute-start | bytes 1572872 | tf_op jit(solution)/shard_map/ppermute | solution.py:396
  250.5 26.0 %collective-permute-start.29 = (bf16[256,768]{1,0:T(8,128)(2,1)}, bf16[256,768]{1,0:T(8,128)(2,1)S(1)}, u32[]{:S(2)}, u32[]{:S(2)}) collective-permute-start(bf16[256,768]{1,0:T(8,128)(2,1)} %copy-done.71), channel_id=1, source_target_pairs={{0,8},{4,12},{8,0},{12,4},{16,24},{20,28},{24,16},{28,20},{1,9},{5... | collective-permute-start | bytes 1179656 | tf_op jit(solution)/shard_map/ppermute | solution.py:396
  251.0 27.1 %collective-permute-start.30 = (bf16[256,768]{1,0:T(8,128)(2,1)}, bf16[256,768]{1,0:T(8,128)(2,1)}, u32[]{:S(2)}, u32[]{:S(2)}) collective-permute-start(bf16[256,768]{1,0:T(8,128)(2,1)} %copy-done.70), channel_id=1, source_target_pairs={{0,16},{4,20},{8,24},{12,28},{16,0},{20,4},{24,8},{28,12},{1,17},{... | collective-permute-start | bytes 1179656 | tf_op jit(solution)/shard_map/ppermute | solution.py:396
  255.8 48.9 %collective-permute-start.37 = (bf16[1024,512]{1,0:T(8,128)(2,1)}, bf16[1024,512]{1,0:T(8,128)(2,1)}, u32[]{:S(2)}, u32[]{:S(2)}) collective-permute-start(bf16[1024,512]{1,0:T(8,128)(2,1)} %copy-done.55), channel_id=1, source_target_pairs={{0,8},{4,12},{8,0},{12,4},{16,24},{20,28},{24,16},{28,20},{1,9},{5... | collective-permute-start | bytes 3145736 | tf_op jit(solution)/shard_map/ppermute | solution.py:396
  263.0 48.2 %collective-permute-start.38 = (bf16[1024,512]{1,0:T(8,128)(2,1)}, bf16[1024,512]{1,0:T(8,128)(2,1)}, u32[]{:S(2)}, u32[]{:S(2)}) collective-permute-start(bf16[1024,512]{1,0:T(8,128)(2,1)} %copy-done.54), channel_id=1, source_target_pairs={{0,16},{4,20},{8,24},{12,28},{16,0},{20,4},{24,8},{28,12},{1,17},{... | collective-permute-start | bytes 3145736 | tf_op jit(solution)/shard_map/ppermute | solution.py:396
  264.4 53.0 %collective-permute-start.35 = (bf16[256,512]{1,0:T(8,128)(2,1)}, bf16[256,512]{1,0:T(8,128)(2,1)}, u32[]{:S(2)}, u32[]{:S(2)}) collective-permute-start(bf16[256,512]{1,0:T(8,128)(2,1)} %copy-done.65), channel_id=1, source_target_pairs={{0,8},{4,12},{8,0},{12,4},{16,24},{20,28},{24,16},{28,20},{1,9},{5... | collective-permute-start | bytes 786440 | tf_op jit(solution)/shard_map/ppermute | solution.py:396
  276.5 45.7 %collective-permute-start.33 = (bf16[512,1024]{1,0:T(8,128)(2,1)}, bf16[512,1024]{1,0:T(8,128)(2,1)}, u32[]{:S(2)}, u32[]{:S(2)}) collective-permute-start(bf16[512,1024]{1,0:T(8,128)(2,1)} %weight_grad.24), channel_id=1, source_target_pairs={{0,8},{4,12},{8,0},{12,4},{16,24},{20,28},{24,16},{28,20},{1,9},{5... | collective-permute-start | bytes 3145736 | tf_op jit(solution)/shard_map/ppermute | solution.py:396
  278.1 44.1 %collective-permute-start.34 = (bf16[512,1024]{1,0:T(8,128)(2,1)}, bf16[512,1024]{1,0:T(8,128)(2,1)}, u32[]{:S(2)}, u32[]{:S(2)}) collective-permute-start(bf16[512,1024]{1,0:T(8,128)(2,1)} %weight_grad.25), channel_id=1, source_target_pairs={{0,16},{4,20},{8,24},{12,28},{16,0},{20,4},{24,8},{28,12},{1,17},{... | collective-permute-start | bytes 3145736 | tf_op jit(solution)/shard_map/ppermute | solution.py:396
  283.9 17.3 %copy-start.83 = (f32[128]{0:T(128)S(1)}, f32[128]{0:T(128)}, u32[]{:S(2)}) copy-start(f32[128]{0:T(128)} %copy-done.82) | copy-start | bytes 1540
  283.9 17.3 %copy-start.84 = (f32[128]{0:T(128)S(1)}, f32[128]{0:T(128)}, u32[]{:S(2)}) copy-start(f32[128]{0:T(128)} %add_rsqrt_fusion) | copy-start | bytes 1540
  304.7 15.3 %collective-permute-start.36 = (bf16[256,512]{1,0:T(8,128)(2,1)S(1)}, bf16[256,512]{1,0:T(8,128)(2,1)S(1)}, u32[]{:S(2)}, u32[]{:S(2)}) collective-permute-start(bf16[256,512]{1,0:T(8,128)(2,1)S(1)} %copy-done.64), channel_id=1, source_target_pairs={{0,16},{4,20},{8,24},{12,28},{16,0},{20,4},{24,8},{28,12},{1,17},{... | collective-permute-start | bytes 786440 | tf_op jit(solution)/shard_map/ppermute | solution.py:396
  308.1 18.1 %all-to-all-start.1 = ((f32[32,1,768]{2,1,0:T(1,128)}), f32[32,1,768]{2,1,0:T(1,128)S(1)}, u32[]{:S(2)}, u32[]{:S(2)}) async-start(f32[32,1,768]{2,1,0:T(1,128)} %copy.43), calls=%async_computation.3 | async-start | bytes 196608 | tf_op jit(solution)/shard_map/all_to_all | solution.py:821
  326.2 35.8 %copy-start.22 = (bf16[2,512,768]{2,1,0:T(8,128)(2,1)S(1)}, bf16[2,512,768]{2,1,0:T(8,128)(2,1)}, u32[]{:S(2)}) copy-start(bf16[2,512,768]{2,1,0:T(8,128)(2,1)} %copy-done.19) | copy-start | bytes 4718596
  326.2 29.5 %all-to-all-start.2 = ((bf16[512,4,256]{2,0,1:T(8,128)(2,1)}), bf16[512,4,256]{2,0,1:T(8,128)(2,1)}, u32[]{:S(2)}, u32[]{:S(2)}) async-start(bf16[512,4,256]{2,0,1:T(8,128)(2,1)} %bitcast.40), calls=%async_computation.4 | async-start | bytes 2097152 | tf_op jit(solution)/shard_map/all_to_all | solution.py:832
  331.2 29.1 %collective-permute-start.31 = (bf16[512,768]{1,0:T(8,128)(2,1)}, bf16[512,768]{1,0:T(8,128)(2,1)S(1)}, u32[]{:S(2)}, u32[]{:S(2)}) collective-permute-start(bf16[512,768]{1,0:T(8,128)(2,1)} %weight_grad.26), channel_id=1, source_target_pairs={{0,8},{4,12},{8,0},{12,4},{16,24},{20,28},{24,16},{28,20},{1,9},{5... | collective-permute-start | bytes 2359304 | tf_op jit(solution)/shard_map/ppermute | solution.py:396
  332.6 28.5 %collective-permute-start.32 = (bf16[512,768]{1,0:T(8,128)(2,1)}, bf16[512,768]{1,0:T(8,128)(2,1)S(1)}, u32[]{:S(2)}, u32[]{:S(2)}) collective-permute-start(bf16[512,768]{1,0:T(8,128)(2,1)} %copy-done.60), channel_id=1, source_target_pairs={{0,16},{4,20},{8,24},{12,28},{16,0},{20,4},{24,8},{28,12},{1,17},{... | collective-permute-start | bytes 2359304 | tf_op jit(solution)/shard_map/ppermute | solution.py:396
  355.7 30.4 %all-to-all-start.3 = ((bf16[4,256,512]{2,1,0:T(8,128)(2,1)}), bf16[4,256,512]{2,1,0:T(8,128)(2,1)}, u32[]{:S(2)}, u32[]{:S(2)}) async-start(bf16[4,256,512]{2,1,0:T(8,128)(2,1)} %bitcast.14), calls=%async_computation.5 | async-start | bytes 2097152 | tf_op jit(solution)/shard_map/all_to_all | solution.py:832
  368.8 19.6 %collective-permute-start.39 = (f32[256,768]{1,0:T(8,128)}, f32[256,768]{1,0:T(8,128)S(1)}, u32[]{:S(2)}, u32[]{:S(2)}) collective-permute-start(f32[256,768]{1,0:T(8,128)} %get-tuple-element.249), channel_id=1, source_target_pairs={{0,4},{4,0},{8,12},{12,8},{16,20},{20,16},{24,28},{28,24},{1,5},{5... | collective-permute-start | bytes 2359304 | tf_op jit(solution)/shard_map/ppermute | solution.py:396
  368.8 4.1 %collective-permute-start.40 = (f32[256,256]{1,0:T(8,128)S(1)}, f32[256,256]{1,0:T(8,128)}, u32[]{:S(2)}, u32[]{:S(2)}) collective-permute-start(f32[256,256]{1,0:T(8,128)S(1)} %get-tuple-element.263), channel_id=1, source_target_pairs={{0,4},{4,0},{8,12},{12,8},{16,20},{20,16},{24,28},{28,24},{1,5},{5... | collective-permute-start | bytes 786440 | tf_op jit(solution)/shard_map/ppermute | solution.py:396
  371.3 27.3 %copy-start.93 = (f32[64]{0:T(128)}, f32[64]{0:T(128)S(1)}, u32[]{:S(2)}) copy-start(f32[64]{0:T(128)S(1)} %get-tuple-element.316) | copy-start | bytes 772
  372.8 15.5 %copy-start.73 = (f32[256,768]{1,0:T(8,128)S(1)}, f32[256,768]{1,0:T(8,128)}, u32[]{:S(2)}) copy-start(f32[256,768]{1,0:T(8,128)} %get-tuple-element.248) | copy-start | bytes 2359300
  372.9 16.8 %collective-permute-start.41 = (bf16[256,1024]{0,1:T(8,128)(2,1)S(1)}, bf16[256,1024]{0,1:T(8,128)(2,1)}, u32[]{:S(2)}, u32[]{:S(2)}) collective-permute-start(bf16[256,1024]{0,1:T(8,128)(2,1)S(1)} %get-tuple-element.253), channel_id=1, source_target_pairs={{0,4},{4,0},{8,12},{12,8},{16,20},{20,16},{24,28},{28,24},{1,5},{5... | collective-permute-start | bytes 1572872 | tf_op jit(solution)/shard_map/ppermute | solution.py:396
  388.3 7.1 %collective-permute-start.42 = (bf16[1024,256]{1,0:T(8,128)(2,1)}, bf16[1024,256]{1,0:T(8,128)(2,1)}, u32[]{:S(2)}, u32[]{:S(2)}) collective-permute-start(bf16[1024,256]{1,0:T(8,128)(2,1)} %get-tuple-element.251), channel_id=1, source_target_pairs={{0,4},{4,0},{8,12},{12,8},{16,20},{20,16},{24,28},{28,24},{1,5},{5... | collective-permute-start | bytes 1572872 | tf_op jit(solution)/shard_map/ppermute | solution.py:396
  (82 other events, 335.6 us)
Sparse Core Ops, SparseCore 0:
  10.2 48.6 all-gather.2
  60.4 44.6 all-gather.4
  211.6 44.1 reduce-scatter.2
  258.0 43.1 reduce-scatter.4

commit v3 on v2

v3 whole, which is shorter than its diff:
```python
import jax
import jax.numpy as jnp
import numpy as np
from jax import lax
from jax.experimental import pallas as pl
from jax.experimental.pallas import tpu as pltpu
from jax.sharding import PartitionSpec as P

H = 8
HS = 256
ROT = 64
HINT = 1.0
LIMIT = 16 * 1024 * 1024
F32 = jnp.float32
BF16 = jnp.bfloat16


def matmul(left, right):
    return jnp.dot(left, right, preferred_element_type=F32)


def times_transposed(left, right):
    return lax.dot_general(left, right, (((1,), (1,)), ((), ())), preferred_element_type=F32)


def left_transposed(left, right):
    return lax.dot_general(left, right, (((0,), (0,)), ((), ())), preferred_element_type=F32)


def cost(flops, reads, writes, transcendentals=0):
    return pl.CostEstimate(
        flops=int(flops * HINT),
        bytes_accessed=int((reads + writes) * HINT),
        transcendentals=int(transcendentals * HINT),
    )


VMEM = pl.BlockSpec(memory_space=pltpu.VMEM)
SMEM = pl.BlockSpec(memory_space=pltpu.SMEM)


def on_chip(body, name, arrays, shapes, estimate, scalars=()):
    return pl.pallas_call(
        body,
        in_specs=[SMEM] * len(scalars) + [VMEM] * len(arrays),
        out_specs=[VMEM] * len(shapes),
        out_shape=[jax.ShapeDtypeStruct(*shape) for shape in shapes],
        compiler_params=pltpu.CompilerParams(vmem_limit_bytes=LIMIT),
        cost_estimate=estimate,
        name=name,
    )(*scalars, *arrays)


def each(total, size, step):
    if total <= size:
        return step(0)

    @pl.loop(0, total // size)
    def _(i):
        step(pl.multiple_of(i * size, size))


def chunks(total, size):
    return [(at, min(size, total - at)) for at in range(0, total, size)]


def two_norms(arrays, scales, blocks):
    rows, width = arrays[0].shape
    total = rows * len(arrays)
    tile = 32

    size = width // blocks

    def body(scales_ref, *refs):
        ones, twos, stats_ref = refs[len(arrays) : -1 - blocks], refs[-1 - blocks : -1], refs[-1]
        for k in range(len(arrays)):

            @pl.loop(0, rows // tile)
            def _(i, k=k):
                values = refs[k][pl.ds(pl.multiple_of(i * tile, tile), tile), :].astype(F32)
                average = jnp.mean(values, axis=-1, keepdims=True)
                centred = values - average
                variance = jnp.mean(centred * centred, axis=-1, keepdims=True)
                inverse = lax.rsqrt(variance + 1e-05)
                xhat = centred * inverse
                span = pl.ds(pl.multiple_of(k * rows + i * tile, tile), tile)
                one = (xhat * scales_ref[0:1, :] + scales_ref[1:2, :]).astype(BF16)
                two = (xhat * scales_ref[2:3, :] + scales_ref[3:4, :]).astype(BF16)
                for n in range(blocks):
                    ones[n][span, :] = one[:, n * size : (n + 1) * size]
                    twos[n][span, :] = two[:, n * size : (n + 1) * size]
                stats_ref[span, :] = jnp.concatenate([average, inverse], axis=1)

    return on_chip(
        body,
        "two_norms",
        [scales, *arrays],
        [((total, size), BF16)] * (2 * blocks) + [((total, 2), F32)],
        cost(total * width * 24, total * width * 2, total * width * 4),
    )


class Pieces:
    def __init__(self, arrays, tiles, size, blocks=None, columns=None):
        self.arrays, self.tiles, self.size, self.blocks = arrays, tiles, size, blocks
        self.first, self.width = columns or (0, arrays[0].shape[1])

    def inside(self, size):
        cut = []
        for which, first, count, k, place in self.runs():
            start = k * self.size + place
            while count:
                take = min(count, size - start % size)
                cut.append((which, first, take, start // size, start % size))
                first, start, count = first + take, start + take, count - take
        return cut

    def runs(self):
        found = []
        for k, tile in enumerate(self.tiles):
            at = 0
            for which, first, count in tile:
                last = found[-1] if found else None
                joins = last and self.blocks is None and last[0] == which and last[1] + last[2] == first
                if joins:
                    found[-1] = (which, last[1], last[2] + count, last[3], last[4])
                else:
                    found.append((which, first, count, k, at))
                at += count
        return found


def feed_up(x, pieces, b):
    rows, size = x[0].shape
    width = size * len(x)
    units = pieces.width

    def body(b_ref, *refs):
        x_refs, w_refs, (act_ref, slope_ref) = refs[: len(x)], refs[len(x) : -2], refs[-2:]
        def step(row):
            for col, cols in chunks(units, 512):
                at = (pl.ds(row, min(256, rows)), pl.ds(col, cols))
                hidden = b_ref[:, at[1]]
                for which, first, depth, k, place in pieces.inside(size):
                    hidden = hidden + matmul(
                        x_refs[k][at[0], place : place + depth],
                        w_refs[which][first : first + depth, pl.ds(pieces.first + col, cols)],
                    )
                cdf = 0.5 + 0.5 * lax.erf(hidden * (0.5**0.5))
                act_ref[at] = (hidden * cdf).astype(BF16)
                slope_ref[at] = cdf + hidden * (jnp.exp(-0.5 * hidden * hidden) * 0.3989422804014327)

        each(rows, 256, step)

    return on_chip(
        body,
        "feed_up",
        [b, *x, *pieces.arrays],
        [((rows, units), BF16), ((rows, units), F32)],
        cost(4 * rows * width * units, 2 * (rows + units) * width, 6 * rows * units, 2 * rows * units),
    )


def cotangent_blocks(streams, at, blocks):
    rows, width = streams[0].shape
    size = width // blocks

    def body(at_ref, *refs):
        ins, outs = refs[: len(streams)], refs[len(streams) :]
        for off in range(blocks):
            place = pl.ds(pl.multiple_of((at_ref[2] ^ off) * size, 128), size)
            for n in range(len(streams)):
                outs[off][n * rows : (n + 1) * rows, :] = ins[n][:, place]

    return on_chip(
        body,
        "cotangent_blocks",
        streams,
        [((rows * len(streams), size), BF16)] * blocks,
        cost(0, rows * width * 4, rows * width * 4),
        [at],
    )


def hidden_grad(g, pieces, slope, at):
    rows, size = g[0].shape
    width = size * len(g)
    units = slope.shape[1]

    def body(blocks_ref, at_ref, slope_ref, *refs):
        g_refs, w_refs, (out_ref, sum_ref) = refs[: len(g)], refs[len(g) : -2], refs[-2:]
        for which, first, count, k, place in pieces.runs():
            columns = pl.ds(pl.multiple_of(blocks_ref[k] * pieces.size + place, 128), count)
            total = jnp.zeros((1, count), F32)
            for row, tall in chunks(rows, 256):
                span = pl.ds(row, tall)
                value = jnp.zeros((tall, count), F32)
                for off in range(len(g)):
                    block = pl.ds(pl.multiple_of((at_ref[2] ^ off) * size, 128), size)
                    value = value + times_transposed(
                        g_refs[off][span, :], w_refs[which][first : first + count, block]
                    )
                value = (value * slope_ref[span, columns]).astype(BF16)
                out_ref[span, columns] = value
                total = total + jnp.sum(value.astype(F32), axis=0, keepdims=True)
            sum_ref[:, columns] = total

    return on_chip(
        body,
        "hidden_grad",
        [slope, *g, *pieces.arrays],
        [((rows, units), BF16), ((1, units), F32)],
        cost(4 * rows * width * units, 2 * (rows + units) * width + 4 * rows * units, 2 * rows * units),
        [pieces.blocks, at],
    )


def turn(values, cosine, before, after, sign):
    lanes = cosine.shape[1]
    half = ROT // 2
    first = values[:, :lanes]
    first = first * cosine + sign * (
        pltpu.roll(first, lanes - half, 1) * before + pltpu.roll(first, half, 1) * after
    )
    return jnp.concatenate([first, values[:, lanes:]], axis=1)


def attention_forward(x, pieces, bias, tables, begins):
    count, size = tables[0].shape[:2]
    part = x[0].shape[1]
    width = part * len(x)
    columns = bias.shape[1]

    def body(b_ref, cos_ref, before_ref, after_ref, begin_ref, *refs):
        x_refs, w_refs, (qkv_ref, probs_ref, out_ref) = refs[: len(x)], refs[len(x) : -3], refs[-3:]
        @pl.loop(0, count)
        def _(n):
            turns = (cos_ref[n], before_ref[n], after_ref[n])
            projected = b_ref[...]
            for which, first, rows, k, place in pieces.inside(part):
                projected = projected + matmul(
                    x_refs[k][pl.ds(pl.multiple_of(n * size, size), size), place : place + rows],
                    w_refs[which][first : first + rows, pl.ds(pieces.first, columns)],
                )
            queries = turn(projected[:, :HS], *turns, 1.0).astype(BF16)
            keys = turn(projected[:, HS : 2 * HS], *turns, 1.0).astype(BF16)
            values = projected[:, 2 * HS :].astype(BF16)
            qkv_ref[n, :, :HS] = queries
            qkv_ref[n, :, HS : 2 * HS] = keys
            qkv_ref[n, :, 2 * HS :] = values
            for row, tile in chunks(size, 256):
                rows = slice(row, row + tile)
                scores = times_transposed(queries[rows], keys) * (HS**-0.5)
                places = lax.broadcasted_iota(jnp.int32, (tile, size), 1)
                here = lax.broadcasted_iota(jnp.int32, (tile, size), 0) + row
                allowed = (places >= begin_ref[n, rows, :]) & (places <= here)
                masked = jnp.where(allowed, scores, -1e30)
                exponent = jnp.exp(masked - jnp.max(masked, axis=-1, keepdims=True))
                probs = exponent / jnp.sum(exponent, axis=-1, keepdims=True)
                probs_ref[n, rows, :] = probs
                out_ref[n, rows, :] = matmul(probs.astype(BF16), values).astype(BF16)

    return on_chip(
        body,
        "attention_forward",
        [bias, *tables, begins, *x, *pieces.arrays],
        [
            ((count, size, columns), BF16),
            ((count, size, size), F32),
            ((count, size, HS), BF16),
        ],
        cost(
            count * size * (size * HS * 8 + 4 * width * columns),
            count * size * width * 2,
            count * size * (columns * 2 + size * 4),
            count * size * size,
        ),
    )


def attention_backward(qkv, probs, g, w_dense, tables, at):
    count, size, columns = qkv.shape
    scale = HS**-0.5
    part = g[0].shape[1]

    def body(at_ref, qkv_ref, probs_ref, w_ref, cos_ref, before_ref, after_ref, *refs):
        g_refs, (out_ref, sum_ref) = refs[:-2], refs[-2:]
        sum_ref[...] = jnp.zeros((1, columns), F32)

        @pl.loop(0, count)
        def _(n):
            turns = (cos_ref[n], before_ref[n], after_ref[n])
            queries = qkv_ref[n, :, :HS]
            keys = qkv_ref[n, :, HS : 2 * HS]
            values = qkv_ref[n, :, 2 * HS :]
            grad = jnp.zeros((size, HS), F32)
            for off in range(len(g)):
                block = pl.ds(pl.multiple_of((at_ref[2] ^ off) * part, 128), part)
                grad = grad + times_transposed(g_refs[off][pl.ds(pl.multiple_of(n * size, size), size), :], w_ref[:, block])
            grad = grad.astype(BF16)
            probs_now = probs_ref[n]
            grad_probs = times_transposed(grad, values)
            inner = jnp.sum(probs_now * grad_probs, axis=-1, keepdims=True)
            grad_scores = (probs_now * (grad_probs - inner)).astype(BF16)
            grad_queries = turn(matmul(grad_scores, keys) * scale, *turns, -1.0).astype(BF16)
            grad_keys = turn(left_transposed(grad_scores, queries) * scale, *turns, -1.0).astype(BF16)
            grad_values = left_transposed(probs_now.astype(BF16), grad).astype(BF16)
            whole = jnp.concatenate([grad_queries, grad_keys, grad_values], axis=1)
            out_ref[n] = whole
            sum_ref[...] += jnp.sum(whole.astype(F32), axis=0, keepdims=True)

    return on_chip(
        body,
        "attention_backward",
        [qkv, probs, w_dense, *tables, *g],
        [((count, size, columns), BF16), ((1, columns), F32)],
        cost(
            count * size * (size * HS * 16 + 4 * HS * part * len(g)),
            count * size * (columns * 4 + size * 4),
            count * size * columns * 2,
        ),
        [at],
    )


def branch_rows_of(attended, w_dense, activated, pieces, first, count, extra=None):
    width = w_dense.shape[1]
    inner, units = attended.shape[1], activated.shape[1]
    arrays = [attended, w_dense, activated] + ([] if extra is None else [extra])

    def body(blocks_ref, a_ref, wa_ref, b_ref, *refs):
        if extra is not None:
            extra_ref, *refs = refs
        for row, rows in chunks(count, 256):
            span = pl.ds(first * count + row, rows)
            for col, cols in chunks(width, 512):
                at = pl.ds(col, cols)
                value = matmul(a_ref[span, :], wa_ref[:, at])
                for which, start, depth, k, place in pieces.runs():
                    columns = pl.ds(pl.multiple_of(blocks_ref[k] * pieces.size + place, 128), depth)
                    value = value + matmul(b_ref[span, columns], refs[which][start : start + depth, at])
                if extra is not None:
                    value = value + extra_ref[pl.ds(row, rows), at].astype(F32)
                refs[-1][pl.ds(row, rows), at] = value.astype(BF16)

    return on_chip(
        body,
        "branch_rows",
        arrays + pieces.arrays,
        [((count, width), BF16)],
        cost(4 * count * (inner + units) * width, 2 * (inner + units) * (width + count), 2 * count * width),
        [pieces.blocks],
    )[0]


def input_terms(grad_proj, qkv_pieces, grad_hid, up_pieces, x, stats, scales, first, extra=None):
    count, width = x.shape
    tile = up_pieces.size
    columns, units = grad_proj.shape[1], grad_hid.shape[1]
    weights = up_pieces.arrays
    arrays = [grad_proj, grad_hid, x, stats, scales] + ([] if extra is None else [extra])

    def body(gp_ref, gh_ref, x_ref, stats_ref, scales_ref, *refs):
        if extra is not None:
            extra_ref, *refs = refs
        out_ref, sums_ref = refs[-2:]
        for k, up_tile in enumerate(up_pieces.tiles):
            ((which, start, _),) = up_tile
            wq = refs[which][start : start + tile, pl.ds(qkv_pieces.first, columns)]
            wu = refs[which][start : start + tile, pl.ds(up_pieces.first, units)]
            at = pl.ds(k * tile, tile)
            sums = [jnp.zeros((1, tile), F32)] * 4
            for row, rows in chunks(count, 256):
                span = pl.ds(row, rows)
                there = pl.ds(first * count + row, rows)
                one = times_transposed(gp_ref[there, :], wq)
                two = times_transposed(gh_ref[there, :], wu)
                xhat = (x_ref[span, at].astype(F32) - stats_ref[there, 0:1]) * stats_ref[there, 1:2]
                value = one * scales_ref[0:1, at] + two * scales_ref[2:3, at]
                if extra is not None:
                    value = value + extra_ref[span, at].astype(F32)
                out_ref[span, at] = value.astype(BF16)
                for n, term in enumerate((one * xhat, one, two * xhat, two)):
                    sums[n] = sums[n] + jnp.sum(term, axis=0, keepdims=True)
            sums_ref[:, at] = jnp.concatenate(sums, axis=0)

    return on_chip(
        body,
        "input_terms",
        arrays + weights,
        [((count, width), BF16), ((4, width), F32)],
        cost(
            4 * count * (columns + units) * width,
            2 * (columns + units) * (width + count) + 2 * count * width,
            2 * count * width,
        ),
    )


def weight_grad(left, right, extras=(), halves=False, kind=BF16):
    depth, rows = left.shape
    cols = right.shape[1]

    def body(l_ref, r_ref, *refs):
        extra_refs, outs = refs[: len(extras)], refs[len(extras) :]
        for row, size in chunks(rows, min(256, rows // 2)):
            value = left_transposed(l_ref[:, pl.ds(row, size)], r_ref[...])
            for ref, (array, first) in zip(extra_refs, extras):
                if first <= row < first + array.shape[0]:
                    value = value + ref[pl.ds(row - first, size), :].astype(F32)
            if halves:
                half = rows // 2
                outs[row // half][pl.ds(row % half, size), :] = value.astype(kind)
            else:
                outs[0][pl.ds(row, size), :] = value.astype(kind)

    shapes = [((rows // 2, cols), kind)] * 2 if halves else [((rows, cols), kind)]
    found = on_chip(
        body,
        "weight_grad",
        [left, right, *[e[0] for e in extras]],
        shapes,
        cost(4 * depth * rows * cols, 2 * depth * (rows + cols), rows * cols * 2),
    )
    return found if halves else found[0]


ANY = pl.BlockSpec(memory_space=pl.ANY)


def copies(name, scalars, arrays, shapes, moves):
    def body(at_ref, *refs):
        ins, outs, sems = refs[: len(arrays)], refs[len(arrays) : -1], refs[-1]
        jobs = [
            pltpu.make_async_copy(source, target, sems.at[n])
            for n, (source, target) in enumerate(moves(at_ref, ins, outs))
        ]
        for job in jobs:
            job.start()
        for job in jobs:
            job.wait()

    return pl.pallas_call(
        body,
        in_specs=[SMEM] + [ANY] * len(arrays),
        out_specs=[VMEM] * len(shapes),
        out_shape=[jax.ShapeDtypeStruct(shape, BF16) for shape in shapes],
        scratch_shapes=[pltpu.SemaphoreType.DMA((24,))],
        compiler_params=pltpu.CompilerParams(vmem_limit_bytes=48 * 1024 * 1024),
        cost_estimate=cost(0, 2 * sum(int(np.prod(shape)) for shape in shapes), 0),
        name=name,
    )(scalars, *arrays)


def rotary_tables(lengths, size):
    lanes, half = 128, ROT // 2
    power = -(np.arange(half, dtype=np.float32) * np.float32(2.0 / ROT))
    inverse = np.zeros((1, lanes), np.float32)
    inverse[0, :half] = inverse[0, half:ROT] = np.float32(10000.0) ** power
    count = len(lengths)

    def body(*refs):
        inverse_ref, cos_ref, before_ref, after_ref, begin_ref = refs[count:]
        for n in range(count):
            row = lax.broadcasted_iota(jnp.int32, (size, 1), 0)
            begin = jnp.zeros((size, 1), jnp.int32)
            start = jnp.int32(0)
            for k in range(lengths[n].shape[1]):
                begin = jnp.where(row >= start, start, begin)
                start = start + refs[n][0, k]
            angle = (row - begin).astype(F32) * inverse_ref[...]
            sine = jnp.sin(angle)
            lane = lax.broadcasted_iota(jnp.int32, (size, lanes), 1)
            cos_ref[n] = jnp.cos(angle)
            before_ref[n] = jnp.where(lane < half, -sine, 0.0)
            after_ref[n] = jnp.where((lane >= half) & (lane < ROT), sine, 0.0)
            begin_ref[n] = begin

    table = ((count, size, lanes), F32)
    *tables, begins = on_chip(
        body,
        "rotary_tables",
        [jnp.asarray(inverse)],
        [table, table, table, ((count, size, 1), jnp.int32)],
        cost(0, 0, 12 * count * size * lanes),
        lengths,
    )
    return tuple(tables), begins


def small_params(packed, at, spans, blocks, slice_rows):
    rows = packed.shape[0]
    first = np.cumsum([0] + spans)
    width = spans[2] * rows

    def body(at_ref, p_ref, qkv_ref, up_ref, out_ref, scales_ref, table):
        z, part, block = at_ref[0], at_ref[1], at_ref[2]
        table[...] = p_ref[...].astype(F32)
        qkv_ref[...] = table[pl.ds(2 * z + part, 1), : spans[0]]
        for k in range(blocks):
            columns = pl.ds(pl.multiple_of(first[1] + z * slice_rows, 128), slice_rows)
            up_ref[:, k * slice_rows : (k + 1) * slice_rows] = table[pl.ds(2 * k + part, 1), columns]
        each = spans[2]
        for i in range(rows):
            out_ref[:, i * each : (i + 1) * each] = (
                table[i : i + 1, first[2] : first[3]] + table[i : i + 1, first[3] : first[4]]
            )
        for off in range(blocks):
            for c in range(2):
                row = pl.ds(2 * (block ^ off) + c, 1)
                place = (off * 2 + c) * each
                for k in range(4):
                    scales_ref[k : k + 1, place : place + each] = table[row, first[4 + k] : first[5 + k]]

    return pl.pallas_call(
        body,
        in_specs=[SMEM, VMEM],
        out_specs=[VMEM] * 4,
        out_shape=[
            jax.ShapeDtypeStruct(shape, F32)
            for shape in ((1, spans[0]), (1, blocks * slice_rows), (1, width), (4, width))
        ],
        scratch_shapes=[pltpu.VMEM(packed.shape, F32)],
        compiler_params=pltpu.CompilerParams(vmem_limit_bytes=4 * 1024 * 1024),
        cost_estimate=cost(0, 0, 0),
        name="small_params",
    )(at, packed)


def copied(value):
    def body(from_ref, to_ref):
        to_ref[...] = from_ref[...]

    return on_chip(body, "copied", [value], [(value.shape, value.dtype)], cost(0, 0, 2 * value.size))[0]


def chip_pair(own, other, at):
    rows, columns = own.shape

    def body(at_ref, own_ref, other_ref, out_ref):
        part = at_ref[1]
        out_ref[pl.ds(pl.multiple_of(part * rows, rows), rows), :] = own_ref[...]
        out_ref[pl.ds(pl.multiple_of((1 - part) * rows, rows), rows), :] = other_ref[...]

    return on_chip(
        body, "chip_pair", [own, other], [((2 * rows, columns), BF16)], cost(0, 0, 0), [at]
    )[0]


class Place:
    def __init__(self):
        self.n_dp = lax.axis_size("dp")
        self.n_seq = lax.axis_size("seq")
        assert self.n_dp == 2 * self.n_seq
        self.split = 2 if H % (2 * self.n_seq) == 0 else 1
        self.blocks = self.n_dp // self.split
        self.dp = lax.axis_index("dp")
        self.z = lax.axis_index("seq")
        self.block = self.dp // self.split
        self.part = self.dp % self.split
        self.at = jnp.stack([self.z, self.part, self.block]).astype(jnp.int32)
        self.masks = [1 << k for k in range(self.blocks.bit_length() - 1)]
        self.order = list(range(self.blocks))
        self.paired = self.split == 2 and self.blocks == 4

    def swap(self, value, mask):
        return lax.ppermute(value, "dp", [(i, i ^ mask) for i in range(self.n_dp)])

    def to_relative(self, value, axis):
        size = value.shape[axis] // self.blocks
        return jnp.concatenate(
            [
                lax.dynamic_slice_in_dim(value, (self.block ^ off) * size, size, axis)
                for off in self.order
            ],
            axis=axis,
        )

    def to_natural(self, value, axis):
        return self.to_relative(value, axis)

    def pair(self, own, other, axis):
        return jnp.where(
            self.part == 0,
            jnp.concatenate([own, other], axis=axis),
            jnp.concatenate([other, own], axis=axis),
        )

    def gather(self, piece):
        half = piece.shape[0] // 2
        gathered = []
        for rows, masks in ((piece[:half], self.masks), (piece[half:], self.masks[::-1])):
            have = {0: rows}
            for mask in masks:
                offs = list(have)
                sent = jnp.concatenate([have[o] for o in offs], 0) if len(offs) > 1 else have[offs[0]]
                got = self.swap(sent, mask * self.split)
                for k, o in enumerate(offs):
                    have[o ^ mask] = got[k * half : (k + 1) * half]
            gathered.append(have)
        return gathered

    def scatter_sum(self, product, halves):
        out = []
        for half, masks in zip(halves, (self.masks, self.masks[::-1])):
            live = list(range(self.blocks))
            extra = {}

            def total(offs):
                whole = product(half, offs)
                if all(o not in extra for o in offs):
                    return whole
                axis, size = whole.ndim and product.axis, whole.shape[product.axis] // len(offs)
                parts = []
                for k, o in enumerate(offs):
                    value = lax.slice_in_dim(whole, k * size, (k + 1) * size, axis=axis)
                    for more in extra.get(o, ()):
                        value = value + more.astype(F32)
                    parts.append(value)
                return parts[0] if len(parts) == 1 else jnp.concatenate(parts, axis=axis)

            for mask in masks:
                away = [o for o in self.order if o in live and o & mask]
                sent = total(away).astype(BF16)
                got = self.swap(sent, mask * self.split)
                size = got.shape[product.axis] // len(away)
                for k, o in enumerate(away):
                    extra.setdefault(o ^ mask, []).append(
                        lax.slice_in_dim(got, k * size, (k + 1) * size, axis=product.axis)
                    )
                live = [o for o in live if not o & mask]
            out.append(total([0]))
        return out


class Product:
    def __init__(self, place, by_block, other, axis):
        self.place, self.by_block, self.other, self.axis = place, by_block, other, axis
        self.size = by_block.shape[1] // place.blocks

    def __call__(self, half, offs):
        where = [self.place.order.index(o) for o in offs]
        if where == list(range(where[0], where[0] + len(where))):
            blocks = self.by_block[:, where[0] * self.size : (where[-1] + 1) * self.size]
        else:
            blocks = jnp.concatenate(
                [self.by_block[:, w * self.size : (w + 1) * self.size] for w in where], axis=1
            )
        width = self.other.shape[1] // 2
        others = self.other[:, half * width : (half + 1) * width]
        if self.axis == 0:
            return left_transposed(blocks, others)
        return left_transposed(others, blocks)


class Chain:
    def __init__(self):
        self.last = None

    def __call__(self, *values):
        if self.last is not None:
            values = tuple(lax.optimization_barrier((values, self.last))[0])
        return values if len(values) > 1 else values[0]

    def done(self, value):
        self.last = value
        return value

    def wait(self, value):
        if value is not None:
            self.last = (self.last, value)


class Gathered:
    def __init__(self, here, piece):
        self.here, self.piece = here, piece
        self.half = piece.shape[0] // 2

    def send(self):
        here = self.here
        if here.paired:
            self.by_x, self.by_y = here.swap(self.piece, 2), here.swap(self.piece, 4)
            return self.by_x, self.by_y

    def hand_on(self, chain):
        if self.here.paired:
            half = self.half
            columns = self.piece.shape[1]

            def body(x_ref, y_ref, first_ref, second_ref):
                first_ref[...] = x_ref[:half, :]
                second_ref[...] = y_ref[half:, :]

            first, second = on_chip(
                body,
                "hand_on",
                chain(self.by_x, self.by_y),
                [((half, columns), BF16)] * 2,
                cost(0, 0, 4 * half * columns),
            )
            chain.done((first, second))
            self.handed = (self.here.swap(first, 4), self.here.swap(second, 2))
            return self.handed

    def rows(self, size, moving, columns=None):
        here, block = self.here, self.piece.shape[0]
        if here.paired:
            arrays = [self.piece, self.by_x, self.by_y, *self.handed]
            tiles, now, left = [], [], size
            for which, count in enumerate([block] * 3 + [self.half] * 2):
                first = 0
                while count:
                    take = min(left, count)
                    now.append((which, first, take))
                    first, count, left = first + take, count - take, left - take
                    if not left:
                        tiles.append(now)
                        now, left = [], size
            blocks = None
            if moving:
                assert size == block
                blocks = here.block ^ jnp.arange(here.blocks, dtype=jnp.int32)
            return Pieces(arrays, tiles, size, blocks, columns)
        if not hasattr(self, "whole"):
            halves = here.gather(self.piece)
            whole = jnp.concatenate([half[o] for o in range(here.blocks) for half in halves], axis=0)
            self.whole = here.to_natural(whole, 0) if moving else whole
        count = self.whole.shape[0] // size
        blocks = jnp.arange(count, dtype=jnp.int32) if moving else None
        return Pieces([self.whole], [[(0, k * size, size)] for k in range(count)], size, blocks, columns)


class Spread:
    def __init__(self, here, piece):
        self.here, self.step = here, 0
        chips = here.n_dp // 2
        masks = [1 << k for k in range(chips.bit_length() - 1)]
        self.steps = len(masks)
        self.offset = (here.dp // 2) ^ here.z
        self.states = [(piece[0], masks, [0]), (piece[1], masks[::-1], [0])]

    def send(self):
        here, self.got = self.here, []
        for rows, order, held in self.states:
            pairs = [
                (
                    (2 * (z ^ o) + c) * here.n_seq + z,
                    (2 * (z ^ o ^ order[self.step]) + c) * here.n_seq + z,
                )
                for z in range(here.n_seq)
                for o in held
                for c in range(2)
            ]
            self.got.append(lax.ppermute(rows, ("dp", "seq"), pairs))
        return tuple(self.got)

    def take(self, chain):
        got = chain(*self.got)
        after = []
        for new, (rows, order, held) in zip(got, self.states):
            takes = jnp.zeros((), jnp.bool_)
            for o in held:
                takes = takes | (self.offset == (o ^ order[self.step]))
            after.append(
                (
                    jnp.where(takes, new, rows),
                    order,
                    held + [o ^ order[self.step] for o in held],
                )
            )
        self.states = after
        self.step += 1
        chain.done(tuple(state[0] for state in after))

    def finish(self, chain):
        self.take(chain)
        here = self.here
        rows = jnp.concatenate([state[0] for state in self.states], axis=0)
        if here.split == 1:
            other = here.swap(rows, 1)
            rows = jnp.where(
                here.dp % 2 == 0,
                jnp.concatenate([rows, other], 0),
                jnp.concatenate([other, rows], 0),
            )
        return rows


class Scattered:
    def __init__(self, here, left, right):
        self.here, self.left, self.right = here, left, right
        self.axis = 0 if isinstance(left, (list, tuple)) else 1

    def part(self, off, **more):
        if self.axis == 0:
            return weight_grad(self.left[off], self.right, **more)
        return weight_grad(self.left, self.right[off], **more)

    def first(self, chain):
        if self.here.paired:
            if self.axis == 0:
                self.right = chain(self.right)
            else:
                self.left = chain(self.left)
            one, two = chain.done(self.part(3, halves=True))
            self.by_x, self.by_y = self.here.swap(one, 2), self.here.swap(two, 4)
            return self.by_x, self.by_y

    def second(self, chain):
        if self.here.paired:
            by_x, by_y = chain(self.by_x, self.by_y)
            half = by_x.shape[0]
            to_x = self.part(1, extras=((by_y, half),))
            to_y = self.part(2, extras=((by_x, 0),))
            chain.done((to_x, to_y))
            self.by_x, self.by_y = self.here.swap(to_x, 2), self.here.swap(to_y, 4)
            return self.by_x, self.by_y

    def last(self, chain, kind):
        if self.here.paired:
            by_x, by_y = chain(self.by_x, self.by_y)
            return chain.done(self.part(0, extras=((by_x, 0), (by_y, 0)), kind=kind))
        if self.axis == 1:
            product = Product(self.here, jnp.concatenate(self.right, axis=1), self.left, 1)
        else:
            product = Product(self.here, jnp.concatenate(self.left, axis=1), self.right, 0)
        halves = self.here.scatter_sum(product, (0, 1))
        return jnp.concatenate(halves, axis=1 - self.axis).astype(kind)


def on_device(
    tokens,
    doc_lengths,
    qkv_weight,
    qkv_bias,
    dense_weight,
    dense_bias,
    up_weight,
    up_bias,
    down_weight,
    down_bias,
    norm1_gain,
    norm1_shift,
    norm2_gain,
    norm2_shift,
    cotangent,
):
    here = Place()
    chain = Chain()
    n_dp, n_seq, split, blocks = here.n_dp, here.n_seq, here.split, here.blocks
    z, part = here.z, here.part
    rows_here, width = tokens.shape
    seq_len = rows_here * n_seq
    hidden_rows = down_weight.shape[0]
    slice_rows = hidden_rows // n_seq
    assert H == n_seq * split
    head_cols = 3 * HS

    def column_places(core):
        head = (z * split + core) * head_cols
        return head, [(k * split + core) * hidden_rows + z * slice_rows for k in range(blocks)]

    half_dense = dense_weight.shape[0] // 2
    wide_cols = head_cols + blocks * slice_rows
    if here.paired:
        size = width // blocks

        def moves(at, ins, outs):
            tokens_in, qkv_in, up_in, down_in, dense_in = ins
            plane, core, block = at[0], at[1], at[2]
            jobs = []
            for off in range(blocks):
                place = pl.multiple_of((block ^ off) * size, size)
                jobs.append((tokens_in.at[:, pl.ds(place, size)], outs[0].at[:, off * size : (off + 1) * size]))
            for out, its in ((outs[1], 1 - core), (outs[2], core)):
                place = pl.multiple_of((plane * split + its) * head_cols, 128)
                jobs.append((qkv_in.at[:, pl.ds(place, head_cols)], out.at[:, :head_cols]))
                for k in range(blocks):
                    place = pl.multiple_of((k * split + its) * hidden_rows + plane * slice_rows, 128)
                    to = head_cols + k * slice_rows
                    jobs.append((up_in.at[:, pl.ds(place, slice_rows)], out.at[:, to : to + slice_rows]))
            place = pl.multiple_of(plane * slice_rows, slice_rows)
            jobs.append((down_in.at[pl.ds(place, slice_rows), :], outs[3]))
            jobs.append((dense_in.at[:half_dense], outs[4]))
            jobs.append((dense_in.at[half_dense:], outs[5]))
            return jobs

        shapes = [tokens.shape] + [(qkv_weight.shape[0], wide_cols)] * 2 + [(slice_rows, width)]
        shapes = shapes + [(half_dense, width)] * 2
        tokens_rel, wide_other, wide_piece, down_piece, *dense_halves = chain.done(
            copies(
                "first_copies",
                here.at,
                (tokens, qkv_weight, up_weight, down_weight, dense_weight),
                shapes,
                moves,
            )
        )
        got = here.swap(wide_other, 1)
    else:
        tokens_rel = here.to_relative(tokens, 1)
        head, places = column_places(part)
        wide_piece = jnp.concatenate(
            [lax.dynamic_slice_in_dim(qkv_weight, head, head_cols, 1)]
            + [lax.dynamic_slice_in_dim(up_weight, place, slice_rows, 1) for place in places],
            axis=1,
        )
        down_piece = lax.dynamic_slice_in_dim(down_weight, z * slice_rows, slice_rows, 0)
        dense_halves = dense_weight[:half_dense], dense_weight[half_dense:]
    x_own = lax.all_gather(tokens_rel, "seq", axis=0, tiled=True)
    g_own = lax.all_gather(chain(cotangent), "seq", axis=0, tiled=True)
    dense_rows = Spread(here, dense_halves)
    dense_pair = dense_rows.send()
    small = (qkv_bias, up_bias, dense_bias, down_bias, norm1_gain, norm1_shift, norm2_gain, norm2_shift)
    packed_small = chain.done(jnp.concatenate(chain(*small)))
    packed_small = jnp.broadcast_to(packed_small[None], (n_dp,) + packed_small.shape)
    packed_small = lax.all_to_all(packed_small, "dp", 0, 0, tiled=True)
    lengths = [doc_lengths] + ([here.swap(doc_lengths, 1)] if split == 2 else [])
    if here.paired:
        wide_piece = chain.done(chip_pair(chain(wide_piece), got, here.at))
    wide_rows = Gathered(here, wide_piece)
    wide_pair = wide_rows.send()
    lengths = [chain(v) for v in lengths]
    tables, begins = chain.done(rotary_tables(lengths, seq_len))
    spans = [v.shape[0] for v in small]

    chain.wait(dense_pair)
    while dense_rows.step < dense_rows.steps - 1:
        dense_rows.take(chain)
        dense_pair = dense_rows.send()
        chain.wait(dense_pair)
    chain.wait(wide_pair)
    wide_pair = wide_rows.hand_on(chain)
    down_rows = Gathered(here, chain(down_piece))
    down_pair = down_rows.send()
    w_dense = dense_rows.finish(chain)
    if here.paired:
        b_qkv, b_up, b_out, scales = chain.done(
            small_params(chain(packed_small), here.at, spans, blocks, slice_rows)
        )
    else:
        pieces, first = [], 0
        for span in spans:
            pieces.append(packed_small[:, first : first + span].astype(F32))
            first += span
        b_qkv, b_up, b_dense, b_down = pieces[:4]
        head = (z * split + part) * head_cols
        b_qkv = lax.dynamic_slice_in_dim(b_qkv.reshape(1, -1), head, head_cols, 1)
        b_up = lax.dynamic_slice_in_dim(b_up, z * slice_rows, slice_rows, 1)
        b_up = b_up.reshape(blocks, split, slice_rows)
        b_up = lax.dynamic_index_in_dim(b_up, part, 1, keepdims=False).reshape(1, -1)
        b_out = (b_dense + b_down).reshape(1, -1)
        scales = here.to_relative(jnp.stack([v.reshape(-1) for v in pieces[4:]]), 1)
    streams = [x_own] + ([here.swap(chain(x_own), 1)] if split == 2 else [])
    normed = chain.done(two_norms(chain(*streams) if split == 2 else streams, scales, blocks))
    normed_one, normed_two, stats = normed[:blocks], normed[blocks:-1], normed[-1]
    chain.wait(wide_pair)
    g_own = chain(g_own)
    streams_g = [g_own] + ([here.swap(g_own, 1)] if split == 2 else [])
    qkv_pieces = wide_rows.rows(256, False, (0, head_cols))
    up_pieces = wide_rows.rows(256, False, (head_cols, blocks * slice_rows))
    activated, slope = chain.done(feed_up(normed_two, up_pieces, chain(b_up)))
    qkv, probs, attended = chain.done(
        attention_forward(normed_one, qkv_pieces, chain(b_qkv), tables, begins)
    )
    attended = attended.reshape(split * seq_len, HS)
    chain.wait(down_pair)

    down_pair = down_rows.hand_on(chain)
    g_blocks = chain.done(cotangent_blocks(chain(*streams_g) if split == 2 else streams_g, here.at, blocks))
    sum_down = Scattered(here, activated, g_blocks)
    sum_dense = Scattered(here, attended, g_blocks)
    pair_down = sum_down.first(chain)
    grad_projected, grad_qkv_bias = chain.done(
        attention_backward(chain(qkv), probs, g_blocks, w_dense, tables, here.at)
    )
    grad_projected = grad_projected.reshape(split * seq_len, head_cols)
    sum_qkv = Scattered(here, normed_one, grad_projected)
    chain.wait(down_pair)
    pair_qkv = sum_qkv.first(chain)
    down_pieces = down_rows.rows(down_piece.shape[0] if here.paired else 256, True)

    def join(value):
        return lax.psum_scatter(value, "seq", scatter_dimension=0, tiled=True).astype(F32)

    def branches(first, extra=None):
        return chain.done(
            branch_rows_of(chain(attended), w_dense, activated, down_pieces, first, seq_len, extra)
        )

    def terms(first, extra=None):
        return chain.done(
            input_terms(
                chain(grad_projected),
                qkv_pieces,
                grad_hidden,
                up_pieces,
                streams[first],
                stats,
                scales,
                first,
                extra,
            )
        )

    branch_other = branches(1) if split == 2 else None
    chain.wait(pair_down)
    chain.wait(pair_qkv)
    if split == 2:
        branch_other = here.swap(chain(branch_other), 1)
    branch_rows = join(branches(0, branch_other))
    pair_down = sum_down.second(chain)
    pair_dense = sum_dense.first(chain)
    grad_hidden, grad_up_bias = chain.done(hidden_grad(g_blocks, down_pieces, chain(slope), here.at))
    sum_up = Scattered(here, normed_two, grad_hidden)
    term_other, norm_sums = None, jnp.zeros((4, width), F32)
    if split == 2:
        term_other, norm_sums = terms(1)
    chain.wait(pair_dense)
    chain.wait(pair_down)
    sum_down_last = sum_down.last(chain, BF16)
    if split == 2:
        term_other = here.swap(chain(term_other), 1)
    pair_up = sum_up.first(chain)
    pair_dense = sum_dense.second(chain)
    term_own, more_sums = terms(0, term_other)
    norm_sums = norm_sums + more_sums

    norm_sums = here.to_natural(chain(norm_sums), 1)
    wide_qkv = lax.dynamic_update_slice_in_dim(
        jnp.zeros((H * head_cols,), F32), grad_qkv_bias.reshape(-1), (z * split + part) * head_cols, 0
    )
    wide_up = lax.dynamic_update_slice(
        jnp.zeros((blocks, split, n_seq, slice_rows), F32),
        grad_up_bias.reshape(blocks, 1, 1, slice_rows),
        (0, part, z, 0),
    )
    cotan_rows = cotangent.astype(F32)
    column_total = jnp.sum(cotan_rows, axis=0)
    devices = n_dp * n_seq
    wide = [wide_qkv, wide_up, column_total] + [norm_sums[k] for k in range(4)]
    wide = [v.reshape(devices, -1) for v in wide]
    sizes = [v.shape[1] for v in wide]
    swapped = lax.all_to_all(
        chain.done(jnp.concatenate(wide, axis=1)), ("dp", "seq"), split_axis=0, concat_axis=0, tiled=True
    )

    chain.wait(pair_up)
    chain.wait(pair_dense)
    term_rows = join(chain.done(copied(chain(term_own))))
    pair_up = sum_up.second(chain)
    pair_qkv = sum_qkv.second(chain)
    sum_dense_last = sum_dense.last(chain, F32)
    output = chain.done((chain(branch_rows) + tokens.astype(F32) + b_out).astype(BF16))
    chain.wait(pair_up)
    chain.wait(pair_qkv)
    chain.wait(swapped)
    sum_up_last = sum_up.last(chain, BF16)
    sum_qkv_last = sum_qkv.last(chain, F32)

    values = tokens_rel.astype(F32)
    centred = values - jnp.mean(values, axis=-1, keepdims=True)
    inverse = lax.rsqrt(jnp.mean(centred * centred, axis=-1, keepdims=True) + 1e-05)
    xhat = centred * inverse
    term_rows = chain(term_rows)
    term = (
        term_rows
        - jnp.mean(term_rows, axis=-1, keepdims=True)
        - xhat * jnp.mean(term_rows * xhat, axis=-1, keepdims=True)
    ) * inverse
    input_grad = chain.done((cotan_rows + here.to_natural(term, 1)).astype(BF16))
    total = jnp.sum(swapped, axis=0)
    sums, first = [], 0
    for size in sizes:
        sums.append(total[first : first + size])
        first += size
    sum_qkv_bias, sum_up_bias, sum_column, sum_gain_one, sum_shift_one, sum_gain_two, sum_shift_two = sums

    def to_plane(whole, axis):
        moved = lax.all_to_all(whole, "seq", split_axis=axis, concat_axis=axis, tiled=True)
        if split == 1:
            per = moved.shape[axis] // (n_seq * 2)
            if axis == 0:
                moved = moved.reshape(n_seq, 2, per, -1).transpose(1, 0, 2, 3).reshape(moved.shape)
            else:
                moved = moved.reshape(-1, n_seq, 2, per).transpose(0, 2, 1, 3).reshape(moved.shape)
        return moved

    def to_cores(value, axis):
        if split == 1:
            return value.astype(F32)
        size = value.shape[axis] // 2
        mine = lax.dynamic_slice_in_dim(value, part * size, size, axis)
        other = lax.dynamic_slice_in_dim(value, (1 - part) * size, size, axis)
        return here.pair(mine, here.swap(other, 1), 1 - axis).astype(F32)

    grad_down = to_cores(to_plane(sum_down_last, 0), 1)
    grad_dense = to_cores(sum_dense_last, 1)
    grad_up = to_cores(to_plane(sum_up_last, 1), 0)
    grad_qkv = to_cores(sum_qkv_last, 0)

    return (
        output,
        input_grad,
        grad_qkv,
        sum_qkv_bias,
        grad_dense,
        sum_column,
        grad_up,
        sum_up_bias,
        grad_down,
        sum_column,
        sum_gain_one,
        sum_shift_one,
        sum_gain_two,
        sum_shift_two,
    )


def solution(mesh):
    rows = P(("dp", "seq"), None)
    flat = P(("dp", "seq"))
    placed = (rows,) + (P("dp", None),) * 2 + (P("dp"), P("dp", None)) * 3 + (P("dp"),) * 5 + (rows,)
    return jax.shard_map(
        on_device,
        mesh=mesh,
        in_specs=placed,
        out_specs=(
            rows,
            rows,
            P("dp", "seq"),
            flat,
            P("seq", "dp"),
            flat,
            P("dp", "seq"),
            flat,
            P("seq", "dp"),
            flat,
            flat,
            flat,
            flat,
            flat,
        ),
        check_vma=False,
    )
```

time: 413 us -> 397 us (0.961)
  Pallas kernels: 89.6 us -> 113 us
  waiting for transfers between devices: 122 us -> 108 us
  local copies, waits for them, and re-layouts: 82.4 us -> 72.9 us
  other arithmetic: 32.3 us -> 23.4 us
  starting transfers between devices: 64.2 us -> 57.4 us
    all_to_all x1, waiting for transfers between devices: 9.63 us -> 36.3 us  [on_device(): packed_small = lax.all_to_all(packed_small, 'dp', 0, 0, tiled=True)]
    all_to_all x2, waiting for transfers between devices: 33.9 us -> 12.7 us  [to_plane(): lax.all_to_all(whole, 'seq', split_axis=axis, concat_axis=axis, tiled=True)]
    pallas_call x25 -> x31, Pallas kernels: 89.6 us -> 109 us  [on_chip(): pl.pallas_call(body, in_specs=[SMEM] * len(scalars) + [VMEM] * len(arrays...]
    reduce_scatter x2, waiting for transfers between devices: 15 us -> 0.02 us  [join(): lax.psum_scatter(value, 'seq', scatter_dimension=0, tiled=True).astype(F32)]
    unnamed x209 -> x242, local copies, waits for them, and re-layouts: 46.1 us -> 61 us
    slice x8 -> x0, local copies, waits for them, and re-layouts: 7.72 us -> none  [the longest x6 5.44 us: hand_on(): first, second = (by_x[:self.half], by_y[self.half:])]
    dynamic_slice x7 -> x0, local copies, waits for them, and re-layouts: 6.45 us -> none  [the longest x2 2.93 us: up_columns(): lax.dynamic_slice_in_dim(weight, (k * split + core) * hidden_rows + z * s...]
    ppermute x39 -> x34, starting transfers between devices: 30.6 us -> 24.3 us  [swap(): return lax.ppermute(value, 'dp', [(i, i ^ mask) for i in range(self.n_dp)])]
  transfers between devices with their start and end apart: 51 -> 46, of which waited for: 15 -> 15; matrix products, arithmetic and copies ran while one was open for 17% -> 9% of each run, Pallas kernels for 20% -> 26%
where the time goes in v3:
time: 397 us; the launch traced here: 390 us
  Pallas kernels  113 us (28%)
  waiting for transfers between devices  108 us (27%)
  local copies, waits for them, and re-layouts  72.9 us (18%)
  starting transfers between devices  57.4 us (14%)
  other arithmetic  23.4 us (6%)
  between operations  15.2 us (4%)
    pallas_call x31, Pallas kernels, on_chip(): pl.pallas_call(body, in_specs=[SMEM] * len(scalars) + [VMEM] * len(arrays...  109 us
    unnamed x242, local copies, waits for them, and re-layouts  61 us
    ppermute x34, waiting for transfers between devices, swap(): return lax.ppermute(value, 'dp', [(i, i ^ mask) for i in range(self.n_dp)])  52.6 us
    all_to_all x1, waiting for transfers between devices, on_device(): packed_small = lax.all_to_all(packed_small, 'dp', 0, 0, tiled=True)  36.3 us
    ppermute x34, starting transfers between devices, swap(): return lax.ppermute(value, 'dp', [(i, i ^ mask) for i in range(self.n_dp)])  24.3 us
    ppermute x4, starting transfers between devices, send(): self.got.append(lax.ppermute(rows, ('dp', 'seq'), pairs))  14.9 us
    all_to_all x2, waiting for transfers between devices, to_plane(): lax.all_to_all(whole, 'seq', split_axis=axis, concat_axis=axis, tiled=True)  12.7 us
    all_to_all x2, starting transfers between devices, to_plane(): lax.all_to_all(whole, 'seq', split_axis=axis, concat_axis=axis, tiled=True)  9.66 us
  transfers between devices with their start and end apart: 46, of which 15 were waited for; matrix products, arithmetic and copies ran while one was open for 9% of the time, Pallas kernels for 26%

profile of v3, /device:TPU:0, one launch (start us, length us, event | category | flops | bytes accessed | tf_op | source)
XLA Modules:
  0.0 390.4 jit_solution(17055474231284576617)
XLA Ops:
  9.7 3.5 first_copies.1
  15.5 5.2 %collective-permute-start = (bf16[128,2048]{1,0:T(8,128)(2,1)S(1)}, bf16[128,2048]{1,0:T(8,128)(2,1)}, u32[]{:S(2)}, u32[]{:S(2)}) collective-permute-start(bf16[128,2048]{1,0:T(8,128)(2,1)S(1)} %get-tuple-element.132), channel_id=1, source_target_pairs={{0,8},{4,12},{9,1},{13,5},{18,26},{22,30},{27,19},{31,23}} | collective-permute-start | bytes 1572872 | tf_op jit(solution)/shard_map/ppermute | solution.py:754
  20.7 2.1 collective-permute-start.1
  24.3 1.9 chip_pair.1.refs_4_.refs_0_.refs_1_
  27.4 2.6 rotary_tables.1
  30.1 2.0 collective-permute-done
  32.1 2.1 collective-permute-done.1
  35.1 3.2 collective-permute-start.5
  38.4 4.4 %collective-permute-start.4 = (bf16[128,2048]{1,0:T(8,128)(2,1)S(1)}, bf16[128,2048]{1,0:T(8,128)(2,1)S(1)}, u32[]{:S(2)}, u32[]{:S(2)}) collective-permute-start(bf16[128,2048]{1,0:T(8,128)(2,1)S(1)} %broadcast_select_fusion.2), channel_id=1, source_target_pairs={{0,16},{4,20},{8,24},{12,28},{9,25},{13,29},{1,17},{5,21},{18,2},{... | collective-permute-start | bytes 1572872 | tf_op jit(solution)/shard_map/ppermute | solution.py:754
  45.0 3.3 all-to-all-start
  48.7 36.3 %all-to-all-done = bf16[8,2,1664]{2,1,0:T(2,128)(2,1)S(1)} async-done(((bf16[8,2,1664]{2,1,0:T(2,128)(2,1)}), bf16[8,2,1664]{2,1,0:T(2,128)(2,1)S(1)}, u32[]{:S(2)}, u32[]{:S(2)}) %all-to-all-start) | async-done | bytes 53280 | tf_op jit(solution)/shard_map/all_to_all | solution.py:917
  85.1 2.3 hand_on.2
  87.4 2.5 broadcast_select_fusion
  91.1 2.2 collective-permute-start.9
  93.3 1.7 collective-permute-done.8.refs_1_.x_ref
  95.0 1.6 copy-done
  96.6 8.6 %two_norms.1 = (bf16[1024,512]{1,0:T(8,128)(2,1)S(1)}, bf16[1024,512]{1,0:T(8,128)(2,1)S(1)}, bf16[1024,512]{1,0:T(8,128)(2,1)S(1)}, bf16[1024,512]{1,0:T(8,128)...) custom-call(f32[4,2048]{1,0:T(4,128)S(1)} %get-tuple-element.160.sca, ...), custom_call_target="tpu_custom_call" | custom-call | flops 50331648 | bytes 12582912 | tf_op jit(solution)/shard_map/two_norms/pallas_call | solution.py:43
  114.5 1.7 collective-permute-start.12
  116.2 1.7 collective-permute-start.13
  124.2 8.8 %feed_up.1 = (bf16[1024,1024]{1,0:T(8,128)(2,1)S(1)}, f32[1024,1024]{1,0:T(8,128)S(1)}) custom-call(f32[1,1024]{1,0:T(1,128)S(1)} %get-tuple-element.174.b_ref, bf16[1024,512]{1,0:T(8,128)(2,1)S(1)} %copy-done.24, bf16[1024,512]{1,0:T(8,128)(2,1)S(1)} %copy-done.33, bf16[1024,512]{1,0:T(8,128)(2,1)S(1)} %copy-done.36, bf16[1024,512]{1,0:T(8,128)(2,1)S(1)} %copy-done.42, ...), custom_call_target="tpu_custom_call" | custom-call | flops 8589934592 | bytes 14680064 | tf_op jit(solution)/shard_map/feed_up/pallas_call | solution.py:43
  133.1 2.0 copy-done.100
  135.1 9.3 %attention_forward.1 = (bf16[2,512,768]{2,1,0:T(8,128)(2,1)S(1)}, f32[2,512,512]{2,1,0:T(8,128)S(1)}, bf16[2,512,256]{2,1,0:T(8,128)(2,1)S(1)}) custom-call(f32[1,768]{1,0:T(1,128)S(1)} %get-tuple-element.177.b_ref, f32[2,512,128]{2,1,0:T(8,128)S(1)} %copy-done.79, f32[2,512,128]{2,1,0:T(8,128)S(1)} %copy-done.81, f32[2,512,128]{2,1,0:T(8,128)S(1)} %copy-done.83, ...), custom_call_target="tpu_custom_call" | custom-call | flops 7516192768 | bytes 7864320 | tf_op jit(solution)/shard_map/attention_forward/pallas_call | solution.py:43
  145.3 1.8 copy-done.2
  151.1 5.7 %attention_backward.1 = (bf16[2,512,768]{2,1,0:T(8,128)(2,1)S(1)}, f32[1,768]{1,0:T(1,128)S(1)}) custom-call(s32[3]{0:T(128)S(1)} %pad_add_fusion.at_ref, bf16[2,512,768]{2,1,0:T(8,128)(2,1)S(1)} %get-tuple-element.197.qkv_ref, f32[2,512,512]{2,1,0:T(8,128)S(1)} %get-tuple-element.183.probs_ref, bf16[256,2048]{1,0:T(8,128)(2,1)S(1)} %pad_maximum_fusion.w_ref.wa_ref, ...), custom_call_target="tpu_custom_call" | custom-call | flops 4294967296 | bytes 6815744 | tf_op jit(solution)/shard_map/attention_backward/pallas_call | solution.py:43
  156.8 2.7 collective-permute-done.14.refs_3_.refs_4_.refs_7_
  161.2 1.8 collective-permute-start.19
  163.0 4.0 %branch_rows.2 = bf16[512,2048]{1,0:T(8,128)(2,1)S(1)} custom-call(s32[4]{0:T(128)S(1)} %iota_xor_fusion.blocks_ref, bf16[1024,256]{1,0:T(8,128)(2,1)S(1)} %bitcast.20, bf16[256,2048]{1,0:T(8,128)(2,1)S(1)} %pad_maximum_fusion.w_ref.wa_ref, bf16[1024,1024]{1,0:T(8,128)(2,1)S(1)} %get-tuple-element.194.l_ref.b_ref, bf16[256,2048]{1,0:T(8,128)(2,1)S(1)} %copy-done.39, ...), custom_call_target="tpu_custom_call" | custom-call | flops 5368709120 | bytes 8650752 | tf_op jit(solution)/shard_map/branch_rows/pallas_call | solution.py:43
  167.0 11.2 %collective-permute-done.18.refs_0_ = bf16[256,768]{1,0:T(8,128)(2,1)S(1)} collective-permute-done((bf16[256,768]{1,0:T(8,128)(2,1)S(1)}, bf16[256,768]{1,0:T(8,128)(2,1)S(1)}, u32[]{:S(2)}, u32[]{:S(2)}) %collective-permute-start.18) | collective-permute-done | bytes 393248 | tf_op jit(solution)/shard_map/ppermute | solution.py:567
  181.4 4.2 %collective-permute-done.20.refs_0_ = bf16[512,2048]{1,0:T(8,128)(2,1)S(1)} collective-permute-done((bf16[512,2048]{1,0:T(8,128)(2,1)S(1)}, bf16[512,2048]{1,0:T(8,128)(2,1)S(1)}, u32[]{:S(2)}, u32[]{:S(2)}) %collective-permute-start.20) | collective-permute-done | bytes 2097184 | tf_op jit(solution)/shard_map/ppermute | solution.py:567
  185.6 5.4 %branch_rows.3 = bf16[512,2048]{1,0:T(8,128)(2,1)} custom-call(s32[4]{0:T(128)S(1)} %iota_xor_fusion.blocks_ref, bf16[1024,256]{1,0:T(8,128)(2,1)S(1)} %bitcast.21, bf16[256,2048]{1,0:T(8,128)(2,1)S(1)} %pad_maximum_fusion.w_ref.wa_ref, bf16[1024,1024]{1,0:T(8,128)(2,1)S(1)} %get-tuple-element.194.l_ref.b_ref, ...), custom_call_target="tpu_custom_call" | custom-call | flops 5368709120 | bytes 8650752 | tf_op jit(solution)/shard_map/branch_rows/pallas_call | solution.py:43
  193.2 1.6 copy-done.98
  194.8 2.3 weight_grad.19
  197.1 2.2 weight_grad.18
  199.4 1.7 collective-permute-start.24
  202.8 1.8 collective-permute-start.23
  214.2 2.2 copy-done.101
  216.4 6.7 %hidden_grad.1 = (bf16[1024,1024]{1,0:T(8,128)(2,1)S(1)}, f32[1,1024]{1,0:T(1,128)S(1)}) custom-call(s32[4]{0:T(128)S(1)} %iota_xor_fusion.blocks_ref, s32[3]{0:T(128)S(1)} %pad_add_fusion.at_ref, f32[1024,1024]{1,0:T(8,128)S(1)} %copy-done.101, bf16[1024,512]{1,0:T(8,128)(2,1)S(1)} %get-tuple-element.190.refs_0_.r_ref, bf16[1024,512]{1,0:T(8,128)(2,1)S(1)} %copy-done.46, ...), custom_call_target="tpu_custom_call" | custom-call | flops 8589934592 | bytes 14680064 | tf_op jit(solution)/shard_map/hidden_grad/pallas_call | solution.py:43
  223.1 9.6 %input_terms.2 = (bf16[512,2048]{1,0:T(8,128)(2,1)}, f32[4,2048]{1,0:T(4,128)S(1)}) custom-call(bf16[1024,768]{1,0:T(8,128)(2,1)S(1)} %bitcast.30, bf16[1024,1024]{1,0:T(8,128)(2,1)S(1)} %get-tuple-element.219.gh_ref.r_ref, bf16[512,2048]{1,0:T(8,128)(2,1)S(1)} %collective-permute-done.8.refs_1_.x_ref, f32[1024,2]{1,0:T(8,128)S(1)} %copy-done.61, ...), custom_call_target="tpu_custom_call" | custom-call | flops 7516192768 | bytes 13369344 | tf_op jit(solution)/shard_map/input_terms/pallas_call | solution.py:43
  232.8 3.0 weight_grad.21
  239.7 2.1 weight_grad.22
  241.8 2.1 weight_grad.24
  243.9 1.7 collective-permute-start.26
  247.0 1.8 collective-permute-start.27
  249.1 5.2 %all-to-all-start.3 = ((bf16[4,256,512]{2,1,0:T(8,128)(2,1)}), bf16[4,256,512]{2,1,0:T(8,128)(2,1)}, u32[]{:S(2)}, u32[]{:S(2)}) async-start(bf16[4,256,512]{2,1,0:T(8,128)(2,1)} %bitcast.18), calls=%async_computation.5 | async-start | bytes 2097152 | tf_op jit(solution)/shard_map/all_to_all | solution.py:1080
  258.4 1.6 copy-done.94
  260.0 8.0 %input_terms.3 = (bf16[512,2048]{1,0:T(8,128)(2,1)S(1)}, f32[4,2048]{1,0:T(4,128)S(1)}) custom-call(bf16[1024,768]{1,0:T(8,128)(2,1)S(1)} %bitcast.31, bf16[1024,1024]{1,0:T(8,128)(2,1)S(1)} %copy-done.94, bf16[512,2048]{1,0:T(8,128)(2,1)S(1)} %copy-done.1, f32[1024,2]{1,0:T(8,128)S(1)} %copy-done.62, f32[4,2048]{1,0:T(4,128)S(1)} %get-tuple-element.160.scales_ref, ...), custom_call_target="tpu_custom_call" | custom-call | flops 7516192768 | bytes 13369344 | tf_op jit(solution)/shard_map/input_terms/pallas_call | solution.py:43
  275.5 1.6 copy-done.95
  277.0 3.4 weight_grad.26
  281.3 3.6 weight_grad.25
  286.0 1.9 weight_grad.28
  287.9 1.9 weight_grad.27
  296.3 25.4 %collective-permute-done.31.refs_1_ = bf16[512,768]{1,0:T(8,128)(2,1)} collective-permute-done((bf16[512,768]{1,0:T(8,128)(2,1)}, bf16[512,768]{1,0:T(8,128)(2,1)}, u32[]{:S(2)}, u32[]{:S(2)}) %collective-permute-start.31) | collective-permute-done | bytes 786464 | tf_op jit(solution)/shard_map/ppermute | solution.py:567
  321.8 4.6 %collective-permute-done.30.refs_0_ = bf16[512,768]{1,0:T(8,128)(2,1)} collective-permute-done((bf16[512,768]{1,0:T(8,128)(2,1)}, bf16[512,768]{1,0:T(8,128)(2,1)}, u32[]{:S(2)}, u32[]{:S(2)}) %collective-permute-start.30) | collective-permute-done | bytes 786464 | tf_op jit(solution)/shard_map/ppermute | solution.py:567
  326.4 4.7 %all-to-all-start.1 = ((f32[32,1,768]{2,1,0:T(1,128)}), f32[32,1,768]{2,1,0:T(1,128)S(1)}, u32[]{:S(2)}, u32[]{:S(2)}) async-start(f32[32,1,768]{2,1,0:T(1,128)} %copy.35), calls=%async_computation.3 | async-start | bytes 196608 | tf_op jit(solution)/shard_map/all_to_all | solution.py:1044
  332.7 2.9 weight_grad.30
  336.6 2.4 all-to-all-done.1
  339.0 4.5 %all-to-all-start.2 = ((bf16[512,4,256]{2,0,1:T(8,128)(2,1)}), bf16[512,4,256]{2,0,1:T(8,128)(2,1)}, u32[]{:S(2)}, u32[]{:S(2)}) async-start(bf16[512,4,256]{2,0,1:T(8,128)(2,1)} %bitcast.16), calls=%async_computation.4 | async-start | bytes 2097152 | tf_op jit(solution)/shard_map/all_to_all | solution.py:1080
  346.2 2.2 constant_dynamic-slice_fusion.1
  348.5 2.4 weight_grad.31
  352.3 2.9 fusion.10
  356.5 12.7 %all-to-all-done.2 = bf16[512,4,256]{2,0,1:T(8,128)(2,1)} async-done(((bf16[512,4,256]{2,0,1:T(8,128)(2,1)}), bf16[512,4,256]{2,0,1:T(8,128)(2,1)}, u32[]{:S(2)}, u32[]{:S(2)}) %all-to-all-start.2) | async-done | bytes 1048608 | tf_op jit(solution)/shard_map/all_to_all | solution.py:1080
  371.4 1.9 maximum_select_fusion.3
  373.3 2.7 maximum_select_fusion
  376.3 1.8 copy.38
  (364 shorter events, 92.2 us)
Async XLA Ops:
  7.2 83.4 %all-gather.3.cloned.1.call-start = ((), (), s32[]{:S(2)}) async-start(), calls=%async_computation.6 | async-start | bytes 2621440 | tf_op jit(solution)/shard_map/all_gather | solution.py:910
  9.6 13.2 %copy-start.106 = (bf16[768]{0:T(1024)(128)(2,1)S(1)}, bf16[768]{0:T(1024)(128)(2,1)}, u32[]{:S(2)}) copy-start(bf16[768]{0:T(1024)(128)(2,1)} %param.19) | copy-start | bytes 4612
  9.6 13.4 %copy-start.107 = (bf16[1024]{0:T(1024)(128)(2,1)S(1)}, bf16[1024]{0:T(1024)(128)(2,1)}, u32[]{:S(2)}) copy-start(bf16[1024]{0:T(1024)(128)(2,1)} %param.23) | copy-start | bytes 6148
  9.6 13.6 %copy-start.108 = (bf16[256]{0:T(256)(128)(2,1)S(1)}, bf16[256]{0:T(256)(128)(2,1)}, u32[]{:S(2)}) copy-start(bf16[256]{0:T(256)(128)(2,1)} %param.21) | copy-start | bytes 1540
  9.6 13.8 %copy-start.109 = (bf16[256]{0:T(256)(128)(2,1)S(1)}, bf16[256]{0:T(256)(128)(2,1)}, u32[]{:S(2)}) copy-start(bf16[256]{0:T(256)(128)(2,1)} %param.25) | copy-start | bytes 1540
  9.6 14.0 %copy-start.110 = (bf16[256]{0:T(256)(128)(2,1)S(1)}, bf16[256]{0:T(256)(128)(2,1)}, u32[]{:S(2)}) copy-start(bf16[256]{0:T(256)(128)(2,1)} %param.26) | copy-start | bytes 1540
  9.6 14.2 %copy-start.111 = (bf16[256]{0:T(256)(128)(2,1)S(1)}, bf16[256]{0:T(256)(128)(2,1)}, u32[]{:S(2)}) copy-start(bf16[256]{0:T(256)(128)(2,1)} %param.27) | copy-start | bytes 1540
  9.6 14.4 %copy-start.112 = (bf16[256]{0:T(256)(128)(2,1)S(1)}, bf16[256]{0:T(256)(128)(2,1)}, u32[]{:S(2)}) copy-start(bf16[256]{0:T(256)(128)(2,1)} %param.28) | copy-start | bytes 1540
  9.6 14.7 %copy-start.114 = (bf16[256]{0:T(256)(128)(2,1)S(1)}, bf16[256]{0:T(256)(128)(2,1)}, u32[]{:S(2)}) copy-start(bf16[256]{0:T(256)(128)(2,1)} %param.29) | copy-start | bytes 1540
  14.2 12.1 %copy-start.77 = (s32[1,4]{1,0:T(1,128)S(1)}, s32[1,4]{1,0:T(1,128)}, u32[]{:S(2)}) copy-start(s32[1,4]{1,0:T(1,128)} %refs_0_.2) | copy-start | bytes 52
  14.2 13.2 %copy-start.91 = (f32[1,128]{1,0:T(1,128)S(1)}, f32[1,128]{1,0:T(1,128)}, u32[]{:S(2)}) copy-start(f32[1,128]{1,0:T(1,128)} %constant.65.clone.refs_2_) | copy-start | bytes 1540
  14.2 98.7 %all-gather.5.cloned.1.call-start = ((), (), s32[]{:S(2)}) async-start(), calls=%async_computation.7 | async-start | bytes 2621440 | tf_op jit(solution)/shard_map/all_gather | solution.py:911
  15.1 9.2 %collective-permute-start.2 = (bf16[256,1792]{1,0:T(8,128)(2,1)}, bf16[256,1792]{1,0:T(8,128)(2,1)S(1)}, u32[]{:S(2)}, u32[]{:S(2)}) collective-permute-start(bf16[256,1792]{1,0:T(8,128)(2,1)} %copy-done.58), channel_id=1, source_target_pairs={{0,4},{4,0},{8,12},{12,8},{16,20},{20,16},{24,28},{28,24},{1,5},{5... | collective-permute-start | bytes 2752520 | tf_op jit(solution)/shard_map/ppermute | solution.py:567
  15.5 16.6 %collective-permute-start = (bf16[128,2048]{1,0:T(8,128)(2,1)S(1)}, bf16[128,2048]{1,0:T(8,128)(2,1)}, u32[]{:S(2)}, u32[]{:S(2)}) collective-permute-start(bf16[128,2048]{1,0:T(8,128)(2,1)S(1)} %get-tuple-element.132), channel_id=1, source_target_pairs={{0,8},{4,12},{9,1},{13,5},{18,26},{22,30},{27,19},{31,23}} | collective-permute-start | bytes 1572872 | tf_op jit(solution)/shard_map/ppermute | solution.py:754
  20.7 13.5 %collective-permute-start.1 = (bf16[128,2048]{1,0:T(8,128)(2,1)S(1)}, bf16[128,2048]{1,0:T(8,128)(2,1)}, u32[]{:S(2)}, u32[]{:S(2)}) collective-permute-start(bf16[128,2048]{1,0:T(8,128)(2,1)S(1)} %get-tuple-element.133), channel_id=1, source_target_pairs={{0,16},{4,20},{9,25},{13,29},{18,2},{22,6},{27,11},{31,15}} | collective-permute-start | bytes 1572872 | tf_op jit(solution)/shard_map/ppermute | solution.py:754
  26.2 58.8 %collective-permute-start.6 = (bf16[512,1792]{1,0:T(8,128)(2,1)}, bf16[512,1792]{1,0:T(8,128)(2,1)S(1)}, u32[]{:S(2)}, u32[]{:S(2)}) collective-permute-start(bf16[512,1792]{1,0:T(8,128)(2,1)} %chip_pair.1.refs_4_.refs_0_.refs_1_), channel_id=1, source_target_pairs={{0,8},{4,12},{8,0},{12,4},{16,24},{20,28},{24,16},{28,20},{1,9},{5... | collective-permute-start | bytes 5505032 | tf_op jit(solution)/shard_map/ppermute | solution.py:567
  26.2 58.9 %collective-permute-start.7 = (bf16[512,1792]{1,0:T(8,128)(2,1)}, bf16[512,1792]{1,0:T(8,128)(2,1)}, u32[]{:S(2)}, u32[]{:S(2)}) collective-permute-start(bf16[512,1792]{1,0:T(8,128)(2,1)} %chip_pair.1.refs_4_.refs_0_.refs_1_), channel_id=1, source_target_pairs={{0,16},{4,20},{8,24},{12,28},{16,0},{20,4},{24,8},{28,12},{1,17},{... | collective-permute-start | bytes 5505032 | tf_op jit(solution)/shard_map/ppermute | solution.py:567
  26.2 1.2 collective-permute-start.3
  35.1 50.0 %collective-permute-start.5 = (bf16[128,2048]{1,0:T(8,128)(2,1)}, bf16[128,2048]{1,0:T(8,128)(2,1)}, u32[]{:S(2)}, u32[]{:S(2)}) collective-permute-start(bf16[128,2048]{1,0:T(8,128)(2,1)} %broadcast_select_fusion.1), channel_id=1, source_target_pairs={{0,8},{4,12},{16,24},{20,28},{9,1},{13,5},{25,17},{29,21},{18,26},... | collective-permute-start | bytes 1572872 | tf_op jit(solution)/shard_map/ppermute | solution.py:754
  38.4 46.6 %collective-permute-start.4 = (bf16[128,2048]{1,0:T(8,128)(2,1)S(1)}, bf16[128,2048]{1,0:T(8,128)(2,1)S(1)}, u32[]{:S(2)}, u32[]{:S(2)}) collective-permute-start(bf16[128,2048]{1,0:T(8,128)(2,1)S(1)} %broadcast_select_fusion.2), channel_id=1, source_target_pairs={{0,16},{4,20},{8,24},{12,28},{9,25},{13,29},{1,17},{5,21},{18,2},{... | collective-permute-start | bytes 1572872 | tf_op jit(solution)/shard_map/ppermute | solution.py:754
  45.0 39.9 %all-to-all-start = ((bf16[8,2,1664]{2,1,0:T(2,128)(2,1)}), bf16[8,2,1664]{2,1,0:T(2,128)(2,1)S(1)}, u32[]{:S(2)}, u32[]{:S(2)}) async-start(bf16[8,2,1664]{2,1,0:T(2,128)(2,1)} %reshape.111), calls=%async_computation | async-start | bytes 106496 | tf_op jit(solution)/shard_map/all_to_all | solution.py:917
  48.4 245.8 %reduce-scatter.3.cloned.1.call-start = ((), (), s32[]{:S(2)}) async-start(), calls=%async_computation.8 | async-start | bytes 2621440 | tf_op jit(solution)/shard_map/reduce_scatter | solution.py:984
  90.6 4.4 %collective-permute-start.8 = (bf16[512,2048]{1,0:T(8,128)(2,1)}, bf16[512,2048]{1,0:T(8,128)(2,1)S(1)}, u32[]{:S(2)}, u32[]{:S(2)}) collective-permute-start(bf16[512,2048]{1,0:T(8,128)(2,1)} %all-gather.3.cloned.1.call-done.refs_0_.x_ref), channel_id=1, source_target_pairs={{0,4},{4,0},{8,12},{12,8},{16,20},{20,16},{24,28},{28,24},{1,5},{5... | collective-permute-start | bytes 6291464 | tf_op jit(solution)/shard_map/ppermute | solution.py:567
  90.6 23.1 %collective-permute-start.10 = (bf16[256,1792]{1,0:T(8,128)(2,1)}, bf16[256,1792]{1,0:T(8,128)(2,1)}, u32[]{:S(2)}, u32[]{:S(2)}) collective-permute-start(bf16[256,1792]{1,0:T(8,128)(2,1)} %copy-done.59), channel_id=1, source_target_pairs={{0,8},{4,12},{8,0},{12,4},{16,24},{20,28},{24,16},{28,20},{1,9},{5... | collective-permute-start | bytes 2752520 | tf_op jit(solution)/shard_map/ppermute | solution.py:567
  91.1 23.3 %collective-permute-start.9 = (bf16[256,1792]{1,0:T(8,128)(2,1)}, bf16[256,1792]{1,0:T(8,128)(2,1)}, u32[]{:S(2)}, u32[]{:S(2)}) collective-permute-start(bf16[256,1792]{1,0:T(8,128)(2,1)} %copy-done.57), channel_id=1, source_target_pairs={{0,16},{4,20},{8,24},{12,28},{16,0},{20,4},{24,8},{28,12},{1,17},{... | collective-permute-start | bytes 2752520 | tf_op jit(solution)/shard_map/ppermute | solution.py:567
  112.9 22.2 %copy-start.21 = (bf16[1024,512]{1,0:T(8,128)(2,1)}, bf16[1024,512]{1,0:T(8,128)(2,1)S(1)}, u32[]{:S(2)}) copy-start(bf16[1024,512]{1,0:T(8,128)(2,1)S(1)} %get-tuple-element.165.refs_0_.l_ref) | copy-start | bytes 3145732
  114.5 30.8 %collective-permute-start.11 = (bf16[512,2048]{1,0:T(8,128)(2,1)}, bf16[512,2048]{1,0:T(8,128)(2,1)S(1)}, u32[]{:S(2)}, u32[]{:S(2)}) collective-permute-start(bf16[512,2048]{1,0:T(8,128)(2,1)} %all-gather.5.cloned.1.call-done.refs_0_), channel_id=1, source_target_pairs={{0,4},{4,0},{8,12},{12,8},{16,20},{20,16},{24,28},{28,24},{1,5},{5... | collective-permute-start | bytes 6291464 | tf_op jit(solution)/shard_map/ppermute | solution.py:567
  114.5 30.1 %collective-permute-start.12 = (bf16[256,2048]{1,0:T(8,128)(2,1)}, bf16[256,2048]{1,0:T(8,128)(2,1)S(1)}, u32[]{:S(2)}, u32[]{:S(2)}) collective-permute-start(bf16[256,2048]{1,0:T(8,128)(2,1)} %copy-done.38), channel_id=1, source_target_pairs={{0,8},{4,12},{8,0},{12,4},{16,24},{20,28},{24,16},{28,20},{1,9},{5... | collective-permute-start | bytes 3145736 | tf_op jit(solution)/shard_map/ppermute | solution.py:567
  116.2 28.3 %collective-permute-start.13 = (bf16[256,2048]{1,0:T(8,128)(2,1)}, bf16[256,2048]{1,0:T(8,128)(2,1)S(1)}, u32[]{:S(2)}, u32[]{:S(2)}) collective-permute-start(bf16[256,2048]{1,0:T(8,128)(2,1)} %copy-done.38), channel_id=1, source_target_pairs={{0,16},{4,20},{8,24},{12,28},{16,0},{20,4},{24,8},{28,12},{1,17},{... | collective-permute-start | bytes 3145736 | tf_op jit(solution)/shard_map/ppermute | solution.py:567
  135.1 50.5 %copy-start.97 = (bf16[1024,1024]{1,0:T(8,128)(2,1)}, bf16[1024,1024]{1,0:T(8,128)(2,1)S(1)}, u32[]{:S(2)}) copy-start(bf16[1024,1024]{1,0:T(8,128)(2,1)S(1)} %get-tuple-element.194.l_ref.b_ref) | copy-start | bytes 6291460
  144.5 41.0 %copy-start.17 = (bf16[2,512,256]{2,1,0:T(8,128)(2,1)}, bf16[2,512,256]{2,1,0:T(8,128)(2,1)S(1)}, u32[]{:S(2)}) copy-start(bf16[2,512,256]{2,1,0:T(8,128)(2,1)S(1)} %get-tuple-element.178) | copy-start | bytes 1572868
  144.5 41.0 %copy-start.13 = (bf16[256,2048]{1,0:T(8,128)(2,1)}, bf16[256,2048]{1,0:T(8,128)(2,1)S(1)}, u32[]{:S(2)}) copy-start(bf16[256,2048]{1,0:T(8,128)(2,1)S(1)} %collective-permute-done.12.x_ref.refs_1_.refs_2_.refs_5_) | copy-start | bytes 3145732
  144.5 41.0 %copy-start.15 = (bf16[256,2048]{1,0:T(8,128)(2,1)}, bf16[256,2048]{1,0:T(8,128)(2,1)S(1)}, u32[]{:S(2)}) copy-start(bf16[256,2048]{1,0:T(8,128)(2,1)S(1)} %collective-permute-done.13.y_ref.refs_2_.refs_3_.refs_6_) | copy-start | bytes 3145732
  144.6 14.9 %collective-permute-start.14 = (bf16[128,2048]{1,0:T(8,128)(2,1)S(1)}, bf16[128,2048]{1,0:T(8,128)(2,1)S(1)}, u32[]{:S(2)}, u32[]{:S(2)}) collective-permute-start(bf16[128,2048]{1,0:T(8,128)(2,1)S(1)} %get-tuple-element.186), channel_id=1, source_target_pairs={{0,16},{4,20},{8,24},{12,28},{16,0},{20,4},{24,8},{28,12},{1,17},{... | collective-permute-start | bytes 1572872 | tf_op jit(solution)/shard_map/ppermute | solution.py:567
  145.0 14.8 %collective-permute-start.15 = (bf16[128,2048]{1,0:T(8,128)(2,1)S(1)}, bf16[128,2048]{1,0:T(8,128)(2,1)S(1)}, u32[]{:S(2)}, u32[]{:S(2)}) collective-permute-start(bf16[128,2048]{1,0:T(8,128)(2,1)S(1)} %get-tuple-element.187), channel_id=1, source_target_pairs={{0,8},{4,12},{8,0},{12,4},{16,24},{20,28},{24,16},{28,20},{1,9},{5... | collective-permute-start | bytes 1572872 | tf_op jit(solution)/shard_map/ppermute | solution.py:567
  149.3 30.5 %collective-permute-start.16 = (bf16[512,512]{1,0:T(8,128)(2,1)S(1)}, bf16[512,512]{1,0:T(8,128)(2,1)S(1)}, u32[]{:S(2)}, u32[]{:S(2)}) collective-permute-start(bf16[512,512]{1,0:T(8,128)(2,1)S(1)} %get-tuple-element.195), channel_id=1, source_target_pairs={{0,8},{4,12},{8,0},{12,4},{16,24},{20,28},{24,16},{28,20},{1,9},{5... | collective-permute-start | bytes 1572872 | tf_op jit(solution)/shard_map/ppermute | solution.py:567
  149.7 30.8 %collective-permute-start.17 = (bf16[512,512]{1,0:T(8,128)(2,1)S(1)}, bf16[512,512]{1,0:T(8,128)(2,1)S(1)}, u32[]{:S(2)}, u32[]{:S(2)}) collective-permute-start(bf16[512,512]{1,0:T(8,128)(2,1)S(1)} %get-tuple-element.196), channel_id=1, source_target_pairs={{0,16},{4,20},{8,24},{12,28},{16,0},{20,4},{24,8},{28,12},{1,17},{... | collective-permute-start | bytes 1572872 | tf_op jit(solution)/shard_map/ppermute | solution.py:567
  159.5 26.1 %copy-start.63 = (bf16[128,2048]{1,0:T(8,128)(2,1)}, bf16[128,2048]{1,0:T(8,128)(2,1)S(1)}, u32[]{:S(2)}) copy-start(bf16[128,2048]{1,0:T(8,128)(2,1)S(1)} %collective-permute-done.14.refs_3_.refs_4_.refs_7_) | copy-start | bytes 1572868
  159.8 25.7 %copy-start.65 = (bf16[128,2048]{1,0:T(8,128)(2,1)}, bf16[128,2048]{1,0:T(8,128)(2,1)S(1)}, u32[]{:S(2)}) copy-start(bf16[128,2048]{1,0:T(8,128)(2,1)S(1)} %collective-permute-done.15.refs_4_.refs_5_.refs_8_) | copy-start | bytes 1572868
  160.8 17.4 %collective-permute-start.18 = (bf16[256,768]{1,0:T(8,128)(2,1)S(1)}, bf16[256,768]{1,0:T(8,128)(2,1)S(1)}, u32[]{:S(2)}, u32[]{:S(2)}) collective-permute-start(bf16[256,768]{1,0:T(8,128)(2,1)S(1)} %get-tuple-element.201), channel_id=1, source_target_pairs={{0,8},{4,12},{8,0},{12,4},{16,24},{20,28},{24,16},{28,20},{1,9},{5... | collective-permute-start | bytes 1179656 | tf_op jit(solution)/shard_map/ppermute | solution.py:567
  161.2 17.8 %collective-permute-start.19 = (bf16[256,768]{1,0:T(8,128)(2,1)S(1)}, bf16[256,768]{1,0:T(8,128)(2,1)S(1)}, u32[]{:S(2)}, u32[]{:S(2)}) collective-permute-start(bf16[256,768]{1,0:T(8,128)(2,1)S(1)} %get-tuple-element.202), channel_id=1, source_target_pairs={{0,16},{4,20},{8,24},{12,28},{16,0},{20,4},{24,8},{28,12},{1,17},{... | collective-permute-start | bytes 1179656 | tf_op jit(solution)/shard_map/ppermute | solution.py:567
  181.4 4.2 %collective-permute-start.20 = (bf16[512,2048]{1,0:T(8,128)(2,1)S(1)}, bf16[512,2048]{1,0:T(8,128)(2,1)S(1)}, u32[]{:S(2)}, u32[]{:S(2)}) collective-permute-start(bf16[512,2048]{1,0:T(8,128)(2,1)S(1)} %branch_rows.2), channel_id=1, source_target_pairs={{0,4},{4,0},{8,12},{12,8},{16,20},{20,16},{24,28},{28,24},{1,5},{5... | collective-permute-start | bytes 6291464 | tf_op jit(solution)/shard_map/ppermute | solution.py:567
  199.4 33.3 %collective-permute-start.24 = (bf16[1024,512]{1,0:T(8,128)(2,1)}, bf16[1024,512]{1,0:T(8,128)(2,1)}, u32[]{:S(2)}, u32[]{:S(2)}) collective-permute-start(bf16[1024,512]{1,0:T(8,128)(2,1)} %weight_grad.19), channel_id=1, source_target_pairs={{0,16},{4,20},{8,24},{12,28},{16,0},{20,4},{24,8},{28,12},{1,17},{... | collective-permute-start | bytes 3145736 | tf_op jit(solution)/shard_map/ppermute | solution.py:567
  202.2 30.5 %collective-permute-start.21 = (bf16[128,512]{1,0:T(8,128)(2,1)}, bf16[128,512]{1,0:T(8,128)(2,1)}, u32[]{:S(2)}, u32[]{:S(2)}) collective-permute-start(bf16[128,512]{1,0:T(8,128)(2,1)} %get-tuple-element.209), channel_id=1, source_target_pairs={{0,8},{4,12},{8,0},{12,4},{16,24},{20,28},{24,16},{28,20},{1,9},{5... | collective-permute-start | bytes 393224 | tf_op jit(solution)/shard_map/ppermute | solution.py:567
  202.5 30.2 %collective-permute-start.22 = (bf16[128,512]{1,0:T(8,128)(2,1)}, bf16[128,512]{1,0:T(8,128)(2,1)S(1)}, u32[]{:S(2)}, u32[]{:S(2)}) collective-permute-start(bf16[128,512]{1,0:T(8,128)(2,1)} %get-tuple-element.210), channel_id=1, source_target_pairs={{0,16},{4,20},{8,24},{12,28},{16,0},{20,4},{24,8},{28,12},{1,17},{... | collective-permute-start | bytes 393224 | tf_op jit(solution)/shard_map/ppermute | solution.py:567
  202.8 29.9 %collective-permute-start.23 = (bf16[1024,512]{1,0:T(8,128)(2,1)}, bf16[1024,512]{1,0:T(8,128)(2,1)}, u32[]{:S(2)}, u32[]{:S(2)}) collective-permute-start(bf16[1024,512]{1,0:T(8,128)(2,1)} %weight_grad.18), channel_id=1, source_target_pairs={{0,8},{4,12},{8,0},{12,4},{16,24},{20,28},{24,16},{28,20},{1,9},{5... | collective-permute-start | bytes 3145736 | tf_op jit(solution)/shard_map/ppermute | solution.py:567
  236.8 17.7 %collective-permute-start.29 = (bf16[512,2048]{1,0:T(8,128)(2,1)}, bf16[512,2048]{1,0:T(8,128)(2,1)}, u32[]{:S(2)}, u32[]{:S(2)}) collective-permute-start(bf16[512,2048]{1,0:T(8,128)(2,1)} %get-tuple-element.225), channel_id=1, source_target_pairs={{0,4},{4,0},{8,12},{12,8},{16,20},{20,16},{24,28},{28,24},{1,5},{5... | collective-permute-start | bytes 6291464 | tf_op jit(solution)/shard_map/ppermute | solution.py:567
  243.9 27.3 %collective-permute-start.26 = (bf16[256,512]{1,0:T(8,128)(2,1)}, bf16[256,512]{1,0:T(8,128)(2,1)S(1)}, u32[]{:S(2)}, u32[]{:S(2)}) collective-permute-start(bf16[256,512]{1,0:T(8,128)(2,1)} %weight_grad.24), channel_id=1, source_target_pairs={{0,16},{4,20},{8,24},{12,28},{16,0},{20,4},{24,8},{28,12},{1,17},{... | collective-permute-start | bytes 786440 | tf_op jit(solution)/shard_map/ppermute | solution.py:567
  246.8 24.4 %collective-permute-start.25 = (bf16[256,512]{1,0:T(8,128)(2,1)}, bf16[256,512]{1,0:T(8,128)(2,1)}, u32[]{:S(2)}, u32[]{:S(2)}) collective-permute-start(bf16[256,512]{1,0:T(8,128)(2,1)} %weight_grad.23), channel_id=1, source_target_pairs={{0,8},{4,12},{8,0},{12,4},{16,24},{20,28},{24,16},{28,20},{1,9},{5... | collective-permute-start | bytes 786440 | tf_op jit(solution)/shard_map/ppermute | solution.py:567
  247.0 24.1 %collective-permute-start.27 = (bf16[256,1024]{1,0:T(8,128)(2,1)}, bf16[256,1024]{1,0:T(8,128)(2,1)}, u32[]{:S(2)}, u32[]{:S(2)}) collective-permute-start(bf16[256,1024]{1,0:T(8,128)(2,1)} %get-tuple-element.220), channel_id=1, source_target_pairs={{0,8},{4,12},{8,0},{12,4},{16,24},{20,28},{24,16},{28,20},{1,9},{5... | collective-permute-start | bytes 1572872 | tf_op jit(solution)/shard_map/ppermute | solution.py:567
  248.8 22.4 %collective-permute-start.28 = (bf16[256,1024]{1,0:T(8,128)(2,1)}, bf16[256,1024]{1,0:T(8,128)(2,1)}, u32[]{:S(2)}, u32[]{:S(2)}) collective-permute-start(bf16[256,1024]{1,0:T(8,128)(2,1)} %get-tuple-element.221), channel_id=1, source_target_pairs={{0,16},{4,20},{8,24},{12,28},{16,0},{20,4},{24,8},{28,12},{1,17},{... | collective-permute-start | bytes 1572872 | tf_op jit(solution)/shard_map/ppermute | solution.py:567
  249.1 77.3 %all-to-all-start.3 = ((bf16[4,256,512]{2,1,0:T(8,128)(2,1)}), bf16[4,256,512]{2,1,0:T(8,128)(2,1)}, u32[]{:S(2)}, u32[]{:S(2)}) async-start(bf16[4,256,512]{2,1,0:T(8,128)(2,1)} %bitcast.18), calls=%async_computation.5 | async-start | bytes 2097152 | tf_op jit(solution)/shard_map/all_to_all | solution.py:1080
  254.3 123.8 %reduce-scatter.5.cloned.1.call-start = ((), (), s32[]{:S(2)}) async-start(), calls=%async_computation.9 | async-start | bytes 2621440 | tf_op jit(solution)/shard_map/reduce_scatter | solution.py:984
  280.4 45.9 %collective-permute-start.33 = (bf16[512,1024]{1,0:T(8,128)(2,1)}, bf16[512,1024]{1,0:T(8,128)(2,1)}, u32[]{:S(2)}, u32[]{:S(2)}) collective-permute-start(bf16[512,1024]{1,0:T(8,128)(2,1)} %weight_grad.26), channel_id=1, source_target_pairs={{0,16},{4,20},{8,24},{12,28},{16,0},{20,4},{24,8},{28,12},{1,17},{... | collective-permute-start | bytes 3145736 | tf_op jit(solution)/shard_map/ppermute | solution.py:567
  284.9 41.5 %collective-permute-start.32 = (bf16[512,1024]{1,0:T(8,128)(2,1)}, bf16[512,1024]{1,0:T(8,128)(2,1)}, u32[]{:S(2)}, u32[]{:S(2)}) collective-permute-start(bf16[512,1024]{1,0:T(8,128)(2,1)} %weight_grad.25), channel_id=1, source_target_pairs={{0,8},{4,12},{8,0},{12,4},{16,24},{20,28},{24,16},{28,20},{1,9},{5... | collective-permute-start | bytes 3145736 | tf_op jit(solution)/shard_map/ppermute | solution.py:567
  289.8 32.0 %collective-permute-start.31 = (bf16[512,768]{1,0:T(8,128)(2,1)}, bf16[512,768]{1,0:T(8,128)(2,1)}, u32[]{:S(2)}, u32[]{:S(2)}) collective-permute-start(bf16[512,768]{1,0:T(8,128)(2,1)} %weight_grad.28), channel_id=1, source_target_pairs={{0,16},{4,20},{8,24},{12,28},{16,0},{20,4},{24,8},{28,12},{1,17},{... | collective-permute-start | bytes 2359304 | tf_op jit(solution)/shard_map/ppermute | solution.py:567
  291.2 35.2 %collective-permute-start.30 = (bf16[512,768]{1,0:T(8,128)(2,1)}, bf16[512,768]{1,0:T(8,128)(2,1)}, u32[]{:S(2)}, u32[]{:S(2)}) collective-permute-start(bf16[512,768]{1,0:T(8,128)(2,1)} %weight_grad.27), channel_id=1, source_target_pairs={{0,8},{4,12},{8,0},{12,4},{16,24},{20,28},{24,16},{28,20},{1,9},{5... | collective-permute-start | bytes 2359304 | tf_op jit(solution)/shard_map/ppermute | solution.py:567
  294.1 37.0 %copy-start.25 = (bf16[1024,512]{1,0:T(8,128)(2,1)S(1)}, bf16[1024,512]{1,0:T(8,128)(2,1)}, u32[]{:S(2)}) copy-start(bf16[1024,512]{1,0:T(8,128)(2,1)} %copy-done.23) | copy-start | bytes 3145732
  326.4 12.6 %all-to-all-start.1 = ((f32[32,1,768]{2,1,0:T(1,128)}), f32[32,1,768]{2,1,0:T(1,128)S(1)}, u32[]{:S(2)}, u32[]{:S(2)}) async-start(f32[32,1,768]{2,1,0:T(1,128)} %copy.35), calls=%async_computation.3 | async-start | bytes 196608 | tf_op jit(solution)/shard_map/all_to_all | solution.py:1044
  339.0 30.1 %all-to-all-start.2 = ((bf16[512,4,256]{2,0,1:T(8,128)(2,1)}), bf16[512,4,256]{2,0,1:T(8,128)(2,1)}, u32[]{:S(2)}, u32[]{:S(2)}) async-start(bf16[512,4,256]{2,0,1:T(8,128)(2,1)} %bitcast.16), calls=%async_computation.4 | async-start | bytes 2097152 | tf_op jit(solution)/shard_map/all_to_all | solution.py:1080
  348.5 3.9 collective-permute-start.37
  351.0 22.3 %collective-permute-start.34 = (f32[256,768]{1,0:T(8,128)S(1)}, f32[256,768]{1,0:T(8,128)}, u32[]{:S(2)}, u32[]{:S(2)}) collective-permute-start(f32[256,768]{1,0:T(8,128)S(1)} %get-tuple-element.263), channel_id=1, source_target_pairs={{0,4},{4,0},{8,12},{12,8},{16,20},{20,16},{24,28},{28,24},{1,5},{5... | collective-permute-start | bytes 2359304 | tf_op jit(solution)/shard_map/ppermute | solution.py:567
  352.3 19.1 %collective-permute-start.35 = (f32[256,256]{1,0:T(8,128)}, f32[256,256]{1,0:T(8,128)}, u32[]{:S(2)}, u32[]{:S(2)}) collective-permute-start(f32[256,256]{1,0:T(8,128)} %get-tuple-element.273), channel_id=1, source_target_pairs={{0,4},{4,0},{8,12},{12,8},{16,20},{20,16},{24,28},{28,24},{1,5},{5... | collective-permute-start | bytes 786440 | tf_op jit(solution)/shard_map/ppermute | solution.py:567
  370.8 5.3 %collective-permute-start.36 = (bf16[256,1024]{0,1:T(8,128)(2,1)S(1)}, bf16[256,1024]{0,1:T(8,128)(2,1)S(1)}, u32[]{:S(2)}, u32[]{:S(2)}) collective-permute-start(bf16[256,1024]{0,1:T(8,128)(2,1)S(1)} %get-tuple-element.267), channel_id=1, source_target_pairs={{0,4},{4,0},{8,12},{12,8},{16,20},{20,16},{24,28},{28,24},{1,5},{5... | collective-permute-start | bytes 1572872 | tf_op jit(solution)/shard_map/ppermute | solution.py:567
  (97 other events, 353.8 us)
Sparse Core Ops, SparseCore 0:
  14.3 48.6 all-gather.2
  64.5 44.6 all-gather.4
  204.7 44.3 reduce-scatter.2
  274.4 44.2 reduce-scatter.4

commit v4 on v3

--- a/solution.py
+++ b/solution.py
@@ -527,6 +527,54 @@
     )(at, packed)
 
 
+def chunk_rows(value, count):
+    rows, columns = value.shape
+    size = columns // count
+
+    def body(from_ref, to_ref):
+        for k in range(count):
+            to_ref[k * rows : (k + 1) * rows, :] = from_ref[:, k * size : (k + 1) * size]
+
+    return on_chip(
+        body, "chunk_rows", [value], [((rows * count, size), value.dtype)], cost(0, 0, 4 * value.size)
+    )[0]
+
+
+def core_shares(value, axis, at, count=1):
+    rows, columns = value.shape[0] // count, value.shape[1]
+    shape = (rows // 2, columns * count) if axis == 0 else (rows, columns // 2)
+
+    def body(at_ref, from_ref, mine_ref, other_ref):
+        part = at_ref[1]
+        for ref, which in ((mine_ref, part), (other_ref, 1 - part)):
+            if axis == 0:
+                for k in range(count):
+                    place = pl.multiple_of(k * rows + which * shape[0], shape[0])
+                    ref[:, k * columns : (k + 1) * columns] = from_ref[pl.ds(place, shape[0]), :]
+            else:
+                ref[...] = from_ref[:, pl.ds(pl.multiple_of(which * shape[1], shape[1]), shape[1])]
+
+    return on_chip(
+        body, "core_shares", [value], [(shape, value.dtype)] * 2, cost(0, 0, 4 * value.size), [at]
+    )
+
+
+def core_join(mine, got, axis, at):
+    rows, columns = mine.shape
+    shape = (2 * rows, columns) if axis == 0 else (rows, 2 * columns)
+
+    def body(at_ref, mine_ref, got_ref, out_ref):
+        part = at_ref[1]
+        for ref, which in ((mine_ref, part), (got_ref, 1 - part)):
+            if axis == 0:
+                out_ref[pl.ds(pl.multiple_of(which * rows, rows), rows), :] = ref[...].astype(F32)
+            else:
+                place = pl.multiple_of(which * columns, columns)
+                out_ref[:, pl.ds(place, columns)] = ref[...].astype(F32)
+
+    return on_chip(body, "core_join", [mine, got], [(shape, F32)], cost(0, 0, 8 * mine.size), [at])[0]
+
+
 def copied(value):
     def body(from_ref, to_ref):
         to_ref[...] = from_ref[...]
@@ -771,6 +819,9 @@
         self.states = after
         self.step += 1
         chain.done(tuple(state[0] for state in after))
+
+    def hold(self, chain):
+        self.states = [(chain(rows), order, held) for rows, order, held in self.states]
 
     def finish(self, chain):
         self.take(chain)
@@ -925,15 +976,9 @@
     spans = [v.shape[0] for v in small]
 
     chain.wait(dense_pair)
-    while dense_rows.step < dense_rows.steps - 1:
-        dense_rows.take(chain)
-        dense_pair = dense_rows.send()
-        chain.wait(dense_pair)
+    dense_rows.take(chain)
     chain.wait(wide_pair)
     wide_pair = wide_rows.hand_on(chain)
-    down_rows = Gathered(here, chain(down_piece))
-    down_pair = down_rows.send()
-    w_dense = dense_rows.finish(chain)
     if here.paired:
         b_qkv, b_up, b_out, scales = chain.done(
             small_params(chain(packed_small), here.at, spans, blocks, slice_rows)
@@ -955,6 +1000,13 @@
     normed = chain.done(two_norms(chain(*streams) if split == 2 else streams, scales, blocks))
     normed_one, normed_two, stats = normed[:blocks], normed[blocks:-1], normed[-1]
     chain.wait(wide_pair)
+    down_rows = Gathered(here, chain(down_piece))
+    down_pair = down_rows.send()
+    dense_rows.hold(chain)
+    dense_pair = dense_rows.send()
+    while dense_rows.step < dense_rows.steps - 1:
+        dense_rows.take(chain)
+        dense_pair = dense_rows.send()
     g_own = chain(g_own)
     streams_g = [g_own] + ([here.swap(g_own, 1)] if split == 2 else [])
     qkv_pieces = wide_rows.rows(256, False, (0, head_cols))
@@ -965,12 +1017,14 @@
     )
     attended = attended.reshape(split * seq_len, HS)
     chain.wait(down_pair)
+    chain.wait(dense_pair)
 
     down_pair = down_rows.hand_on(chain)
     g_blocks = chain.done(cotangent_blocks(chain(*streams_g) if split == 2 else streams_g, here.at, blocks))
     sum_down = Scattered(here, activated, g_blocks)
     sum_dense = Scattered(here, attended, g_blocks)
     pair_down = sum_down.first(chain)
+    w_dense = dense_rows.finish(chain)
     grad_projected, grad_qkv_bias = chain.done(
         attention_backward(chain(qkv), probs, g_blocks, w_dense, tables, here.at)
     )
@@ -979,6 +1033,16 @@
     chain.wait(down_pair)
     pair_qkv = sum_qkv.first(chain)
     down_pieces = down_rows.rows(down_piece.shape[0] if here.paired else 256, True)
+
+    def to_plane(whole, axis):
+        if here.paired:
+            whole = chunk_rows(whole, n_seq) if axis == 1 else whole
+            return lax.all_to_all(whole, "seq", split_axis=0, concat_axis=0, tiled=True)
+        moved = lax.all_to_all(whole, "seq", split_axis=axis, concat_axis=axis, tiled=True)
+        per = moved.shape[axis] // (n_seq * 2)
+        if axis == 0:
+            return moved.reshape(n_seq, 2, per, -1).transpose(1, 0, 2, 3).reshape(moved.shape)
+        return moved.reshape(-1, n_seq, 2, per).transpose(0, 2, 1, 3).reshape(moved.shape)
 
     def join(value):
         return lax.psum_scatter(value, "seq", scatter_dimension=0, tiled=True).astype(F32)
@@ -1008,8 +1072,8 @@
     chain.wait(pair_qkv)
     if split == 2:
         branch_other = here.swap(chain(branch_other), 1)
+    pair_down = sum_down.second(chain)
     branch_rows = join(branches(0, branch_other))
-    pair_down = sum_down.second(chain)
     pair_dense = sum_dense.first(chain)
     grad_hidden, grad_up_bias = chain.done(hidden_grad(g_blocks, down_pieces, chain(slope), here.at))
     sum_up = Scattered(here, normed_two, grad_hidden)
@@ -1018,11 +1082,11 @@
         term_other, norm_sums = terms(1)
     chain.wait(pair_dense)
     chain.wait(pair_down)
-    sum_down_last = sum_down.last(chain, BF16)
+    plane_down = to_plane(sum_down.last(chain, BF16), 0)
     if split == 2:
         term_other = here.swap(chain(term_other), 1)
     pair_up = sum_up.first(chain)
-    pair_dense = sum_dense.second(chain)
+    pair_qkv = sum_qkv.second(chain)
     term_own, more_sums = terms(0, term_other)
     norm_sums = norm_sums + more_sums
 
@@ -1041,24 +1105,32 @@
     wide = [wide_qkv, wide_up, column_total] + [norm_sums[k] for k in range(4)]
     wide = [v.reshape(devices, -1) for v in wide]
     sizes = [v.shape[1] for v in wide]
-    swapped = lax.all_to_all(
-        chain.done(jnp.concatenate(wide, axis=1)), ("dp", "seq"), split_axis=0, concat_axis=0, tiled=True
-    )
+    wide = chain.done(jnp.concatenate(wide, axis=1))
+
+    def to_cores(value, axis, count=1):
+        if not here.paired:
+            return lambda: value.astype(F32)
+        mine, other = chain.done(core_shares(chain(value), axis, here.at, count))
+        got = here.swap(other, 1)
+        return lambda: chain.done(core_join(*chain(mine, got), 1 - axis, here.at))
 
     chain.wait(pair_up)
-    chain.wait(pair_dense)
+    chain.wait(pair_qkv)
+    chain.wait(plane_down)
     term_rows = join(chain.done(copied(chain(term_own))))
     pair_up = sum_up.second(chain)
-    pair_qkv = sum_qkv.second(chain)
-    sum_dense_last = sum_dense.last(chain, F32)
+    pair_dense = sum_dense.second(chain)
+    sum_qkv_last = sum_qkv.last(chain, F32)
     output = chain.done((chain(branch_rows) + tokens.astype(F32) + b_out).astype(BF16))
     chain.wait(pair_up)
-    chain.wait(pair_qkv)
-    chain.wait(swapped)
-    sum_up_last = sum_up.last(chain, BF16)
-    sum_qkv_last = sum_qkv.last(chain, F32)
-
-    values = tokens_rel.astype(F32)
+    plane_up = to_plane(sum_up.last(chain, BF16), 1)
+    grad_qkv = to_cores(sum_qkv_last, 0)
+    grad_down = to_cores(plane_down, 1)
+    chain.wait(pair_dense)
+    grad_dense = to_cores(sum_dense.last(chain, F32), 1)
+    grad_qkv, grad_down = grad_qkv(), grad_down()
+
+    values = chain(tokens_rel).astype(F32)
     centred = values - jnp.mean(values, axis=-1, keepdims=True)
     inverse = lax.rsqrt(jnp.mean(centred * centred, axis=-1, keepdims=True) + 1e-05)
     xhat = centred * inverse
@@ -1069,6 +1141,9 @@
         - xhat * jnp.mean(term_rows * xhat, axis=-1, keepdims=True)
     ) * inverse
     input_grad = chain.done((cotan_rows + here.to_natural(term, 1)).astype(BF16))
+    grad_dense = grad_dense()
+    wide, plane_up = lax.optimization_barrier((wide, plane_up))
+    swapped = lax.all_to_all(wide, ("dp", "seq"), split_axis=0, concat_axis=0, tiled=True)
     total = jnp.sum(swapped, axis=0)
     sums, first = [], 0
     for size in sizes:
@@ -1076,29 +1151,7 @@
         first += size
     sum_qkv_bias, sum_up_bias, sum_column, sum_gain_one, sum_shift_one, sum_gain_two, sum_shift_two = sums
 
-    def to_plane(whole, axis):
-        moved = lax.all_to_all(whole, "seq", split_axis=axis, concat_axis=axis, tiled=True)
-        if split == 1:
-            per = moved.shape[axis] // (n_seq * 2)
-            if axis == 0:
-                moved = moved.reshape(n_seq, 2, per, -1).transpose(1, 0, 2, 3).reshape(moved.shape)
-            else:
-                moved = moved.reshape(-1, n_seq, 2, per).transpose(0, 2, 1, 3).reshape(moved.shape)
-        return moved
-
-    def to_cores(value, axis):
-        if split == 1:
-            return value.astype(F32)
-        size = value.shape[axis] // 2
-        mine = lax.dynamic_slice_in_dim(value, part * size, size, axis)
-        other = lax.dynamic_slice_in_dim(value, (1 - part) * size, size, axis)
-        return here.pair(mine, here.swap(other, 1), 1 - axis).astype(F32)
-
-    grad_down = to_cores(to_plane(sum_down_last, 0), 1)
-    grad_dense = to_cores(sum_dense_last, 1)
-    grad_up = to_cores(to_plane(sum_up_last, 1), 0)
-    grad_qkv = to_cores(sum_qkv_last, 0)
-
+    grad_up = to_cores(plane_up, 0, n_seq)()
     return (
         output,
         input_grad,

time: 397 us -> 384 us (0.967)
  local copies, waits for them, and re-layouts: 72.9 us -> 57.2 us
  blocking collectives: 0 us -> 11.3 us
  Pallas kernels: 113 us -> 124 us
  other arithmetic: 23.4 us -> 12.4 us
  waiting for transfers between devices: 108 us -> 102 us
    all_to_all x3 -> x2, waiting for transfers between devices: 15.1 us -> 3.09 us  [to_plane(): return lax.all_to_all(whole, 'seq', split_axis=0, concat_axis=0, tiled=True)]
    all_to_all x0 -> x1, blocking collectives: none -> 11.3 us  [on_device(): lax.all_to_all(wide, ('dp', 'seq'), split_axis=0, concat_axis=0, tiled=True)]
    pallas_call x31 -> x40, Pallas kernels: 109 us -> 120 us  [on_chip(): pl.pallas_call(body, in_specs=[SMEM] * len(scalars) + [VMEM] * len(arrays...]
    unnamed x242 -> x235, local copies, waits for them, and re-layouts: 61 us -> 53 us
    ppermute x34, starting transfers between devices: 24.3 us -> 30.3 us  [swap(): return lax.ppermute(value, 'dp', [(i, i ^ mask) for i in range(self.n_dp)])]
    all_to_all x3 -> x2, starting transfers between devices: 14.3 us -> 8.49 us  [to_plane(): return lax.all_to_all(whole, 'seq', split_axis=0, concat_axis=0, tiled=True)]
    select_n x2 -> x0, other arithmetic: 4.58 us -> none  [pair(): jnp.where(self.part == 0, jnp.concatenate([own, other], axis=axis), jnp.c...]
  transfers between devices with their start and end apart: 46 -> 45, of which waited for: 15 -> 17; matrix products, arithmetic and copies ran while one was open for 9% -> 5% of each run, Pallas kernels for 26% -> 31%
where the time goes in v4:
time: 384 us; the launch traced here: 377 us
  Pallas kernels  124 us (32%)
  waiting for transfers between devices  102 us (27%)
  local copies, waits for them, and re-layouts  57.2 us (15%)
  starting transfers between devices  55 us (14%)
  between operations  15.1 us (4%)
  other arithmetic  12.4 us (3%)
  blocking collectives  11.3 us (3%)
    pallas_call x40, Pallas kernels, on_chip(): pl.pallas_call(body, in_specs=[SMEM] * len(scalars) + [VMEM] * len(arrays...  120 us
    ppermute x34, waiting for transfers between devices, swap(): return lax.ppermute(value, 'dp', [(i, i ^ mask) for i in range(self.n_dp)])  55.9 us
    unnamed x235, local copies, waits for them, and re-layouts  53 us
    all_to_all x1, waiting for transfers between devices, on_device(): packed_small = lax.all_to_all(packed_small, 'dp', 0, 0, tiled=True)  39.9 us
    ppermute x34, starting transfers between devices, swap(): return lax.ppermute(value, 'dp', [(i, i ^ mask) for i in range(self.n_dp)])  30.3 us
    ppermute x4, starting transfers between devices, send(): self.got.append(lax.ppermute(rows, ('dp', 'seq'), pairs))  12.7 us
    all_to_all x1, blocking collectives, on_device(): lax.all_to_all(wide, ('dp', 'seq'), split_axis=0, concat_axis=0, tiled=True)  11.3 us
    all_to_all x2, starting transfers between devices, to_plane(): return lax.all_to_all(whole, 'seq', split_axis=0, concat_axis=0, tiled=True)  8.49 us
  transfers between devices with their start and end apart: 45, of which 17 were waited for; matrix products, arithmetic and copies ran while one was open for 5% of the time, Pallas kernels for 31%

profile of v4, /device:TPU:0, one launch (start us, length us, event | category | flops | bytes accessed | tf_op | source)
XLA Modules:
  0.0 376.8 jit_solution(17197056088831153515)
XLA Ops:
  9.7 3.5 first_copies.1
  17.8 1.9 chip_pair.1.refs_4_.refs_0_.refs_1_
  19.7 2.8 collective-permute-start.1
  22.5 1.5 collective-permute-start.2
  24.1 3.2 collective-permute-start.3
  27.3 2.1 collective-permute-start.4
  31.6 3.3 all-to-all-start
  35.5 39.9 %all-to-all-done = bf16[8,2,1664]{2,1,0:T(2,128)(2,1)S(1)} async-done(((bf16[8,2,1664]{2,1,0:T(2,128)(2,1)}), bf16[8,2,1664]{2,1,0:T(2,128)(2,1)S(1)}, u32[]{:S(2)}, u32[]{:S(2)}) %all-to-all-start) | async-done | bytes 53280 | tf_op jit(solution)/shard_map/all_to_all | solution.py:968
  75.5 2.6 rotary_tables.1
  81.0 3.5 hand_on.2
  85.2 3.9 %collective-permute-start.7 = (bf16[256,1792]{1,0:T(8,128)(2,1)}, bf16[256,1792]{1,0:T(8,128)(2,1)}, u32[]{:S(2)}, u32[]{:S(2)}) collective-permute-start(bf16[256,1792]{1,0:T(8,128)(2,1)} %get-tuple-element.177), channel_id=1, source_target_pairs={{0,16},{4,20},{8,24},{12,28},{16,0},{20,4},{24,8},{28,12},{1,17},{... | collective-permute-start | bytes 2752520 | tf_op jit(solution)/shard_map/ppermute | solution.py:615
  89.6 1.6 copy-done
  91.2 8.6 %two_norms.1 = (bf16[1024,512]{1,0:T(8,128)(2,1)S(1)}, bf16[1024,512]{1,0:T(8,128)(2,1)S(1)}, bf16[1024,512]{1,0:T(8,128)(2,1)S(1)}, bf16[1024,512]{1,0:T(8,128)...) custom-call(f32[4,2048]{1,0:T(4,128)S(1)} %get-tuple-element.182.sca, ...), custom_call_target="tpu_custom_call" | custom-call | flops 50331648 | bytes 12582912 | tf_op jit(solution)/shard_map/two_norms/pallas_call | solution.py:43
  107.6 1.7 all-gather.5.cloned.1.call-done.refs_0_
  110.3 1.5 collective-permute-done.8.refs_8_.refs_4_.refs_5_
  112.6 3.5 collective-permute-start.13
  116.1 3.8 %collective-permute-start.12 = (bf16[128,2048]{1,0:T(8,128)(2,1)}, bf16[128,2048]{1,0:T(8,128)(2,1)S(1)}, u32[]{:S(2)}, u32[]{:S(2)}) collective-permute-start(bf16[128,2048]{1,0:T(8,128)(2,1)} %get-tuple-element.206), channel_id=1, source_target_pairs={{0,16},{4,20},{8,24},{12,28},{9,25},{13,29},{1,17},{5,21},{18,2},{... | collective-permute-start | bytes 1572872 | tf_op jit(solution)/shard_map/ppermute | solution.py:802
  119.9 1.5 copy-done.6
  125.2 8.8 %feed_up.1 = (bf16[1024,1024]{1,0:T(8,128)(2,1)S(1)}, f32[1024,1024]{1,0:T(8,128)S(1)}) custom-call(f32[1,1024]{1,0:T(1,128)S(1)} %get-tuple-element.196.b_ref, bf16[1024,512]{1,0:T(8,128)(2,1)S(1)} %get-tuple-element.191.refs_0_.l_ref, bf16[1024,512]{1,0:T(8,128)(2,1)S(1)} %copy-done.31, bf16[1024,512]{1,0:T(8,128)(2,1)S(1)} %copy-done.34, ...), custom_call_target="tpu_custom_call" | custom-call | flops 8589934592 | bytes 14680064 | tf_op jit(solution)/shard_map/feed_up/pallas_call | solution.py:43
  134.0 2.0 copy-done.96
  136.1 9.3 %attention_forward.1 = (bf16[2,512,768]{2,1,0:T(8,128)(2,1)S(1)}, f32[2,512,512]{2,1,0:T(8,128)S(1)}, bf16[2,512,256]{2,1,0:T(8,128)(2,1)S(1)}) custom-call(f32[1,768]{1,0:T(1,128)S(1)} %get-tuple-element.199.b_ref, f32[2,512,128]{2,1,0:T(8,128)S(1)} %copy-done.77, f32[2,512,128]{2,1,0:T(8,128)S(1)} %copy-done.79, f32[2,512,128]{2,1,0:T(8,128)S(1)} %copy-done.81, ...), custom_call_target="tpu_custom_call" | custom-call | flops 7516192768 | bytes 7864320 | tf_op jit(solution)/shard_map/attention_forward/pallas_call | solution.py:43
  147.1 2.4 collective-permute-start.16
  149.5 1.5 collective-permute-start.17
  151.1 1.9 cotangent_blocks.1
  155.8 5.9 %attention_backward.1 = (bf16[2,512,768]{2,1,0:T(8,128)(2,1)S(1)}, f32[1,768]{1,0:T(1,128)S(1)}) custom-call(s32[3]{0:T(128)S(1)} %pad_add_fusion.at_ref, bf16[2,512,768]{2,1,0:T(8,128)(2,1)S(1)} %get-tuple-element.223.qkv_ref, f32[2,512,512]{2,1,0:T(8,128)S(1)} %get-tuple-element.205.probs_ref, bf16[256,2048]{1,0:T(8,128)(2,1)S(1)} %pad_maximum_fusion.w_ref.wa_ref, ...), custom_call_target="tpu_custom_call" | custom-call | flops 4294967296 | bytes 6815744 | tf_op jit(solution)/shard_map/attention_backward/pallas_call | solution.py:43
  162.3 2.0 collective-permute-done.17.refs_4_.refs_5_.refs_8_
  165.4 1.6 collective-permute-start.18
  167.3 4.0 %branch_rows.2 = bf16[512,2048]{1,0:T(8,128)(2,1)S(1)} custom-call(s32[4]{0:T(128)S(1)} %iota_xor_fusion.blocks_ref, bf16[1024,256]{1,0:T(8,128)(2,1)S(1)} %bitcast.17, bf16[256,2048]{1,0:T(8,128)(2,1)S(1)} %pad_maximum_fusion.w_ref.wa_ref, bf16[1024,1024]{1,0:T(8,128)(2,1)S(1)} %get-tuple-element.218.l_ref.b_ref, bf16[256,2048]{1,0:T(8,128)(2,1)S(1)} %copy-done.43, ...), custom_call_target="tpu_custom_call" | custom-call | flops 5368709120 | bytes 8650752 | tf_op jit(solution)/shard_map/branch_rows/pallas_call | solution.py:43
  171.3 10.8 %collective-permute-done.18.refs_0_ = bf16[256,768]{1,0:T(8,128)(2,1)S(1)} collective-permute-done((bf16[256,768]{1,0:T(8,128)(2,1)S(1)}, bf16[256,768]{1,0:T(8,128)(2,1)S(1)}, u32[]{:S(2)}, u32[]{:S(2)}) %collective-permute-start.18) | collective-permute-done | bytes 393248 | tf_op jit(solution)/shard_map/ppermute | solution.py:615
  183.6 2.3 weight_grad.19
  186.4 2.4 weight_grad.18
  188.7 1.7 collective-permute-start.21
  190.5 5.4 %branch_rows.3 = bf16[512,2048]{1,0:T(8,128)(2,1)} custom-call(s32[4]{0:T(128)S(1)} %iota_xor_fusion.blocks_ref, bf16[1024,256]{1,0:T(8,128)(2,1)S(1)} %bitcast.18, bf16[256,2048]{1,0:T(8,128)(2,1)S(1)} %pad_maximum_fusion.w_ref.wa_ref, bf16[1024,1024]{1,0:T(8,128)(2,1)S(1)} %get-tuple-element.218.l_ref.b_ref, ...), custom_call_target="tpu_custom_call" | custom-call | flops 5368709120 | bytes 8650752 | tf_op jit(solution)/shard_map/branch_rows/pallas_call | solution.py:43
  199.5 1.7 collective-permute-start.24
  210.8 2.2 copy-done.97
  213.0 6.4 %hidden_grad.1 = (bf16[1024,1024]{1,0:T(8,128)(2,1)S(1)}, f32[1,1024]{1,0:T(1,128)S(1)}) custom-call(s32[4]{0:T(128)S(1)} %iota_xor_fusion.blocks_ref, s32[3]{0:T(128)S(1)} %pad_add_fusion.at_ref, f32[1024,1024]{1,0:T(8,128)S(1)} %copy-done.97, bf16[1024,512]{1,0:T(8,128)(2,1)S(1)} %get-tuple-element.214.refs_0_.r_ref, bf16[1024,512]{1,0:T(8,128)(2,1)S(1)} %copy-done.37, ...), custom_call_target="tpu_custom_call" | custom-call | flops 8589934592 | bytes 14680064 | tf_op jit(solution)/shard_map/hidden_grad/pallas_call | solution.py:43
  219.4 9.6 %input_terms.2 = (bf16[512,2048]{1,0:T(8,128)(2,1)}, f32[4,2048]{1,0:T(4,128)S(1)}) custom-call(bf16[1024,768]{1,0:T(8,128)(2,1)S(1)} %bitcast.27, bf16[1024,1024]{1,0:T(8,128)(2,1)S(1)} %get-tuple-element.245.gh_ref.r_ref, bf16[512,2048]{1,0:T(8,128)(2,1)S(1)} %collective-permute-done.6.refs_1_.x_ref, f32[1024,2]{1,0:T(8,128)S(1)} %copy-done.61, ...), custom_call_target="tpu_custom_call" | custom-call | flops 7516192768 | bytes 13369344 | tf_op jit(solution)/shard_map/input_terms/pallas_call | solution.py:43
  229.1 3.9 %weight_grad.21 = bf16[1024,512]{1,0:T(8,128)(2,1)} custom-call(bf16[1024,1024]{1,0:T(8,128)(2,1)S(1)} %copy-done.95, bf16[1024,512]{1,0:T(8,128)(2,1)S(1)} %get-tuple-element.214.refs_0_.r_ref, bf16[1024,512]{1,0:T(8,128)(2,1)} %collective-permute-done.21.refs_0_, bf16[1024,512]{1,0:T(8,128)(2,1)} %collective-permute-done.22.refs_1_), custom_call_target="tpu_custom_call" | custom-call | flops 2147483648 | bytes 4194304 | tf_op jit(solution)/shard_map/weight_grad/pallas_call | solution.py:43
  233.7 4.0 %all-to-all-start.1 = ((bf16[4,256,512]{2,1,0:T(8,128)(2,1)}), bf16[4,256,512]{2,1,0:T(8,128)(2,1)S(1)}, u32[]{:S(2)}, u32[]{:S(2)}) async-start(bf16[4,256,512]{2,1,0:T(8,128)(2,1)} %bitcast.6), calls=%async_computation.2 | async-start | bytes 2097152 | tf_op jit(solution)/shard_map/all_to_all | solution.py:1040
  238.9 1.6 copy-done.90
  240.5 2.1 weight_grad.22
  242.7 1.9 weight_grad.24
  246.0 1.9 weight_grad.23
  247.9 1.4 collective-permute-start.25
  251.9 1.6 copy-done.24
  253.5 7.4 %input_terms.3 = (bf16[512,2048]{1,0:T(8,128)(2,1)S(1)}, f32[4,2048]{1,0:T(4,128)S(1)}) custom-call(bf16[1024,768]{1,0:T(8,128)(2,1)S(1)} %bitcast.30, bf16[1024,1024]{1,0:T(8,128)(2,1)S(1)} %copy-done.91, bf16[512,2048]{1,0:T(8,128)(2,1)S(1)} %copy-done.1, f32[1024,2]{1,0:T(8,128)S(1)} %copy-done.62, f32[4,2048]{1,0:T(4,128)S(1)} %get-tuple-element.182.scales_ref, ...), custom_call_target="tpu_custom_call" | custom-call | flops 7516192768 | bytes 13369344 | tf_op jit(solution)/shard_map/input_terms/pallas_call | solution.py:43
  262.0 16.8 %collective-permute-done.27.refs_0_ = bf16[256,1024]{1,0:T(8,128)(2,1)} collective-permute-done((bf16[256,1024]{1,0:T(8,128)(2,1)}, bf16[256,1024]{1,0:T(8,128)(2,1)}, u32[]{:S(2)}, u32[]{:S(2)}) %collective-permute-start.27) | collective-permute-done | bytes 524320 | tf_op jit(solution)/shard_map/ppermute | solution.py:615
  278.9 1.4 copied.1
  281.5 1.6 copy-done.92
  283.1 3.4 weight_grad.26
  286.6 3.5 weight_grad.25
  290.6 1.5 collective-permute-start.30
  293.8 2.4 weight_grad.29.from_ref
  299.7 14.8 %collective-permute-done.31.refs_1_ = bf16[512,1024]{1,0:T(8,128)(2,1)} collective-permute-done((bf16[512,1024]{1,0:T(8,128)(2,1)}, bf16[512,1024]{1,0:T(8,128)(2,1)}, u32[]{:S(2)}, u32[]{:S(2)}) %collective-permute-start.31) | collective-permute-done | bytes 1048608 | tf_op jit(solution)/shard_map/ppermute | solution.py:615
  314.9 3.2 weight_grad.30.from_ref
  319.1 4.5 %all-to-all-start.2 = ((bf16[4,512,256]{2,1,0:T(8,128)(2,1)}), bf16[4,512,256]{2,1,0:T(8,128)(2,1)S(1)}, u32[]{:S(2)}, u32[]{:S(2)}) async-start(bf16[4,512,256]{2,1,0:T(8,128)(2,1)} %bitcast.9), calls=%async_computation.4 | async-start | bytes 2097152 | tf_op jit(solution)/shard_map/all_to_all | solution.py:1040
  326.9 1.5 collective-permute-start.35
  329.8 5.4 %collective-permute-done.35.refs_1_ = bf16[256,512]{1,0:T(8,128)(2,1)S(1)} collective-permute-done((bf16[256,512]{1,0:T(8,128)(2,1)S(1)}, bf16[256,512]{1,0:T(8,128)(2,1)S(1)}, u32[]{:S(2)}, u32[]{:S(2)}) %collective-permute-start.35) | collective-permute-done | bytes 262176 | tf_op jit(solution)/shard_map/ppermute | solution.py:615
  337.6 1.8 core_join.4
  339.4 2.0 core_join.5
  343.9 3.1 all-to-all-done.2
  349.5 1.5 fusion.6
  354.3 11.3 %all_to_all.42 = f32[32,1,768]{2,1,0:T(1,128)S(1)} all-to-all(f32[32,1,768]{2,1,0:T(1,128)S(1)} %copy.34), channel_id=1, replica_groups=mesh['dp'=8,'seq'=4] {'dp','seq'}, dimensions={0} | all-to-all | bytes 196608 | tf_op jit(solution)/shard_map/all_to_all | solution.py:1146
  367.5 2.0 core_join.7
  (355 shorter events, 81.2 us)
Async XLA Ops:
  7.2 77.9 %all-gather.3.cloned.1.call-start = ((), (), s32[]{:S(2)}) async-start(), calls=%async_computation.6 | async-start | bytes 2621440 | tf_op jit(solution)/shard_map/all_gather | solution.py:961
  14.2 95.1 %all-gather.5.cloned.1.call-start = ((), (), s32[]{:S(2)}) async-start(), calls=%async_computation.7 | async-start | bytes 2621440 | tf_op jit(solution)/shard_map/all_gather | solution.py:962
  15.1 2.8 collective-permute-start
  17.0 18.0 %copy-start.75 = (s32[1,4]{1,0:T(1,128)S(1)}, s32[1,4]{1,0:T(1,128)}, u32[]{:S(2)}) copy-start(s32[1,4]{1,0:T(1,128)} %refs_0_.2) | copy-start | bytes 52
  17.0 58.4 %copy-start.88 = (f32[1,128]{1,0:T(1,128)S(1)}, f32[1,128]{1,0:T(1,128)}, u32[]{:S(2)}) copy-start(f32[1,128]{1,0:T(1,128)} %constant.63.clone.refs_2_) | copy-start | bytes 1540
  19.7 61.2 %collective-permute-start.1 = (bf16[512,1792]{1,0:T(8,128)(2,1)}, bf16[512,1792]{1,0:T(8,128)(2,1)S(1)}, u32[]{:S(2)}, u32[]{:S(2)}) collective-permute-start(bf16[512,1792]{1,0:T(8,128)(2,1)} %chip_pair.1.refs_4_.refs_0_.refs_1_), channel_id=1, source_target_pairs={{0,8},{4,12},{8,0},{12,4},{16,24},{20,28},{24,16},{28,20},{1,9},{5... | collective-permute-start | bytes 5505032 | tf_op jit(solution)/shard_map/ppermute | solution.py:615
  22.5 58.4 %collective-permute-start.2 = (bf16[512,1792]{1,0:T(8,128)(2,1)}, bf16[512,1792]{1,0:T(8,128)(2,1)}, u32[]{:S(2)}, u32[]{:S(2)}) collective-permute-start(bf16[512,1792]{1,0:T(8,128)(2,1)} %chip_pair.1.refs_4_.refs_0_.refs_1_), channel_id=1, source_target_pairs={{0,16},{4,20},{8,24},{12,28},{16,0},{20,4},{24,8},{28,12},{1,17},{... | collective-permute-start | bytes 5505032 | tf_op jit(solution)/shard_map/ppermute | solution.py:615
  24.1 55.6 %collective-permute-start.3 = (bf16[128,2048]{1,0:T(8,128)(2,1)S(1)}, bf16[128,2048]{1,0:T(8,128)(2,1)}, u32[]{:S(2)}, u32[]{:S(2)}) collective-permute-start(bf16[128,2048]{1,0:T(8,128)(2,1)S(1)} %get-tuple-element.156), channel_id=1, source_target_pairs={{0,8},{4,12},{9,1},{13,5},{18,26},{22,30},{27,19},{31,23}} | collective-permute-start | bytes 1572872 | tf_op jit(solution)/shard_map/ppermute | solution.py:802
  27.3 52.4 %collective-permute-start.4 = (bf16[128,2048]{1,0:T(8,128)(2,1)S(1)}, bf16[128,2048]{1,0:T(8,128)(2,1)}, u32[]{:S(2)}, u32[]{:S(2)}) collective-permute-start(bf16[128,2048]{1,0:T(8,128)(2,1)S(1)} %get-tuple-element.157), channel_id=1, source_target_pairs={{0,16},{4,20},{9,25},{13,29},{18,2},{22,6},{27,11},{31,15}} | collective-permute-start | bytes 1572872 | tf_op jit(solution)/shard_map/ppermute | solution.py:802
  31.6 43.7 %all-to-all-start = ((bf16[8,2,1664]{2,1,0:T(2,128)(2,1)}), bf16[8,2,1664]{2,1,0:T(2,128)(2,1)S(1)}, u32[]{:S(2)}, u32[]{:S(2)}) async-start(bf16[8,2,1664]{2,1,0:T(2,128)(2,1)} %reshape.111), calls=%async_computation | async-start | bytes 106496 | tf_op jit(solution)/shard_map/all_to_all | solution.py:968
  35.0 262.4 %reduce-scatter.3.cloned.1.call-start = ((), (), s32[]{:S(2)}) async-start(), calls=%async_computation.8 | async-start | bytes 2621440 | tf_op jit(solution)/shard_map/reduce_scatter | solution.py:1048
  35.1 40.4 %collective-permute-start.5 = (s32[1,4]{1,0:T(1,128)S(1)}, s32[1,4]{1,0:T(1,128)S(1)}, u32[]{:S(2)}, u32[]{:S(2)}) collective-permute-start(s32[1,4]{1,0:T(1,128)S(1)} %copy-done.75), channel_id=1, source_target_pairs={{0,4},{4,0},{8,12},{12,8},{16,20},{20,16},{24,28},{28,24},{1,5},{5... | collective-permute-start | bytes 56 | tf_op jit(solution)/shard_map/ppermute | solution.py:615
  85.1 4.4 %collective-permute-start.6 = (bf16[512,2048]{1,0:T(8,128)(2,1)}, bf16[512,2048]{1,0:T(8,128)(2,1)S(1)}, u32[]{:S(2)}, u32[]{:S(2)}) collective-permute-start(bf16[512,2048]{1,0:T(8,128)(2,1)} %all-gather.3.cloned.1.call-done.refs_0_.x_ref), channel_id=1, source_target_pairs={{0,4},{4,0},{8,12},{12,8},{16,20},{20,16},{24,28},{28,24},{1,5},{5... | collective-permute-start | bytes 6291464 | tf_op jit(solution)/shard_map/ppermute | solution.py:615
  85.2 25.1 %collective-permute-start.7 = (bf16[256,1792]{1,0:T(8,128)(2,1)}, bf16[256,1792]{1,0:T(8,128)(2,1)}, u32[]{:S(2)}, u32[]{:S(2)}) collective-permute-start(bf16[256,1792]{1,0:T(8,128)(2,1)} %get-tuple-element.177), channel_id=1, source_target_pairs={{0,16},{4,20},{8,24},{12,28},{16,0},{20,4},{24,8},{28,12},{1,17},{... | collective-permute-start | bytes 2752520 | tf_op jit(solution)/shard_map/ppermute | solution.py:615
  89.1 22.6 %collective-permute-start.8 = (bf16[256,1792]{1,0:T(8,128)(2,1)}, bf16[256,1792]{1,0:T(8,128)(2,1)}, u32[]{:S(2)}, u32[]{:S(2)}) collective-permute-start(bf16[256,1792]{1,0:T(8,128)(2,1)} %get-tuple-element.178), channel_id=1, source_target_pairs={{0,8},{4,12},{8,0},{12,4},{16,24},{20,28},{24,16},{28,20},{1,9},{5... | collective-permute-start | bytes 2752520 | tf_op jit(solution)/shard_map/ppermute | solution.py:615
  107.6 26.4 %copy-start.25 = (bf16[1024,512]{1,0:T(8,128)(2,1)}, bf16[1024,512]{1,0:T(8,128)(2,1)S(1)}, u32[]{:S(2)}) copy-start(bf16[1024,512]{1,0:T(8,128)(2,1)S(1)} %get-tuple-element.191.refs_0_.l_ref) | copy-start | bytes 3145732
  111.8 39.3 %collective-permute-start.9 = (bf16[512,2048]{1,0:T(8,128)(2,1)}, bf16[512,2048]{1,0:T(8,128)(2,1)}, u32[]{:S(2)}, u32[]{:S(2)}) collective-permute-start(bf16[512,2048]{1,0:T(8,128)(2,1)} %all-gather.5.cloned.1.call-done.refs_0_), channel_id=1, source_target_pairs={{0,4},{4,0},{8,12},{12,8},{16,20},{20,16},{24,28},{28,24},{1,5},{5... | collective-permute-start | bytes 6291464 | tf_op jit(solution)/shard_map/ppermute | solution.py:615
  111.8 35.2 %collective-permute-start.10 = (bf16[256,2048]{1,0:T(8,128)(2,1)}, bf16[256,2048]{1,0:T(8,128)(2,1)S(1)}, u32[]{:S(2)}, u32[]{:S(2)}) collective-permute-start(bf16[256,2048]{1,0:T(8,128)(2,1)} %copy-done.42), channel_id=1, source_target_pairs={{0,8},{4,12},{8,0},{12,4},{16,24},{20,28},{24,16},{28,20},{1,9},{5... | collective-permute-start | bytes 3145736 | tf_op jit(solution)/shard_map/ppermute | solution.py:615
  112.1 34.9 %collective-permute-start.11 = (bf16[256,2048]{1,0:T(8,128)(2,1)}, bf16[256,2048]{1,0:T(8,128)(2,1)S(1)}, u32[]{:S(2)}, u32[]{:S(2)}) collective-permute-start(bf16[256,2048]{1,0:T(8,128)(2,1)} %copy-done.42), channel_id=1, source_target_pairs={{0,16},{4,20},{8,24},{12,28},{16,0},{20,4},{24,8},{28,12},{1,17},{... | collective-permute-start | bytes 3145736 | tf_op jit(solution)/shard_map/ppermute | solution.py:615
  112.6 34.1 %collective-permute-start.13 = (bf16[128,2048]{1,0:T(8,128)(2,1)}, bf16[128,2048]{1,0:T(8,128)(2,1)S(1)}, u32[]{:S(2)}, u32[]{:S(2)}) collective-permute-start(bf16[128,2048]{1,0:T(8,128)(2,1)} %get-tuple-element.207), channel_id=1, source_target_pairs={{0,8},{4,12},{16,24},{20,28},{9,1},{13,5},{25,17},{29,21},{18,26},... | collective-permute-start | bytes 1572872 | tf_op jit(solution)/shard_map/ppermute | solution.py:802
  116.1 30.8 %collective-permute-start.12 = (bf16[128,2048]{1,0:T(8,128)(2,1)}, bf16[128,2048]{1,0:T(8,128)(2,1)S(1)}, u32[]{:S(2)}, u32[]{:S(2)}) collective-permute-start(bf16[128,2048]{1,0:T(8,128)(2,1)} %get-tuple-element.206), channel_id=1, source_target_pairs={{0,16},{4,20},{8,24},{12,28},{9,25},{13,29},{1,17},{5,21},{18,2},{... | collective-permute-start | bytes 1572872 | tf_op jit(solution)/shard_map/ppermute | solution.py:802
  125.1 11.0 %copy-start.55 = (bf16[1024,512]{1,0:T(8,128)(2,1)S(1)}, bf16[1024,512]{1,0:T(8,128)(2,1)}, u32[]{:S(2)}) copy-start(bf16[1024,512]{1,0:T(8,128)(2,1)} %copy-done.54) | copy-start | bytes 3145732
  125.1 11.0 %copy-start.77 = (f32[2,512,128]{2,1,0:T(8,128)S(1)}, f32[2,512,128]{2,1,0:T(8,128)}, u32[]{:S(2)}) copy-start(f32[2,512,128]{2,1,0:T(8,128)} %copy-done.76) | copy-start | bytes 1572868
  125.1 11.0 %copy-start.79 = (f32[2,512,128]{2,1,0:T(8,128)S(1)}, f32[2,512,128]{2,1,0:T(8,128)}, u32[]{:S(2)}) copy-start(f32[2,512,128]{2,1,0:T(8,128)} %copy-done.78) | copy-start | bytes 1572868
  136.0 54.4 %copy-start.94 = (bf16[1024,1024]{1,0:T(8,128)(2,1)}, bf16[1024,1024]{1,0:T(8,128)(2,1)S(1)}, u32[]{:S(2)}) copy-start(bf16[1024,1024]{1,0:T(8,128)(2,1)S(1)} %get-tuple-element.218.l_ref.b_ref) | copy-start | bytes 6291460
  145.5 45.0 %copy-start.19 = (bf16[2,512,256]{2,1,0:T(8,128)(2,1)}, bf16[2,512,256]{2,1,0:T(8,128)(2,1)S(1)}, u32[]{:S(2)}) copy-start(bf16[2,512,256]{2,1,0:T(8,128)(2,1)S(1)} %get-tuple-element.200) | copy-start | bytes 1572868
  147.0 43.5 %copy-start.15 = (bf16[256,2048]{1,0:T(8,128)(2,1)}, bf16[256,2048]{1,0:T(8,128)(2,1)S(1)}, u32[]{:S(2)}) copy-start(bf16[256,2048]{1,0:T(8,128)(2,1)S(1)} %collective-permute-done.10.x_ref.refs_1_.refs_2_.refs_5_) | copy-start | bytes 3145732
  147.0 43.5 %copy-start.17 = (bf16[256,2048]{1,0:T(8,128)(2,1)}, bf16[256,2048]{1,0:T(8,128)(2,1)S(1)}, u32[]{:S(2)}) copy-start(bf16[256,2048]{1,0:T(8,128)(2,1)S(1)} %collective-permute-done.11.y_ref.refs_2_.refs_3_.refs_6_) | copy-start | bytes 3145732
  147.1 15.3 %collective-permute-start.16 = (bf16[128,2048]{1,0:T(8,128)(2,1)S(1)}, bf16[128,2048]{1,0:T(8,128)(2,1)S(1)}, u32[]{:S(2)}, u32[]{:S(2)}) collective-permute-start(bf16[128,2048]{1,0:T(8,128)(2,1)S(1)} %get-tuple-element.210), channel_id=1, source_target_pairs={{0,16},{4,20},{8,24},{12,28},{16,0},{20,4},{24,8},{28,12},{1,17},{... | collective-permute-start | bytes 1572872 | tf_op jit(solution)/shard_map/ppermute | solution.py:615
  149.5 14.9 %collective-permute-start.17 = (bf16[128,2048]{1,0:T(8,128)(2,1)S(1)}, bf16[128,2048]{1,0:T(8,128)(2,1)S(1)}, u32[]{:S(2)}, u32[]{:S(2)}) collective-permute-start(bf16[128,2048]{1,0:T(8,128)(2,1)S(1)} %get-tuple-element.211), channel_id=1, source_target_pairs={{0,8},{4,12},{8,0},{12,4},{16,24},{20,28},{24,16},{28,20},{1,9},{5... | collective-permute-start | bytes 1572872 | tf_op jit(solution)/shard_map/ppermute | solution.py:615
  153.0 30.6 %copy-start.39 = (bf16[1024,512]{1,0:T(8,128)(2,1)}, bf16[1024,512]{1,0:T(8,128)(2,1)S(1)}, u32[]{:S(2)}) copy-start(bf16[1024,512]{1,0:T(8,128)(2,1)S(1)} %get-tuple-element.216.refs_2_.r_ref) | copy-start | bytes 3145732
  153.0 33.3 %copy-start.36 = (bf16[1024,512]{1,0:T(8,128)(2,1)}, bf16[1024,512]{1,0:T(8,128)(2,1)S(1)}, u32[]{:S(2)}) copy-start(bf16[1024,512]{1,0:T(8,128)(2,1)S(1)} %get-tuple-element.215.refs_1_.r_ref) | copy-start | bytes 3145732
  153.0 76.0 %copy-start.13 = (bf16[1024,512]{1,0:T(8,128)(2,1)}, bf16[1024,512]{1,0:T(8,128)(2,1)S(1)}, u32[]{:S(2)}) copy-start(bf16[1024,512]{1,0:T(8,128)(2,1)S(1)} %get-tuple-element.214.refs_0_.r_ref) | copy-start | bytes 3145732
  155.2 28.4 %collective-permute-start.14 = (bf16[512,512]{1,0:T(8,128)(2,1)S(1)}, bf16[512,512]{1,0:T(8,128)(2,1)S(1)}, u32[]{:S(2)}, u32[]{:S(2)}) collective-permute-start(bf16[512,512]{1,0:T(8,128)(2,1)S(1)} %get-tuple-element.219), channel_id=1, source_target_pairs={{0,8},{4,12},{8,0},{12,4},{16,24},{20,28},{24,16},{28,20},{1,9},{5... | collective-permute-start | bytes 1572872 | tf_op jit(solution)/shard_map/ppermute | solution.py:615
  155.7 27.9 %collective-permute-start.15 = (bf16[512,512]{1,0:T(8,128)(2,1)S(1)}, bf16[512,512]{1,0:T(8,128)(2,1)S(1)}, u32[]{:S(2)}, u32[]{:S(2)}) collective-permute-start(bf16[512,512]{1,0:T(8,128)(2,1)S(1)} %get-tuple-element.220), channel_id=1, source_target_pairs={{0,16},{4,20},{8,24},{12,28},{16,0},{20,4},{24,8},{28,12},{1,17},{... | collective-permute-start | bytes 1572872 | tf_op jit(solution)/shard_map/ppermute | solution.py:615
  162.3 28.2 %copy-start.63 = (bf16[128,2048]{1,0:T(8,128)(2,1)}, bf16[128,2048]{1,0:T(8,128)(2,1)S(1)}, u32[]{:S(2)}) copy-start(bf16[128,2048]{1,0:T(8,128)(2,1)S(1)} %collective-permute-done.16.refs_3_.refs_4_.refs_7_) | copy-start | bytes 1572868
  164.4 26.1 %copy-start.65 = (bf16[128,2048]{1,0:T(8,128)(2,1)}, bf16[128,2048]{1,0:T(8,128)(2,1)S(1)}, u32[]{:S(2)}) copy-start(bf16[128,2048]{1,0:T(8,128)(2,1)S(1)} %collective-permute-done.17.refs_4_.refs_5_.refs_8_) | copy-start | bytes 1572868
  165.4 16.7 %collective-permute-start.18 = (bf16[256,768]{1,0:T(8,128)(2,1)S(1)}, bf16[256,768]{1,0:T(8,128)(2,1)S(1)}, u32[]{:S(2)}, u32[]{:S(2)}) collective-permute-start(bf16[256,768]{1,0:T(8,128)(2,1)S(1)} %get-tuple-element.227), channel_id=1, source_target_pairs={{0,8},{4,12},{8,0},{12,4},{16,24},{20,28},{24,16},{28,20},{1,9},{5... | collective-permute-start | bytes 1179656 | tf_op jit(solution)/shard_map/ppermute | solution.py:615
  167.0 15.9 %collective-permute-start.19 = (bf16[256,768]{1,0:T(8,128)(2,1)S(1)}, bf16[256,768]{1,0:T(8,128)(2,1)S(1)}, u32[]{:S(2)}, u32[]{:S(2)}) collective-permute-start(bf16[256,768]{1,0:T(8,128)(2,1)S(1)} %get-tuple-element.228), channel_id=1, source_target_pairs={{0,16},{4,20},{8,24},{12,28},{16,0},{20,4},{24,8},{28,12},{1,17},{... | collective-permute-start | bytes 1179656 | tf_op jit(solution)/shard_map/ppermute | solution.py:615
  183.6 6.8 %collective-permute-start.20 = (bf16[512,2048]{1,0:T(8,128)(2,1)S(1)}, bf16[512,2048]{1,0:T(8,128)(2,1)S(1)}, u32[]{:S(2)}, u32[]{:S(2)}) collective-permute-start(bf16[512,2048]{1,0:T(8,128)(2,1)S(1)} %branch_rows.2), channel_id=1, source_target_pairs={{0,4},{4,0},{8,12},{12,8},{16,20},{20,16},{24,28},{28,24},{1,5},{5... | collective-permute-start | bytes 6291464 | tf_op jit(solution)/shard_map/ppermute | solution.py:615
  186.0 43.0 %collective-permute-start.22 = (bf16[1024,512]{1,0:T(8,128)(2,1)}, bf16[1024,512]{1,0:T(8,128)(2,1)}, u32[]{:S(2)}, u32[]{:S(2)}) collective-permute-start(bf16[1024,512]{1,0:T(8,128)(2,1)} %weight_grad.19), channel_id=1, source_target_pairs={{0,16},{4,20},{8,24},{12,28},{16,0},{20,4},{24,8},{28,12},{1,17},{... | collective-permute-start | bytes 3145736 | tf_op jit(solution)/shard_map/ppermute | solution.py:615
  188.7 40.3 %collective-permute-start.21 = (bf16[1024,512]{1,0:T(8,128)(2,1)}, bf16[1024,512]{1,0:T(8,128)(2,1)}, u32[]{:S(2)}, u32[]{:S(2)}) collective-permute-start(bf16[1024,512]{1,0:T(8,128)(2,1)} %weight_grad.18), channel_id=1, source_target_pairs={{0,8},{4,12},{8,0},{12,4},{16,24},{20,28},{24,16},{28,20},{1,9},{5... | collective-permute-start | bytes 3145736 | tf_op jit(solution)/shard_map/ppermute | solution.py:615
  199.3 29.7 %collective-permute-start.23 = (bf16[128,512]{1,0:T(8,128)(2,1)}, bf16[128,512]{1,0:T(8,128)(2,1)S(1)}, u32[]{:S(2)}, u32[]{:S(2)}) collective-permute-start(bf16[128,512]{1,0:T(8,128)(2,1)} %get-tuple-element.235), channel_id=1, source_target_pairs={{0,8},{4,12},{8,0},{12,4},{16,24},{20,28},{24,16},{28,20},{1,9},{5... | collective-permute-start | bytes 393224 | tf_op jit(solution)/shard_map/ppermute | solution.py:615
  199.5 29.5 %collective-permute-start.24 = (bf16[128,512]{1,0:T(8,128)(2,1)}, bf16[128,512]{1,0:T(8,128)(2,1)S(1)}, u32[]{:S(2)}, u32[]{:S(2)}) collective-permute-start(bf16[128,512]{1,0:T(8,128)(2,1)} %get-tuple-element.236), channel_id=1, source_target_pairs={{0,16},{4,20},{8,24},{12,28},{16,0},{20,4},{24,8},{28,12},{1,17},{... | collective-permute-start | bytes 393224 | tf_op jit(solution)/shard_map/ppermute | solution.py:615
  233.0 17.5 %collective-permute-start.29 = (bf16[512,2048]{1,0:T(8,128)(2,1)}, bf16[512,2048]{1,0:T(8,128)(2,1)S(1)}, u32[]{:S(2)}, u32[]{:S(2)}) collective-permute-start(bf16[512,2048]{1,0:T(8,128)(2,1)} %get-tuple-element.251), channel_id=1, source_target_pairs={{0,4},{4,0},{8,12},{12,8},{16,20},{20,16},{24,28},{28,24},{1,5},{5... | collective-permute-start | bytes 6291464 | tf_op jit(solution)/shard_map/ppermute | solution.py:615
  233.7 45.2 %all-to-all-start.1 = ((bf16[4,256,512]{2,1,0:T(8,128)(2,1)}), bf16[4,256,512]{2,1,0:T(8,128)(2,1)S(1)}, u32[]{:S(2)}, u32[]{:S(2)}) async-start(bf16[4,256,512]{2,1,0:T(8,128)(2,1)} %bitcast.6), calls=%async_computation.2 | async-start | bytes 2097152 | tf_op jit(solution)/shard_map/all_to_all | solution.py:1040
  237.7 109.3 %reduce-scatter.5.cloned.1.call-start = ((), (), s32[]{:S(2)}) async-start(), calls=%async_computation.9 | async-start | bytes 2621440 | tf_op jit(solution)/shard_map/reduce_scatter | solution.py:1048
  244.6 34.3 %collective-permute-start.26 = (bf16[512,768]{1,0:T(8,128)(2,1)}, bf16[512,768]{1,0:T(8,128)(2,1)}, u32[]{:S(2)}, u32[]{:S(2)}) collective-permute-start(bf16[512,768]{1,0:T(8,128)(2,1)} %weight_grad.24), channel_id=1, source_target_pairs={{0,16},{4,20},{8,24},{12,28},{16,0},{20,4},{24,8},{28,12},{1,17},{... | collective-permute-start | bytes 2359304 | tf_op jit(solution)/shard_map/ppermute | solution.py:615
  247.9 30.9 %collective-permute-start.25 = (bf16[512,768]{1,0:T(8,128)(2,1)}, bf16[512,768]{1,0:T(8,128)(2,1)}, u32[]{:S(2)}, u32[]{:S(2)}) collective-permute-start(bf16[512,768]{1,0:T(8,128)(2,1)} %weight_grad.23), channel_id=1, source_target_pairs={{0,8},{4,12},{8,0},{12,4},{16,24},{20,28},{24,16},{28,20},{1,9},{5... | collective-permute-start | bytes 2359304 | tf_op jit(solution)/shard_map/ppermute | solution.py:615
  249.4 29.5 %collective-permute-start.27 = (bf16[256,1024]{1,0:T(8,128)(2,1)}, bf16[256,1024]{1,0:T(8,128)(2,1)}, u32[]{:S(2)}, u32[]{:S(2)}) collective-permute-start(bf16[256,1024]{1,0:T(8,128)(2,1)} %get-tuple-element.246), channel_id=1, source_target_pairs={{0,8},{4,12},{8,0},{12,4},{16,24},{20,28},{24,16},{28,20},{1,9},{5... | collective-permute-start | bytes 1572872 | tf_op jit(solution)/shard_map/ppermute | solution.py:615
  250.0 28.9 %collective-permute-start.28 = (bf16[256,1024]{1,0:T(8,128)(2,1)}, bf16[256,1024]{1,0:T(8,128)(2,1)}, u32[]{:S(2)}, u32[]{:S(2)}) collective-permute-start(bf16[256,1024]{1,0:T(8,128)(2,1)} %get-tuple-element.247), channel_id=1, source_target_pairs={{0,16},{4,20},{8,24},{12,28},{16,0},{20,4},{24,8},{28,12},{1,17},{... | collective-permute-start | bytes 1572872 | tf_op jit(solution)/shard_map/ppermute | solution.py:615
  290.1 24.4 %collective-permute-start.31 = (bf16[512,1024]{1,0:T(8,128)(2,1)}, bf16[512,1024]{1,0:T(8,128)(2,1)}, u32[]{:S(2)}, u32[]{:S(2)}) collective-permute-start(bf16[512,1024]{1,0:T(8,128)(2,1)} %weight_grad.26), channel_id=1, source_target_pairs={{0,16},{4,20},{8,24},{12,28},{16,0},{20,4},{24,8},{28,12},{1,17},{... | collective-permute-start | bytes 3145736 | tf_op jit(solution)/shard_map/ppermute | solution.py:615
  290.6 24.2 %collective-permute-start.30 = (bf16[512,1024]{1,0:T(8,128)(2,1)}, bf16[512,1024]{1,0:T(8,128)(2,1)}, u32[]{:S(2)}, u32[]{:S(2)}) collective-permute-start(bf16[512,1024]{1,0:T(8,128)(2,1)} %weight_grad.25), channel_id=1, source_target_pairs={{0,8},{4,12},{8,0},{12,4},{16,24},{20,28},{24,16},{28,20},{1,9},{5... | collective-permute-start | bytes 3145736 | tf_op jit(solution)/shard_map/ppermute | solution.py:615
  297.4 17.4 %copy-start.26 = (bf16[1024,512]{1,0:T(8,128)(2,1)S(1)}, bf16[1024,512]{1,0:T(8,128)(2,1)}, u32[]{:S(2)}) copy-start(bf16[1024,512]{1,0:T(8,128)(2,1)} %copy-done.25) | copy-start | bytes 3145732
  297.4 17.4 %copy-start.93 = (bf16[1024,1024]{1,0:T(8,128)(2,1)S(1)}, bf16[1024,1024]{1,0:T(8,128)(2,1)}, u32[]{:S(2)}) copy-start(bf16[1024,1024]{1,0:T(8,128)(2,1)} %copy-done.89) | copy-start | bytes 6291460
  319.1 17.4 %copy-start.14 = (bf16[1024,512]{1,0:T(8,128)(2,1)S(1)}, bf16[1024,512]{1,0:T(8,128)(2,1)}, u32[]{:S(2)}) copy-start(bf16[1024,512]{1,0:T(8,128)(2,1)} %copy-done.13) | copy-start | bytes 3145732
  319.1 27.9 %all-to-all-start.2 = ((bf16[4,512,256]{2,1,0:T(8,128)(2,1)}), bf16[4,512,256]{2,1,0:T(8,128)(2,1)S(1)}, u32[]{:S(2)}, u32[]{:S(2)}) async-start(bf16[4,512,256]{2,1,0:T(8,128)(2,1)} %bitcast.9), calls=%async_computation.4 | async-start | bytes 2097152 | tf_op jit(solution)/shard_map/all_to_all | solution.py:1040
  325.0 11.4 %copy-start.22 = (bf16[2,512,256]{2,1,0:T(8,128)(2,1)S(1)}, bf16[2,512,256]{2,1,0:T(8,128)(2,1)}, u32[]{:S(2)}) copy-start(bf16[2,512,256]{2,1,0:T(8,128)(2,1)} %copy-done.19) | copy-start | bytes 1572868
  325.6 11.9 %collective-permute-start.33 = (f32[256,768]{1,0:T(8,128)S(1)}, f32[256,768]{1,0:T(8,128)S(1)}, u32[]{:S(2)}, u32[]{:S(2)}) collective-permute-start(f32[256,768]{1,0:T(8,128)S(1)} %get-tuple-element.267), channel_id=1, source_target_pairs={{0,4},{4,0},{8,12},{12,8},{16,20},{20,16},{24,28},{28,24},{1,5},{5... | collective-permute-start | bytes 2359304 | tf_op jit(solution)/shard_map/ppermute | solution.py:615
  326.3 13.0 %collective-permute-start.32 = (bf16[1024,256]{1,0:T(8,128)(2,1)S(1)}, bf16[1024,256]{1,0:T(8,128)(2,1)S(1)}, u32[]{:S(2)}, u32[]{:S(2)}) collective-permute-start(bf16[1024,256]{1,0:T(8,128)(2,1)S(1)} %get-tuple-element.270), channel_id=1, source_target_pairs={{0,4},{4,0},{8,12},{12,8},{16,20},{20,16},{24,28},{28,24},{1,5},{5... | collective-permute-start | bytes 1572872 | tf_op jit(solution)/shard_map/ppermute | solution.py:615
  326.9 8.3 %collective-permute-start.35 = (bf16[256,512]{1,0:T(8,128)(2,1)S(1)}, bf16[256,512]{1,0:T(8,128)(2,1)S(1)}, u32[]{:S(2)}, u32[]{:S(2)}) collective-permute-start(bf16[256,512]{1,0:T(8,128)(2,1)S(1)} %copy-done.72), channel_id=1, source_target_pairs={{0,16},{4,20},{8,24},{12,28},{16,0},{20,4},{24,8},{28,12},{1,17},{... | collective-permute-start | bytes 786440 | tf_op jit(solution)/shard_map/ppermute | solution.py:615
  328.4 8.0 %collective-permute-start.34 = (bf16[256,512]{1,0:T(8,128)(2,1)S(1)}, bf16[256,512]{1,0:T(8,128)(2,1)S(1)}, u32[]{:S(2)}, u32[]{:S(2)}) collective-permute-start(bf16[256,512]{1,0:T(8,128)(2,1)S(1)} %weight_grad.27), channel_id=1, source_target_pairs={{0,8},{4,12},{8,0},{12,4},{16,24},{20,28},{24,16},{28,20},{1,9},{5... | collective-permute-start | bytes 786440 | tf_op jit(solution)/shard_map/ppermute | solution.py:615
  337.5 14.6 %collective-permute-start.36 = (f32[256,256]{1,0:T(8,128)S(1)}, f32[256,256]{1,0:T(8,128)S(1)}, u32[]{:S(2)}, u32[]{:S(2)}) collective-permute-start(f32[256,256]{1,0:T(8,128)S(1)} %get-tuple-element.274), channel_id=1, source_target_pairs={{0,4},{4,0},{8,12},{12,8},{16,20},{20,16},{24,28},{28,24},{1,5},{5... | collective-permute-start | bytes 786440 | tf_op jit(solution)/shard_map/ppermute | solution.py:615
  354.1 13.4 %collective-permute-start.37 = (bf16[256,1024]{1,0:T(8,128)(2,1)S(1)}, bf16[256,1024]{1,0:T(8,128)(2,1)S(1)}, u32[]{:S(2)}, u32[]{:S(2)}) collective-permute-start(bf16[256,1024]{1,0:T(8,128)(2,1)S(1)} %get-tuple-element.287), channel_id=1, source_target_pairs={{0,4},{4,0},{8,12},{12,8},{16,20},{20,16},{24,28},{28,24},{1,5},{5... | collective-permute-start | bytes 1572872 | tf_op jit(solution)/shard_map/ppermute | solution.py:615
  (93 other events, 337.2 us)
Sparse Core Ops, SparseCore 0:
  14.3 48.6 all-gather.2
  64.5 44.6 all-gather.4
  201.4 45.6 reduce-scatter.2
  280.5 44.0 reduce-scatter.4
